TPU v7x, 32 devices: a whole 2x2x4 slice. The times are simulated.
32 devices in a mesh: gx: 4 (over y, core), gy: 8 (over z, x).
Axes of the slice: x: 2, y: 2, z: 4, core: 2. Of those that a mesh axis runs over, the one named last changes fastest.
Arguments:
- velocity: float32 [3, 32, 64, 128], P(None, 'gx', 'gy'), may hold values from -2 to 2
- pressure: float32 [32, 64, 128], P('gx', 'gy'), may hold values from -6 to 6
- buoyancy: float32 [32, 64, 128], P('gx', 'gy'), may hold values from -6 to 6
- background: float32 [32, 64, 128], P('gx', 'gy'), may hold values from -0.7 to 0.7
- marker_value: float32 [8192, 256], P(('gx', 'gy')), may hold values from -2.5 to 2.5
- marker_height: float32 [8192, 256], P(('gx', 'gy')), may hold values from 0 to 127
- marker_owner: int32 [8192, 1], P(('gx', 'gy')), may hold values from 0 to 31; in each aligned block of 256 rows (0 to 255, 256 to 511, ...) at most 16 rows name the same one
- marker_column: int32 [8192], P(('gx', 'gy')), may hold values from 0 to 63
- block_count: int32 [32], P(('gx', 'gy')), may hold values from 1 to 256, 6144 in all
Outputs:
- new_velocity: float32 [3, 32, 64, 128], P(None, 'gx', 'gy')
- new_pressure: float32 [32, 64, 128], P('gx', 'gy')
- viscosity: float32 [32, 64, 128], P('gx', 'gy')
Inputs may be any that keep to these rules, and one draw needn't show every extreme that they name: `marker_owner`: among the 256 blocks of one device at most 16 name the same owner, and for some owner exactly 16 do. A device's live blocks are its first block_count ones; some device has all 256 live.
All inputs are finite; a program needn't handle non-finite values.
Results may differ from a plain program's by a relative error of at most 0.0003.
Values sent between devices are 32-bit elements; how exact they have to be, the bound alone decides.
No kernel may reach another device: no remote copies, remote signals or barrier semaphores. Data moves between devices by JAX's collectives and lax.ppermute only.
A program may use at most 64 MiB of HBM per device.

v0:
```python
import jax
import jax.numpy as jnp
from jax import lax
from jax.sharding import PartitionSpec as P

ITERS = 2


PRESS_STEP = 0.5
VEL_STEP = 0.05
DAMPING = 0.8


def extended(x, sides, width):
    for axis, dim in sides:
        devices, length = (lax.axis_size(axis), x.shape[dim])
        up = [(i, (i + 1) % devices) for i in range(devices - 1)]
        down = [(j, i) for i, j in up]
        last = lax.slice_in_dim(x, length - width, length, axis=dim)
        first = lax.slice_in_dim(x, 0, width, axis=dim)
        before = lax.ppermute(last, axis, up)
        after = lax.ppermute(first, axis, down)
        x = jnp.concatenate([before, x, after], axis=dim)
    return x


def inner_of(field):
    return field[..., 1:-1, 1:-1, :]


def east_of(field):
    return field[..., 2:, 1:-1, :]


def west_of(field):
    return field[..., :-2, 1:-1, :]


def north_of(field):
    return field[..., 1:-1, 2:, :]


def south_of(field):
    return field[..., 1:-1, :-2, :]


def upper_of(field):
    return jnp.concatenate([field[..., 1:], jnp.zeros_like(field[..., :1])], axis=-1)


def lower_of(field):
    return jnp.concatenate([jnp.zeros_like(field[..., :1]), field[..., :-1]], axis=-1)


def column_profile(values, heights, num_levels):
    lower_f = jnp.minimum(jnp.floor(heights), num_levels - 2.0)
    fraction = heights - lower_f
    lower_idx = lower_f.astype(jnp.int32)
    levels = jnp.arange(num_levels, dtype=jnp.int32)
    at_low = lower_idx[..., None] == levels
    at_up = (lower_idx + 1)[..., None] == levels
    weight = jnp.where(at_low, (1.0 - fraction)[..., None], 0.0) + jnp.where(
        at_up, fraction[..., None], 0.0
    )
    value_sum = jnp.sum(weight * values[..., None], axis=1)
    weight_sum = jnp.sum(weight, axis=1)
    return jnp.stack([value_sum, weight_sum], axis=1)


def place_rows(rows, profile, total_rows):
    one_hot = (jnp.arange(total_rows, dtype=jnp.int32)[:, None] == rows[None, :]).astype(
        jnp.float32
    )
    flat = profile.reshape(profile.shape[0], -1)
    return jnp.dot(
        one_hot, flat, precision=lax.Precision.HIGHEST, preferred_element_type=jnp.float32
    )


def stresses(vel_pad, visc_pad, pressure):
    vel_x = inner_of(vel_pad[0])
    vel_y = inner_of(vel_pad[1])
    vel_z = inner_of(vel_pad[2])
    visc = inner_of(visc_pad)
    grad_xx = vel_x - west_of(vel_pad[0])
    grad_yy = vel_y - south_of(vel_pad[1])
    grad_zz = vel_z - lower_of(vel_z)
    divergence = grad_xx + grad_yy + grad_zz
    new_press = pressure - PRESS_STEP * visc * divergence
    third = divergence / 3.0
    sig_xx = 2.0 * visc * (grad_xx - third) - new_press
    sig_yy = 2.0 * visc * (grad_yy - third) - new_press
    sig_zz = 2.0 * visc * (grad_zz - third) - new_press
    corner_xy = 0.25 * (visc + east_of(visc_pad) + north_of(visc_pad) + visc_pad[..., 2:, 2:, :])
    side_x = visc + east_of(visc_pad)
    side_y = visc + north_of(visc_pad)
    corner_xz = 0.25 * (side_x + upper_of(side_x))
    corner_yz = 0.25 * (side_y + upper_of(side_y))
    tau_xy = corner_xy * (north_of(vel_pad[0]) - vel_x + east_of(vel_pad[1]) - vel_y)
    tau_xz = corner_xz * (upper_of(vel_x) - vel_x + east_of(vel_pad[2]) - vel_z)
    tau_yz = corner_yz * (upper_of(vel_y) - vel_y + north_of(vel_pad[2]) - vel_z)
    return (new_press, jnp.stack([sig_xx, sig_yy, tau_xy, tau_xz, tau_yz]), sig_zz)


def residuals(stress_pad, sig_zz, buoyancy):
    sig_xx = stress_pad[0]
    sig_yy = stress_pad[1]
    tau_xy = stress_pad[2]
    tau_xz = stress_pad[3]
    tau_yz = stress_pad[4]
    mid_xz = inner_of(tau_xz)
    mid_yz = inner_of(tau_yz)
    res_x = (
        east_of(sig_xx)
        - inner_of(sig_xx)
        + inner_of(tau_xy)
        - south_of(tau_xy)
        + mid_xz
        - lower_of(mid_xz)
    )
    res_y = (
        inner_of(tau_xy)
        - west_of(tau_xy)
        + north_of(sig_yy)
        - inner_of(sig_yy)
        + mid_yz
        - lower_of(mid_yz)
    )
    res_z = (
        mid_xz - west_of(tau_xz) + mid_yz - south_of(tau_yz) + upper_of(sig_zz) - sig_zz + buoyancy
    )
    return jnp.stack([res_x, res_y, res_z])


def advance(vel, moment, residual, visc_pad, masks):
    visc = inner_of(visc_pad)
    faces = jnp.stack(
        [
            0.5 * (visc + east_of(visc_pad)),
            0.5 * (visc + north_of(visc_pad)),
            0.5 * (visc + upper_of(visc)),
        ]
    )
    moment = DAMPING * moment + residual
    vel = masks * (vel + VEL_STEP * moment / faces)
    return (vel, moment)


def rims(field):
    return extended(field, (("gx", 1), ("gy", 2)), 1)


def shards(
    velocity,
    pressure,
    buoyancy,
    background,
    marker_value,
    marker_height,
    marker_owner,
    marker_column,
    block_count,
):
    cells_x, cells_y, num_levels = pressure.shape
    block_rows = marker_owner.shape[0]
    size_x = lax.axis_size("gx")
    size_y = lax.axis_size("gy")
    devices = size_x * size_y
    capacity = max(2, (2 * block_rows + devices - 1) // devices)
    columns_n = cells_x * cells_y
    owner = marker_owner[:, 0]
    live = jnp.arange(block_rows) < block_count[0]
    hits = ((owner[:, None] == jnp.arange(devices)[None, :]) & live[:, None]).astype(jnp.int32)
    ranks = jnp.sum((jnp.cumsum(hits, axis=0) - 1) * hits, axis=1)
    slots = jnp.where(live, owner * capacity + ranks, devices * capacity)
    slot_hot = jnp.arange(devices * capacity, dtype=jnp.int32)[:, None] == slots[None, :]
    col_buffer = jnp.sum(jnp.where(slot_hot, (marker_column + 1)[None, :], 0), axis=1) - 1
    col_buffer = col_buffer.reshape(size_x, size_y, capacity)
    slot_matrix = slot_hot.astype(jnp.float32)
    payload = jnp.stack([marker_value, marker_height], axis=1)
    marks = payload.shape[2]
    send_buf = jnp.dot(
        slot_matrix,
        payload.reshape(block_rows, 2 * marks),
        precision=lax.Precision.HIGHEST,
        preferred_element_type=jnp.float32,
    )
    send_buf = send_buf.reshape(size_x, size_y, capacity, 2, marks)
    arrived, arrived_cols = (
        lax.all_to_all(
            lax.all_to_all(send_buf, "gx", split_axis=0, concat_axis=0, tiled=True),
            "gy",
            split_axis=1,
            concat_axis=1,
            tiled=True,
        ),
        lax.all_to_all(
            lax.all_to_all(col_buffer, "gx", split_axis=0, concat_axis=0, tiled=True),
            "gy",
            split_axis=1,
            concat_axis=1,
            tiled=True,
        ),
    )
    arrived = arrived.reshape(devices * capacity, 2, marks)
    arrived_cols = arrived_cols.reshape(devices * capacity)
    rows = jnp.where(arrived_cols >= 0, arrived_cols, columns_n).astype(jnp.int32)
    profile = column_profile(arrived[:, 0], arrived[:, 1], num_levels)
    sums = place_rows(rows, profile, columns_n)
    sums = sums.reshape(cells_x, cells_y, 2, num_levels)
    viscosity = jnp.exp((sums[:, :, 0] + background) / (sums[:, :, 1] + 1.0))
    global_x = lax.axis_index("gx") * cells_x + jnp.arange(cells_x)
    global_y = lax.axis_index("gy") * cells_y + jnp.arange(cells_y)
    mask_x = (global_x < cells_x * size_x - 1).astype(jnp.float32)
    mask_y = (global_y < cells_y * size_y - 1).astype(jnp.float32)
    mask_z = (jnp.arange(num_levels) < num_levels - 1).astype(jnp.float32)
    ones_grid = jnp.ones((cells_x, cells_y, num_levels), jnp.float32)
    masks = jnp.stack(
        [
            ones_grid * mask_x[:, None, None],
            ones_grid * mask_y[None, :, None],
            ones_grid * mask_z[None, None, :],
        ]
    )
    vel = velocity
    moment = jnp.zeros_like(velocity)
    visc_pad = rims(viscosity[None])[0]
    press = pressure
    for sweep_idx in range(ITERS):
        press, stress, sig_zz = stresses(rims(vel), visc_pad, press)
        residual = residuals(rims(stress), sig_zz, buoyancy)
        vel, moment = advance(vel, moment, residual, visc_pad, masks)
    return (vel, press, viscosity)


def solution(mesh):
    return jax.shard_map(
        shards,
        mesh=mesh,
        in_specs=(
            P(None, "gx", "gy", None),
            P("gx", "gy", None),
            P("gx", "gy", None),
            P("gx", "gy", None),
            P(("gx", "gy"), None),
            P(("gx", "gy"), None),
            P(("gx", "gy"), None),
            P(("gx", "gy")),
            P(("gx", "gy")),
        ),
        out_specs=(P(None, "gx", "gy", None), P("gx", "gy", None), P("gx", "gy", None)),
        check_vma=False,
    )
```

profile of v0, /device:TPU:0, one launch (start us, length us, event | category | flops | bytes accessed | tf_op | source)
XLA Modules:
  0.0 228.9 jit_solution(1652927440290417424)
XLA Ops:
  5.2 4.2 %all-to-all-start = ((s32[4,1,128]{2,1,0:T(1,128)}), s32[4,1,128]{2,1,0:T(1,128)S(1)}, u32[]{:S(2)}, u32[]{:S(2)}) async-start(s32[4,1,128]{2,1,0:T(1,128)} %reshape.171), calls=%async_computation | async-start | bytes 4096 | tf_op jit(solution)/shard_map/all_to_all | solution.py:198
  11.6 1.6 fusion.1
  13.2 3.5 %all-to-all-start.2 = ((f32[4,8,16,2,256]{4,2,3,1,0:T(8,128)}), f32[4,8,16,2,256]{4,2,3,1,0:T(8,128)S(1)}, u32[]{:S(2)}, u32[]{:S(2)}) async-start(f32[4,8,16,2,256]{4,2,3,1,0:T(8,128)} %fusion.1), calls=%async_computation.2 | async-start | bytes 2097152 | tf_op jit(solution)/shard_map/all_to_all | solution.py:191
  18.6 12.6 %all-to-all-done.2 = f32[4,8,16,2,256]{4,2,3,1,0:T(8,128)S(1)} async-done(((f32[4,8,16,2,256]{4,2,3,1,0:T(8,128)}), f32[4,8,16,2,256]{4,2,3,1,0:T(8,128)S(1)}, u32[]{:S(2)}, u32[]{:S(2)}) %all-to-all-start.2) | async-done | bytes 1048608 | tf_op jit(solution)/shard_map/all_to_all | solution.py:191
  31.2 6.3 %all-to-all-start.1 = ((s32[4,8,16]{2,0,1:T(4,128)}), s32[4,8,16]{2,0,1:T(4,128)S(1)}, u32[]{:S(2)}, u32[]{:S(2)}) async-start(s32[4,8,16]{2,0,1:T(4,128)} %copy.41), calls=%async_computation.1 | async-start | bytes 32768 | tf_op jit(solution)/shard_map/all_to_all | solution.py:197
  38.5 5.5 %all-to-all-done.1 = s32[4,8,16]{2,0,1:T(4,128)S(1)} async-done(((s32[4,8,16]{2,0,1:T(4,128)}), s32[4,8,16]{2,0,1:T(4,128)S(1)}, u32[]{:S(2)}, u32[]{:S(2)}) %all-to-all-start.1) | async-done | bytes 2080 | tf_op jit(solution)/shard_map/all_to_all | solution.py:197
  44.0 3.6 %all-to-all-start.3 = ((f32[4,8,16,2,256]{4,2,3,0,1:T(8,128)}), f32[4,8,16,2,256]{4,2,3,0,1:T(8,128)S(1)}, u32[]{:S(2)}, u32[]{:S(2)}) async-start(f32[4,8,16,2,256]{4,2,3,0,1:T(8,128)} %copy.45), calls=%async_computation.3 | async-start | bytes 2097152 | tf_op jit(solution)/shard_map/all_to_all | solution.py:190
  48.9 1.3 collective-permute-start.5
  50.4 2.2 collective-permute-done.5
  52.6 3.8 %collective-permute-start.6 = (f32[3,10,1,128]{3,2,1,0:T(1,128)S(1)}, f32[3,10,1,128]{3,2,1,0:T(1,128)S(1)}, u32[]{:S(2)}, u32[]{:S(2)}) collective-permute-start(f32[3,10,1,128]{3,2,1,0:T(1,128)S(1)} %get-tuple-element.44), channel_id=1, source_target_pairs={{0,1},{1,2},{2,3},{3,4},{4,5},{5,6},{6,7},{8,9},{9,10},{10,11},{11... | collective-permute-start | bytes 46088 | tf_op jit(solution)/shard_map/ppermute | solution.py:21
  56.4 1.3 collective-permute-start.7
  57.7 14.6 %all-to-all-done.3 = f32[4,8,16,2,256]{4,2,3,0,1:T(8,128)S(1)} async-done(((f32[4,8,16,2,256]{4,2,3,0,1:T(8,128)}), f32[4,8,16,2,256]{4,2,3,0,1:T(8,128)S(1)}, u32[]{:S(2)}, u32[]{:S(2)}) %all-to-all-start.3) | async-done | bytes 1048608 | tf_op jit(solution)/shard_map/all_to_all | solution.py:190
  72.6 91.5 %multiply_reduce_fusion = (f32[512,128]{1,0:T(8,128)S(1)}, f32[512,128]{1,0:T(8,128)S(1)}) fusion(f32[512,256]{1,0:T(8,128)S(1)} %slice_bitcast_fusion, f32[512,256]{1,0:T(8,128)S(1)} %get-tuple-element.17, s32[512,256]{1,0:T(8,128)S(1)} %broadcast_add_fusion, f32[512,256]{1,0:T(8,128)S(1)} %get-tuple-element.16, s32[512,256]{1,0:T(8,128)S(1)} %get-tuple-element.15), kind=kLoop, calls=%fused_computation | loop fusion | flops 134086656 | bytes 3145728 | tf_op jit(solution)/shard_map/reduce_sum | solution.py:65
  166.3 1.3 collective-permute-start.1
  167.7 2.5 %collective-permute-done.1 = f32[1,1,8,128]{3,2,1,0:T(8,128)S(1)} collective-permute-done((f32[1,1,8,128]{3,2,1,0:T(8,128)S(1)}, f32[1,1,8,128]{3,2,1,0:T(8,128)S(1)}, u32[]{:S(2)}, u32[]{:S(2)}) %collective-permute-start.1) | collective-permute-done | bytes 4128 | tf_op jit(solution)/shard_map/ppermute | solution.py:22
  170.2 3.0 %collective-permute-start.2 = (f32[1,10,1,128]{3,2,1,0:T(1,128)S(1)}, f32[1,10,1,128]{3,2,1,0:T(1,128)S(1)}, u32[]{:S(2)}, u32[]{:S(2)}) collective-permute-start(f32[1,10,1,128]{3,2,1,0:T(1,128)S(1)} %get-tuple-element.60), channel_id=1, source_target_pairs={{0,1},{1,2},{2,3},{3,4},{4,5},{5,6},{6,7},{8,9},{9,10},{10,11},{11... | collective-permute-start | bytes 15368 | tf_op jit(solution)/shard_map/ppermute | solution.py:21
  174.7 4.0 %collective-permute-done.3 = f32[1,10,1,128]{3,2,1,0:T(1,128)S(1)} collective-permute-done((f32[1,10,1,128]{3,2,1,0:T(1,128)S(1)}, f32[1,10,1,128]{3,2,1,0:T(1,128)S(1)}, u32[]{:S(2)}, u32[]{:S(2)}) %collective-permute-start.3) | collective-permute-done | bytes 5152 | tf_op jit(solution)/shard_map/ppermute | solution.py:22
  179.3 2.8 %collective-permute-start.8 = (f32[5,1,8,128]{3,2,1,0:T(8,128)S(1)}, f32[5,1,8,128]{3,2,1,0:T(8,128)S(1)}, u32[]{:S(2)}, u32[]{:S(2)}) collective-permute-start(f32[5,1,8,128]{3,2,1,0:T(8,128)S(1)} %get-tuple-element.40), channel_id=1, source_target_pairs={{0,8},{8,16},{16,24},{1,9},{9,17},{17,25},{2,10},{10,18},{18,26},{... | collective-permute-start | bytes 61448 | tf_op jit(solution)/shard_map/ppermute | solution.py:21
  183.5 2.7 %collective-permute-done.9 = f32[5,1,8,128]{3,2,1,0:T(8,128)S(1)} collective-permute-done((f32[5,1,8,128]{3,2,1,0:T(8,128)S(1)}, f32[5,1,8,128]{3,2,1,0:T(8,128)S(1)}, u32[]{:S(2)}, u32[]{:S(2)}) %collective-permute-start.9) | collective-permute-done | bytes 20512 | tf_op jit(solution)/shard_map/ppermute | solution.py:22
  186.3 2.8 %collective-permute-start.10 = (f32[5,10,1,128]{3,2,1,0:T(1,128)S(1)}, f32[5,10,1,128]{3,2,1,0:T(1,128)S(1)}, u32[]{:S(2)}, u32[]{:S(2)}) collective-permute-start(f32[5,10,1,128]{3,2,1,0:T(1,128)S(1)} %get-tuple-element.36), channel_id=1, source_target_pairs={{0,1},{1,2},{2,3},{3,4},{4,5},{5,6},{6,7},{8,9},{9,10},{10,11},{11... | collective-permute-start | bytes 76808 | tf_op jit(solution)/shard_map/ppermute | solution.py:21
  189.1 1.3 collective-permute-start.11
  190.6 4.2 %collective-permute-done.11 = f32[5,10,1,128]{3,2,1,0:T(1,128)S(1)} collective-permute-done((f32[5,10,1,128]{3,2,1,0:T(1,128)S(1)}, f32[5,10,1,128]{3,2,1,0:T(1,128)S(1)}, u32[]{:S(2)}, u32[]{:S(2)}) %collective-permute-start.11) | collective-permute-done | bytes 25632 | tf_op jit(solution)/shard_map/ppermute | solution.py:22
  195.3 3.0 %collective-permute-start.12 = (f32[3,1,8,128]{3,2,1,0:T(8,128)S(1)}, f32[3,1,8,128]{3,2,1,0:T(8,128)S(1)}, u32[]{:S(2)}, u32[]{:S(2)}) collective-permute-start(f32[3,1,8,128]{3,2,1,0:T(8,128)S(1)} %get-tuple-element.46), channel_id=1, source_target_pairs={{0,8},{8,16},{16,24},{1,9},{9,17},{17,25},{2,10},{10,18},{18,26},{... | collective-permute-start | bytes 36872 | tf_op jit(solution)/shard_map/ppermute | solution.py:21
  199.6 2.7 %collective-permute-done.13 = f32[3,1,8,128]{3,2,1,0:T(8,128)S(1)} collective-permute-done((f32[3,1,8,128]{3,2,1,0:T(8,128)S(1)}, f32[3,1,8,128]{3,2,1,0:T(8,128)S(1)}, u32[]{:S(2)}, u32[]{:S(2)}) %collective-permute-start.13) | collective-permute-done | bytes 12320 | tf_op jit(solution)/shard_map/ppermute | solution.py:22
  202.3 2.8 %collective-permute-start.14 = (f32[3,10,1,128]{3,2,1,0:T(1,128)S(1)}, f32[3,10,1,128]{3,2,1,0:T(1,128)S(1)}, u32[]{:S(2)}, u32[]{:S(2)}) collective-permute-start(f32[3,10,1,128]{3,2,1,0:T(1,128)S(1)} %get-tuple-element.42), channel_id=1, source_target_pairs={{0,1},{1,2},{2,3},{3,4},{4,5},{5,6},{6,7},{8,9},{9,10},{10,11},{11... | collective-permute-start | bytes 46088 | tf_op jit(solution)/shard_map/ppermute | solution.py:21
  205.1 1.3 collective-permute-start.15
  206.6 4.2 %collective-permute-done.15 = f32[3,10,1,128]{3,2,1,0:T(1,128)S(1)} collective-permute-done((f32[3,10,1,128]{3,2,1,0:T(1,128)S(1)}, f32[3,10,1,128]{3,2,1,0:T(1,128)S(1)}, u32[]{:S(2)}, u32[]{:S(2)}) %collective-permute-start.15) | collective-permute-done | bytes 15392 | tf_op jit(solution)/shard_map/ppermute | solution.py:22
  211.2 2.9 %collective-permute-start.16 = (f32[5,1,8,128]{3,2,1,0:T(8,128)S(1)}, f32[5,1,8,128]{3,2,1,0:T(8,128)S(1)}, u32[]{:S(2)}, u32[]{:S(2)}) collective-permute-start(f32[5,1,8,128]{3,2,1,0:T(8,128)S(1)} %get-tuple-element.38), channel_id=1, source_target_pairs={{0,8},{8,16},{16,24},{1,9},{9,17},{17,25},{2,10},{10,18},{18,26},{... | collective-permute-start | bytes 61448 | tf_op jit(solution)/shard_map/ppermute | solution.py:21
  214.2 1.3 collective-permute-start.17
  215.5 2.7 %collective-permute-done.17 = f32[5,1,8,128]{3,2,1,0:T(8,128)S(1)} collective-permute-done((f32[5,1,8,128]{3,2,1,0:T(8,128)S(1)}, f32[5,1,8,128]{3,2,1,0:T(8,128)S(1)}, u32[]{:S(2)}, u32[]{:S(2)}) %collective-permute-start.17) | collective-permute-done | bytes 20512 | tf_op jit(solution)/shard_map/ppermute | solution.py:22
  218.3 4.0 %collective-permute-start.18 = (f32[5,10,1,128]{3,2,1,0:T(1,128)S(1)}, f32[5,10,1,128]{3,2,1,0:T(1,128)S(1)}, u32[]{:S(2)}, u32[]{:S(2)}) collective-permute-start(f32[5,10,1,128]{3,2,1,0:T(1,128)S(1)} %get-tuple-element.34), channel_id=1, source_target_pairs={{0,1},{1,2},{2,3},{3,4},{4,5},{5,6},{6,7},{8,9},{9,10},{10,11},{11... | collective-permute-start | bytes 76808 | tf_op jit(solution)/shard_map/ppermute | solution.py:21
  223.7 4.2 %collective-permute-done.19 = f32[5,10,1,128]{3,2,1,0:T(1,128)S(1)} collective-permute-done((f32[5,10,1,128]{3,2,1,0:T(1,128)S(1)}, f32[5,10,1,128]{3,2,1,0:T(1,128)S(1)}, u32[]{:S(2)}, u32[]{:S(2)}) %collective-permute-start.19) | collective-permute-done | bytes 25632 | tf_op jit(solution)/shard_map/ppermute | solution.py:22
  (123 shorter events, 21.1 us)
Async XLA Ops:
  5.2 8.0 %all-to-all-start = ((s32[4,1,128]{2,1,0:T(1,128)}), s32[4,1,128]{2,1,0:T(1,128)S(1)}, u32[]{:S(2)}, u32[]{:S(2)}) async-start(s32[4,1,128]{2,1,0:T(1,128)} %reshape.171), calls=%async_computation | async-start | bytes 4096 | tf_op jit(solution)/shard_map/all_to_all | solution.py:198
  13.2 18.0 %all-to-all-start.2 = ((f32[4,8,16,2,256]{4,2,3,1,0:T(8,128)}), f32[4,8,16,2,256]{4,2,3,1,0:T(8,128)S(1)}, u32[]{:S(2)}, u32[]{:S(2)}) async-start(f32[4,8,16,2,256]{4,2,3,1,0:T(8,128)} %fusion.1), calls=%async_computation.2 | async-start | bytes 2097152 | tf_op jit(solution)/shard_map/all_to_all | solution.py:191
  31.2 12.8 %all-to-all-start.1 = ((s32[4,8,16]{2,0,1:T(4,128)}), s32[4,8,16]{2,0,1:T(4,128)S(1)}, u32[]{:S(2)}, u32[]{:S(2)}) async-start(s32[4,8,16]{2,0,1:T(4,128)} %copy.41), calls=%async_computation.1 | async-start | bytes 32768 | tf_op jit(solution)/shard_map/all_to_all | solution.py:197
  38.5 9.1 %copy-start = (f32[3,8,8,128]{3,2,1,0:T(8,128)S(1)}, f32[3,8,8,128]{3,2,1,0:T(8,128)}, u32[]{:S(2)}) copy-start(f32[3,8,8,128]{3,2,1,0:T(8,128)} %param.9) | copy-start | bytes 294916
  44.0 28.3 %all-to-all-start.3 = ((f32[4,8,16,2,256]{4,2,3,0,1:T(8,128)}), f32[4,8,16,2,256]{4,2,3,0,1:T(8,128)S(1)}, u32[]{:S(2)}, u32[]{:S(2)}) async-start(f32[4,8,16,2,256]{4,2,3,0,1:T(8,128)} %copy.45), calls=%async_computation.3 | async-start | bytes 2097152 | tf_op jit(solution)/shard_map/all_to_all | solution.py:190
  47.6 2.7 %collective-permute-start.4 = (f32[3,1,8,128]{3,2,1,0:T(8,128)S(1)}, f32[3,1,8,128]{3,2,1,0:T(8,128)S(1)}, u32[]{:S(2)}, u32[]{:S(2)}) collective-permute-start(f32[3,1,8,128]{3,2,1,0:T(8,128)S(1)} %get-tuple-element.49), channel_id=1, source_target_pairs={{0,8},{8,16},{16,24},{1,9},{9,17},{17,25},{2,10},{10,18},{18,26},{... | collective-permute-start | bytes 36872 | tf_op jit(solution)/shard_map/ppermute | solution.py:21
  48.9 3.7 %collective-permute-start.5 = (f32[3,1,8,128]{3,2,1,0:T(8,128)S(1)}, f32[3,1,8,128]{3,2,1,0:T(8,128)S(1)}, u32[]{:S(2)}, u32[]{:S(2)}) collective-permute-start(f32[3,1,8,128]{3,2,1,0:T(8,128)S(1)} %get-tuple-element.48), channel_id=1, source_target_pairs={{8,0},{16,8},{24,16},{9,1},{17,9},{25,17},{10,2},{18,10},{26,18},{... | collective-permute-start | bytes 36872 | tf_op jit(solution)/shard_map/ppermute | solution.py:22
  52.6 115.0 %collective-permute-start.6 = (f32[3,10,1,128]{3,2,1,0:T(1,128)S(1)}, f32[3,10,1,128]{3,2,1,0:T(1,128)S(1)}, u32[]{:S(2)}, u32[]{:S(2)}) collective-permute-start(f32[3,10,1,128]{3,2,1,0:T(1,128)S(1)} %get-tuple-element.44), channel_id=1, source_target_pairs={{0,1},{1,2},{2,3},{3,4},{4,5},{5,6},{6,7},{8,9},{9,10},{10,11},{11... | collective-permute-start | bytes 46088 | tf_op jit(solution)/shard_map/ppermute | solution.py:21
  56.4 111.2 %collective-permute-start.7 = (f32[3,10,1,128]{3,2,1,0:T(1,128)S(1)}, f32[3,10,1,128]{3,2,1,0:T(1,128)S(1)}, u32[]{:S(2)}, u32[]{:S(2)}) collective-permute-start(f32[3,10,1,128]{3,2,1,0:T(1,128)S(1)} %get-tuple-element.45), channel_id=1, source_target_pairs={{1,0},{2,1},{3,2},{4,3},{5,4},{6,5},{7,6},{9,8},{10,9},{11,10},{12... | collective-permute-start | bytes 46088 | tf_op jit(solution)/shard_map/ppermute | solution.py:22
  164.2 0.8 copy-start.4
  164.4 14.4 %copy-start.5 = (f32[8,8,128]{2,1,0:T(8,128)S(1)}, f32[8,8,128]{2,1,0:T(8,128)}, u32[]{:S(2)}) copy-start(f32[8,8,128]{2,1,0:T(8,128)} %param.10) | copy-start | bytes 98308
  165.0 14.0 %copy-start.1 = (f32[8,8,128]{2,1,0:T(8,128)}, f32[8,8,128]{2,1,0:T(8,128)S(1)}, u32[]{:S(2)}) copy-start(f32[8,8,128]{2,1,0:T(8,128)S(1)} %fusion.74) | copy-start | bytes 98308
  165.0 2.7 %collective-permute-start = (f32[1,1,8,128]{3,2,1,0:T(8,128)S(1)}, f32[1,1,8,128]{3,2,1,0:T(8,128)S(1)}, u32[]{:S(2)}, u32[]{:S(2)}) collective-permute-start(f32[1,1,8,128]{3,2,1,0:T(8,128)S(1)} %get-tuple-element.62), channel_id=1, source_target_pairs={{0,8},{8,16},{16,24},{1,9},{9,17},{17,25},{2,10},{10,18},{18,26},{... | collective-permute-start | bytes 12296 | tf_op jit(solution)/shard_map/ppermute | solution.py:21
  166.3 3.9 %collective-permute-start.1 = (f32[1,1,8,128]{3,2,1,0:T(8,128)S(1)}, f32[1,1,8,128]{3,2,1,0:T(8,128)S(1)}, u32[]{:S(2)}, u32[]{:S(2)}) collective-permute-start(f32[1,1,8,128]{3,2,1,0:T(8,128)S(1)} %get-tuple-element.63), channel_id=1, source_target_pairs={{8,0},{16,8},{24,16},{9,1},{17,9},{25,17},{10,2},{18,10},{26,18},{... | collective-permute-start | bytes 12296 | tf_op jit(solution)/shard_map/ppermute | solution.py:22
  170.2 4.5 %collective-permute-start.2 = (f32[1,10,1,128]{3,2,1,0:T(1,128)S(1)}, f32[1,10,1,128]{3,2,1,0:T(1,128)S(1)}, u32[]{:S(2)}, u32[]{:S(2)}) collective-permute-start(f32[1,10,1,128]{3,2,1,0:T(1,128)S(1)} %get-tuple-element.60), channel_id=1, source_target_pairs={{0,1},{1,2},{2,3},{3,4},{4,5},{5,6},{6,7},{8,9},{9,10},{10,11},{11... | collective-permute-start | bytes 15368 | tf_op jit(solution)/shard_map/ppermute | solution.py:21
  173.2 5.5 %collective-permute-start.3 = (f32[1,10,1,128]{3,2,1,0:T(1,128)S(1)}, f32[1,10,1,128]{3,2,1,0:T(1,128)S(1)}, u32[]{:S(2)}, u32[]{:S(2)}) collective-permute-start(f32[1,10,1,128]{3,2,1,0:T(1,128)S(1)} %get-tuple-element.61), channel_id=1, source_target_pairs={{1,0},{2,1},{3,2},{4,3},{5,4},{6,5},{7,6},{9,8},{10,9},{11,10},{12... | collective-permute-start | bytes 15368 | tf_op jit(solution)/shard_map/ppermute | solution.py:22
  179.3 15.7 %copy-start.3 = (f32[8,8,128]{2,1,0:T(8,128)S(1)}, f32[8,8,128]{2,1,0:T(8,128)}, u32[]{:S(2)}) copy-start(f32[8,8,128]{2,1,0:T(8,128)} %param.11) | copy-start | bytes 98308
  179.3 4.2 %collective-permute-start.8 = (f32[5,1,8,128]{3,2,1,0:T(8,128)S(1)}, f32[5,1,8,128]{3,2,1,0:T(8,128)S(1)}, u32[]{:S(2)}, u32[]{:S(2)}) collective-permute-start(f32[5,1,8,128]{3,2,1,0:T(8,128)S(1)} %get-tuple-element.40), channel_id=1, source_target_pairs={{0,8},{8,16},{16,24},{1,9},{9,17},{17,25},{2,10},{10,18},{18,26},{... | collective-permute-start | bytes 61448 | tf_op jit(solution)/shard_map/ppermute | solution.py:21
  182.2 4.1 %collective-permute-start.9 = (f32[5,1,8,128]{3,2,1,0:T(8,128)S(1)}, f32[5,1,8,128]{3,2,1,0:T(8,128)S(1)}, u32[]{:S(2)}, u32[]{:S(2)}) collective-permute-start(f32[5,1,8,128]{3,2,1,0:T(8,128)S(1)} %get-tuple-element.41), channel_id=1, source_target_pairs={{8,0},{16,8},{24,16},{9,1},{17,9},{25,17},{10,2},{18,10},{26,18},{... | collective-permute-start | bytes 61448 | tf_op jit(solution)/shard_map/ppermute | solution.py:22
  186.3 4.3 %collective-permute-start.10 = (f32[5,10,1,128]{3,2,1,0:T(1,128)S(1)}, f32[5,10,1,128]{3,2,1,0:T(1,128)S(1)}, u32[]{:S(2)}, u32[]{:S(2)}) collective-permute-start(f32[5,10,1,128]{3,2,1,0:T(1,128)S(1)} %get-tuple-element.36), channel_id=1, source_target_pairs={{0,1},{1,2},{2,3},{3,4},{4,5},{5,6},{6,7},{8,9},{9,10},{10,11},{11... | collective-permute-start | bytes 76808 | tf_op jit(solution)/shard_map/ppermute | solution.py:21
  189.1 5.7 %collective-permute-start.11 = (f32[5,10,1,128]{3,2,1,0:T(1,128)S(1)}, f32[5,10,1,128]{3,2,1,0:T(1,128)S(1)}, u32[]{:S(2)}, u32[]{:S(2)}) collective-permute-start(f32[5,10,1,128]{3,2,1,0:T(1,128)S(1)} %get-tuple-element.37), channel_id=1, source_target_pairs={{1,0},{2,1},{3,2},{4,3},{5,4},{6,5},{7,6},{9,8},{10,9},{11,10},{12... | collective-permute-start | bytes 76808 | tf_op jit(solution)/shard_map/ppermute | solution.py:22
  195.3 4.3 %collective-permute-start.12 = (f32[3,1,8,128]{3,2,1,0:T(8,128)S(1)}, f32[3,1,8,128]{3,2,1,0:T(8,128)S(1)}, u32[]{:S(2)}, u32[]{:S(2)}) collective-permute-start(f32[3,1,8,128]{3,2,1,0:T(8,128)S(1)} %get-tuple-element.46), channel_id=1, source_target_pairs={{0,8},{8,16},{16,24},{1,9},{9,17},{17,25},{2,10},{10,18},{18,26},{... | collective-permute-start | bytes 36872 | tf_op jit(solution)/shard_map/ppermute | solution.py:21
  198.3 4.0 %collective-permute-start.13 = (f32[3,1,8,128]{3,2,1,0:T(8,128)S(1)}, f32[3,1,8,128]{3,2,1,0:T(8,128)S(1)}, u32[]{:S(2)}, u32[]{:S(2)}) collective-permute-start(f32[3,1,8,128]{3,2,1,0:T(8,128)S(1)} %get-tuple-element.47), channel_id=1, source_target_pairs={{8,0},{16,8},{24,16},{9,1},{17,9},{25,17},{10,2},{18,10},{26,18},{... | collective-permute-start | bytes 36872 | tf_op jit(solution)/shard_map/ppermute | solution.py:22
  202.3 4.2 %collective-permute-start.14 = (f32[3,10,1,128]{3,2,1,0:T(1,128)S(1)}, f32[3,10,1,128]{3,2,1,0:T(1,128)S(1)}, u32[]{:S(2)}, u32[]{:S(2)}) collective-permute-start(f32[3,10,1,128]{3,2,1,0:T(1,128)S(1)} %get-tuple-element.42), channel_id=1, source_target_pairs={{0,1},{1,2},{2,3},{3,4},{4,5},{5,6},{6,7},{8,9},{9,10},{10,11},{11... | collective-permute-start | bytes 46088 | tf_op jit(solution)/shard_map/ppermute | solution.py:21
  205.1 5.6 %collective-permute-start.15 = (f32[3,10,1,128]{3,2,1,0:T(1,128)S(1)}, f32[3,10,1,128]{3,2,1,0:T(1,128)S(1)}, u32[]{:S(2)}, u32[]{:S(2)}) collective-permute-start(f32[3,10,1,128]{3,2,1,0:T(1,128)S(1)} %get-tuple-element.43), channel_id=1, source_target_pairs={{1,0},{2,1},{3,2},{4,3},{5,4},{6,5},{7,6},{9,8},{10,9},{11,10},{12... | collective-permute-start | bytes 46088 | tf_op jit(solution)/shard_map/ppermute | solution.py:22
  211.1 16.9 %copy-start.2 = (f32[8,8,128]{2,1,0:T(8,128)}, f32[8,8,128]{2,1,0:T(8,128)S(1)}, u32[]{:S(2)}) copy-start(f32[8,8,128]{2,1,0:T(8,128)S(1)} %get-tuple-element.6) | copy-start | bytes 98308
  211.2 4.2 %collective-permute-start.16 = (f32[5,1,8,128]{3,2,1,0:T(8,128)S(1)}, f32[5,1,8,128]{3,2,1,0:T(8,128)S(1)}, u32[]{:S(2)}, u32[]{:S(2)}) collective-permute-start(f32[5,1,8,128]{3,2,1,0:T(8,128)S(1)} %get-tuple-element.38), channel_id=1, source_target_pairs={{0,8},{8,16},{16,24},{1,9},{9,17},{17,25},{2,10},{10,18},{18,26},{... | collective-permute-start | bytes 61448 | tf_op jit(solution)/shard_map/ppermute | solution.py:21
  214.2 4.0 %collective-permute-start.17 = (f32[5,1,8,128]{3,2,1,0:T(8,128)S(1)}, f32[5,1,8,128]{3,2,1,0:T(8,128)S(1)}, u32[]{:S(2)}, u32[]{:S(2)}) collective-permute-start(f32[5,1,8,128]{3,2,1,0:T(8,128)S(1)} %get-tuple-element.39), channel_id=1, source_target_pairs={{8,0},{16,8},{24,16},{9,1},{17,9},{25,17},{10,2},{18,10},{26,18},{... | collective-permute-start | bytes 61448 | tf_op jit(solution)/shard_map/ppermute | solution.py:22
  218.3 5.5 %collective-permute-start.18 = (f32[5,10,1,128]{3,2,1,0:T(1,128)S(1)}, f32[5,10,1,128]{3,2,1,0:T(1,128)S(1)}, u32[]{:S(2)}, u32[]{:S(2)}) collective-permute-start(f32[5,10,1,128]{3,2,1,0:T(1,128)S(1)} %get-tuple-element.34), channel_id=1, source_target_pairs={{0,1},{1,2},{2,3},{3,4},{4,5},{5,6},{6,7},{8,9},{9,10},{10,11},{11... | collective-permute-start | bytes 76808 | tf_op jit(solution)/shard_map/ppermute | solution.py:21
  222.2 5.7 %collective-permute-start.19 = (f32[5,10,1,128]{3,2,1,0:T(1,128)S(1)}, f32[5,10,1,128]{3,2,1,0:T(1,128)S(1)}, u32[]{:S(2)}, u32[]{:S(2)}) collective-permute-start(f32[5,10,1,128]{3,2,1,0:T(1,128)S(1)} %get-tuple-element.35), channel_id=1, source_target_pairs={{1,0},{2,1},{3,2},{4,3},{5,4},{6,5},{7,6},{9,8},{10,9},{11,10},{12... | collective-permute-start | bytes 76808 | tf_op jit(solution)/shard_map/ppermute | solution.py:22
where the time goes:
time: 231 us; the launch traced here: 229 us
  other arithmetic  97.2 us (42%)
  waiting for transfers between devices  62.5 us (27%)
  starting transfers between devices  58.2 us (25%)
  local copies, waits for them, and re-layouts  6.92 us (3%)
    reduce_sum x1, other arithmetic, column_profile(): value_sum = jnp.sum(weight * values[..., None], axis=1)  91.5 us
    ppermute x10, waiting for transfers between devices, extended(): after = lax.ppermute(first, axis, down)  29.6 us
    ppermute x10, starting transfers between devices, extended(): before = lax.ppermute(last, axis, up)  27.7 us
    all_to_all x1, waiting for transfers between devices, shards(): lax.all_to_all(lax.all_to_all(send_buf, 'gx', split_axis=0, concat_axis=0...  14.6 us
    ppermute x10, starting transfers between devices, extended(): after = lax.ppermute(first, axis, down)  12.9 us
    all_to_all x1, waiting for transfers between devices, shards(): lax.all_to_all(send_buf, 'gx', split_axis=0, concat_axis=0, tiled=True)  12.6 us
    all_to_all x1, starting transfers between devices, shards(): lax.all_to_all(lax.all_to_all(col_buffer, 'gx', split_axis=0, concat_axis...  6.25 us
    all_to_all x1, waiting for transfers between devices, shards(): lax.all_to_all(lax.all_to_all(col_buffer, 'gx', split_axis=0, concat_axis...  5.52 us
  transfers between devices with their start and end apart: 24, of which 14 were waited for; matrix products, arithmetic and copies ran while one was open for 44% of the time, Pallas kernels for 0%

commit v1 on v0

v1 whole, which is shorter than its diff:
```python
import functools

import jax
import jax.numpy as jnp
from jax import lax
from jax.experimental import pallas as pl
from jax.experimental.pallas import tpu as pltpu
from jax.sharding import PartitionSpec as P

ITERS = 2
HALO = 2

PRESS_STEP = 0.5
VEL_STEP = 0.05
DAMPING = 0.8

F32 = jnp.float32
BF16 = jnp.bfloat16
VMEM = pl.BlockSpec(memory_space=pltpu.VMEM)
SMEM = pl.BlockSpec(memory_space=pltpu.SMEM)
NT = (((1,), (1,)), ((), ()))
TN = (((0,), (0,)), ((), ()))


def split3(x):
    high = x.astype(BF16)
    rest = x - high.astype(F32)
    mid = rest.astype(BF16)
    low = (rest - mid.astype(F32)).astype(BF16)
    return high, mid, low


def deposit_kernel(
    num_owners, capacity, count_ref, owner_ref, column_ref, value_ref, height_ref, out_ref, part_ref
):
    blocks, marks = value_ref.shape
    num_levels = out_ref.shape[1] // 2
    row8 = lax.broadcasted_iota(jnp.int32, (8, marks), 0)
    upper_part = (row8 & 1) == 1
    with_value = (row8 & 2) == 0
    leading = row8 < 4
    level = lax.broadcasted_iota(jnp.int32, (num_levels, marks), 0).astype(F32).astype(BF16)

    def one_block(b):
        height = jnp.broadcast_to(height_ref[pl.ds(b, 1), :], (8, marks))
        value = jnp.broadcast_to(value_ref[pl.ds(b, 1), :], (8, marks))
        lower = jnp.minimum(jnp.floor(height), num_levels - 2.0)
        fraction = height - lower
        share = jnp.where(upper_part, fraction, 1.0 - fraction)
        share = share * jnp.where(with_value, value, 1.0)
        high = share.astype(BF16).astype(F32)
        pieces = jnp.where(leading, high, share - high)
        pieces = jnp.concatenate([pieces, pieces], axis=0).astype(BF16)
        lower16 = jnp.concatenate([lower, lower], axis=0).astype(BF16)
        lower_all = jnp.concatenate([lower16] * (num_levels // 16), axis=0)
        hot = jnp.where(lower_all == level, jnp.ones((), BF16), jnp.zeros((), BF16))
        sums = lax.dot_general(pieces, hot, NT, preferred_element_type=F32)
        part_ref[pl.ds(pl.multiple_of(b * 8, 8), 8), :] = sums[:8]

    def some_blocks(step, carry):
        for k in range(8):
            one_block(step * 8 + k)
        return carry

    lax.fori_loop(0, blocks // 8, some_blocks, 0)

    def part(kind):
        high = part_ref[pl.ds(kind, blocks, stride=8), :]
        return high + part_ref[pl.ds(kind + 4, blocks, stride=8), :]

    value_sum = part(0) + pltpu.roll(part(1), 1, 1)
    weight_sum = part(2) + pltpu.roll(part(3), 1, 1)

    owner = owner_ref[...]
    block_id = lax.broadcasted_iota(jnp.int32, (1, blocks), 1)
    owner = jnp.where(block_id < count_ref[0], owner, num_owners)
    owned = lax.broadcasted_iota(jnp.int32, (num_owners, blocks), 0) == owner
    hits = jnp.where(owned, 1.0, 0.0)
    earlier = jnp.where(
        lax.broadcasted_iota(jnp.int32, (blocks, blocks), 0)
        < lax.broadcasted_iota(jnp.int32, (blocks, blocks), 1),
        1.0,
        0.0,
    ).astype(BF16)
    before = jnp.dot(hits.astype(BF16), earlier, preferred_element_type=F32)
    rank = jnp.sum(hits * before, axis=0, keepdims=True)
    slot = owner * capacity + rank.astype(jnp.int32)
    slots = num_owners * capacity
    place = jnp.where(
        lax.broadcasted_iota(jnp.int32, (slots, blocks), 0) == slot, 1.0, 0.0
    ).astype(BF16)
    code = jnp.broadcast_to((column_ref[...] + 1).astype(F32), (num_levels, blocks)).astype(BF16)
    codes = lax.dot_general(place, code, NT, preferred_element_type=F32)

    def placed(x):
        high, mid, low = (jnp.dot(place, y, preferred_element_type=F32) for y in split3(x))
        return high + (mid + low)

    out_ref[:, :num_levels] = placed(value_sum)
    lane = lax.broadcasted_iota(jnp.int32, (slots, num_levels), 1)
    out_ref[:, num_levels:] = jnp.where(lane == num_levels - 1, codes, placed(weight_sum))


def deposit(count, owner, column, value, height, num_owners, capacity, num_levels):
    blocks, marks = value.shape
    return pl.pallas_call(
        functools.partial(deposit_kernel, num_owners, capacity),
        out_shape=jax.ShapeDtypeStruct((num_owners * capacity, 2 * num_levels), F32),
        in_specs=[SMEM, VMEM, VMEM, VMEM, VMEM],
        out_specs=VMEM,
        scratch_shapes=[pltpu.VMEM((blocks * 8, num_levels), F32)],
        compiler_params=pltpu.CompilerParams(vmem_limit_bytes=48 << 20),
        name="deposit",
    )(count, owner.reshape(1, blocks), column.reshape(1, blocks), value, height)


def gather_kernel(marks, arrived_ref, background_ref, out_ref):
    slots = arrived_ref.shape[0]
    columns, num_levels = out_ref.shape
    values = arrived_ref[:, :num_levels]
    weights = arrived_ref[:, num_levels:]
    lane = lax.broadcasted_iota(jnp.int32, (slots, num_levels), 1)
    last = lane == num_levels - 1
    code = weights[:, num_levels - 1 :]
    others = jnp.sum(jnp.where(last, 0.0, weights), axis=1, keepdims=True)
    weights = jnp.where(last, float(marks) - others, weights)
    place = jnp.where(code == (lane + 1).astype(F32), 1.0, 0.0).astype(BF16)

    def placed(x):
        high, mid, low = (
            lax.dot_general(place, y, TN, preferred_element_type=F32)[:columns] for y in split3(x)
        )
        return high + (mid + low)

    out_ref[...] = jnp.exp((placed(values) + background_ref[...]) / (placed(weights) + 1.0))


def gather(arrived, background, marks):
    cells_x, cells_y, num_levels = background.shape
    out = pl.pallas_call(
        functools.partial(gather_kernel, marks),
        out_shape=jax.ShapeDtypeStruct((cells_x * cells_y, num_levels), F32),
        in_specs=[VMEM, VMEM],
        out_specs=VMEM,
        compiler_params=pltpu.CompilerParams(vmem_limit_bytes=48 << 20),
        name="gather",
    )(arrived, background.reshape(cells_x * cells_y, num_levels))
    return out.reshape(cells_x, cells_y, num_levels)


def stokes_kernel(
    cells_y,
    limits_ref,
    vel_ref,
    press_ref,
    buoy_ref,
    visc_ref,
    new_vel_ref,
    new_press_ref,
):
    wide_x, rows, num_levels = visc_ref.shape
    cells_x = wide_x - 2 * HALO
    row = lax.broadcasted_iota(jnp.int32, (rows, num_levels), 0)
    lane = lax.broadcasted_iota(jnp.int32, (rows, num_levels), 1)
    first_x, size_x, first_y, size_y = (limits_ref[k] for k in range(4))
    at_y = row + (first_y - HALO)
    in_y = (at_y >= 0) & (at_y < size_y)
    in_y_face = (at_y >= 0) & (at_y < size_y - 1)
    low_lane = lane == 0
    high_lane = lane == num_levels - 1

    def north(f):
        return pltpu.roll(f, rows - 1, 0)

    def south(f):
        return pltpu.roll(f, 1, 0)

    def upper(f):
        return jnp.where(high_lane, 0.0, pltpu.roll(f, num_levels - 1, 1))

    def lower(f):
        return jnp.where(low_lane, 0.0, pltpu.roll(f, 1, 1))

    def in_x(x):
        at_x = first_x - HALO + x
        return (at_x >= 0) & (at_x < size_x)

    def in_x_face(x):
        at_x = first_x - HALO + x
        return (at_x >= 0) & (at_x < size_x - 1)

    visc = [visc_ref[x] for x in range(wide_x)]
    vel = [[vel_ref[c, x] for x in range(wide_x)] for c in range(3)]
    press = [press_ref[x] for x in range(wide_x)]
    side_x = [visc[x] + visc[x + 1] for x in range(wide_x - 1)]
    side_y = [visc[x] + north(visc[x]) for x in range(wide_x)]
    side_z = [visc[x] + upper(visc[x]) for x in range(wide_x)]
    corner_xy = [0.25 * (side_y[x] + side_y[x + 1]) for x in range(wide_x - 1)]
    corner_xz = [0.25 * (side_x[x] + upper(side_x[x])) for x in range(wide_x - 1)]
    corner_yz = [0.25 * (side_y[x] + upper(side_y[x])) for x in range(wide_x)]
    rate_x = [(2.0 * VEL_STEP) / side for side in side_x]
    rate_y = [(2.0 * VEL_STEP) / side for side in side_y]
    rate_z = [(2.0 * VEL_STEP) / side for side in side_z]
    moment = [[None] * wide_x for _ in range(3)]
    for sweep in range(ITERS):
        begin, end = sweep, wide_x - sweep
        sig_x, sig_y, sig_z = {}, {}, {}
        tau_xy, tau_xz, tau_yz = {}, {}, {}
        for x in range(begin, end):
            u, v, w = vel[0][x], vel[1][x], vel[2][x]
            if x > begin:
                grad_x = u - vel[0][x - 1]
                grad_y = v - south(v)
                grad_z = w - lower(w)
                div = grad_x + grad_y + grad_z
                press[x] = press[x] - PRESS_STEP * visc[x] * div
                third = div / 3.0
                twice = 2.0 * visc[x]
                sig_x[x] = twice * (grad_x - third) - press[x]
                sig_y[x] = twice * (grad_y - third) - press[x]
                sig_z[x] = twice * (grad_z - third) - press[x]
                tau_yz[x] = jnp.where(
                    in_y, corner_yz[x] * (upper(v) - v + north(w) - w), 0.0
                )
            if x < end - 1:
                inside = in_y & in_x(x)
                tau_xy[x] = jnp.where(
                    inside, corner_xy[x] * (north(u) - u + vel[1][x + 1] - v), 0.0
                )
                tau_xz[x] = jnp.where(
                    in_x(x), corner_xz[x] * (upper(u) - u + vel[2][x + 1] - w), 0.0
                )
        fresh = [[None] * wide_x for _ in range(3)]
        for x in range(begin + 1, end - 1):
            res_x = (
                sig_x[x + 1]
                - sig_x[x]
                + tau_xy[x]
                - south(tau_xy[x])
                + tau_xz[x]
                - lower(tau_xz[x])
            )
            res_y = (
                tau_xy[x]
                - tau_xy[x - 1]
                + north(sig_y[x])
                - sig_y[x]
                + tau_yz[x]
                - lower(tau_yz[x])
            )
            res_z = (
                tau_xz[x]
                - tau_xz[x - 1]
                + tau_yz[x]
                - south(tau_yz[x])
                + upper(sig_z[x])
                - sig_z[x]
                + buoy_ref[x]
            )
            masks = (
                in_y & in_x_face(x),
                in_y_face & in_x(x),
                (in_y & jnp.logical_not(high_lane)) & in_x(x),
            )
            for c, (res, rate, mask) in enumerate(
                zip((res_x, res_y, res_z), (rate_x, rate_y, rate_z), masks)
            ):
                if sweep > 0:
                    res = DAMPING * moment[c][x] + res
                moment[c][x] = res
                fresh[c][x] = jnp.where(mask, vel[c][x] + res * rate[x], 0.0)
        vel = fresh
    for x in range(cells_x):
        for c in range(3):
            new_vel_ref[c, x] = vel[c][x + HALO][HALO : HALO + cells_y]
        new_press_ref[x] = press[x + HALO][HALO : HALO + cells_y]


def stokes(limits, vel, press, buoy, visc, cells_y):
    wide_x, _, num_levels = visc.shape
    cells_x = wide_x - 2 * HALO
    return pl.pallas_call(
        functools.partial(stokes_kernel, cells_y),
        out_shape=(
            jax.ShapeDtypeStruct((3, cells_x, cells_y, num_levels), F32),
            jax.ShapeDtypeStruct((cells_x, cells_y, num_levels), F32),
        ),
        in_specs=[SMEM] + [VMEM] * 4,
        out_specs=(VMEM, VMEM),
        compiler_params=pltpu.CompilerParams(vmem_limit_bytes=48 << 20),
        name="stokes",
    )(limits, vel, press, buoy, visc)


def shifted(x, axis, dim, width):
    devices, length = lax.axis_size(axis), x.shape[dim]
    up = [(i, i + 1) for i in range(devices - 1)]
    down = [(j, i) for i, j in up]
    last = lax.slice_in_dim(x, length - width, length, axis=dim)
    first = lax.slice_in_dim(x, 0, width, axis=dim)
    return lax.ppermute(last, axis, up), lax.ppermute(first, axis, down)


def widened(x):
    before, after = shifted(x, "gx", x.ndim - 3, HALO)
    x = jnp.concatenate([before, x, after], axis=x.ndim - 3)
    before, after = shifted(x, "gy", x.ndim - 2, HALO)
    rows = x.shape[-2] + 2 * HALO
    pad = jnp.zeros(x.shape[:-2] + (-rows % 8, x.shape[-1]), x.dtype)
    return jnp.concatenate([before, x, after, pad], axis=x.ndim - 2)


def shards(
    velocity,
    pressure,
    buoyancy,
    background,
    marker_value,
    marker_height,
    marker_owner,
    marker_column,
    block_count,
):
    cells_x, cells_y, num_levels = pressure.shape
    block_rows, marks = marker_value.shape
    size_x = lax.axis_size("gx")
    size_y = lax.axis_size("gy")
    devices = size_x * size_y
    capacity = max(2, (2 * block_rows + devices - 1) // devices)
    send = deposit(
        block_count,
        marker_owner,
        marker_column,
        marker_value,
        marker_height,
        devices,
        capacity,
        num_levels,
    )
    arrived = lax.all_to_all(
        send.reshape(devices, capacity, 2 * num_levels),
        ("gx", "gy"),
        split_axis=0,
        concat_axis=0,
        tiled=True,
    ).reshape(devices * capacity, 2 * num_levels)
    fields = widened(jnp.concatenate([velocity, pressure[None], buoyancy[None]], axis=0))
    viscosity = gather(arrived, background, marks)
    visc = widened(viscosity)
    limits = jnp.stack(
        [
            lax.axis_index("gx") * cells_x,
            jnp.int32(size_x * cells_x),
            lax.axis_index("gy") * cells_y,
            jnp.int32(size_y * cells_y),
        ]
    ).astype(jnp.int32)
    new_vel, new_press = stokes(limits, fields[:3], fields[3], fields[4], visc, cells_y)
    return (new_vel, new_press, viscosity)


def solution(mesh):
    return jax.shard_map(
        shards,
        mesh=mesh,
        in_specs=(
            P(None, "gx", "gy", None),
            P("gx", "gy", None),
            P("gx", "gy", None),
            P("gx", "gy", None),
            P(("gx", "gy"), None),
            P(("gx", "gy"), None),
            P(("gx", "gy"), None),
            P(("gx", "gy")),
            P(("gx", "gy")),
        ),
        out_specs=(P(None, "gx", "gy", None), P("gx", "gy", None), P("gx", "gy", None)),
        check_vma=False,
    )
```

time: 231 us -> 55.7 us (0.24)
  other arithmetic: 97.2 us -> 0.34 us
  waiting for transfers between devices: 62.5 us -> 14.5 us
  starting transfers between devices: 58.2 us -> 22.1 us
  Pallas kernels: 0 us -> 12.8 us
  local copies, waits for them, and re-layouts: 6.92 us -> 3.43 us
    reduce_sum x3 -> x0, other arithmetic: 92.4 us -> none  [the longest x1 91.5 us: column_profile(): value_sum = jnp.sum(weight * values[..., None], axis=1)]
    all_to_all x4 -> x1, waiting for transfers between devices: 32.6 us -> 5.17 us  [shards(): lax.all_to_all(send.reshape(devices, capacity, 2 * num_levels), ('gx', 'g...]
    ppermute x20 -> x8, starting transfers between devices: 40.6 us -> 14.8 us  [shifted(): return (lax.ppermute(last, axis, up), lax.ppermute(first, axis, down))]
    ppermute x20 -> x8, waiting for transfers between devices: 29.9 us -> 9.31 us  [shifted(): return (lax.ppermute(last, axis, up), lax.ppermute(first, axis, down))]
    pallas_call x0 -> x3, Pallas kernels: none -> 12.8 us  [the longest x1 9.82 us: deposit(): pl.pallas_call(functools.partial(deposit_kernel, num_owners, capacity), o...]
    all_to_all x4 -> x1, starting transfers between devices: 17.6 us -> 7.3 us  [shards(): lax.all_to_all(send.reshape(devices, capacity, 2 * num_levels), ('gx', 'g...]
  transfers between devices with their start and end apart: 24 -> 9, of which waited for: 14 -> 4; matrix products, arithmetic and copies ran while one was open for 44% -> 2% of each run, Pallas kernels for 0% -> 2%
where the time goes in v1:
time: 55.7 us; the launch traced here: 54.7 us
  starting transfers between devices  22.1 us (40%)
  waiting for transfers between devices  14.5 us (26%)
  Pallas kernels  12.8 us (23%)
  local copies, waits for them, and re-layouts  3.43 us (6%)
  between operations  1.48 us (3%)
    ppermute x8, starting transfers between devices, shifted(): return (lax.ppermute(last, axis, up), lax.ppermute(first, axis, down))  14.8 us
    pallas_call x1, Pallas kernels, deposit(): pl.pallas_call(functools.partial(deposit_kernel, num_owners, capacity), o...  9.82 us
    ppermute x8, waiting for transfers between devices, shifted(): return (lax.ppermute(last, axis, up), lax.ppermute(first, axis, down))  9.31 us
    all_to_all x1, starting transfers between devices, shards(): lax.all_to_all(send.reshape(devices, capacity, 2 * num_levels), ('gx', 'g...  7.3 us
    all_to_all x1, waiting for transfers between devices, shards(): lax.all_to_all(send.reshape(devices, capacity, 2 * num_levels), ('gx', 'g...  5.17 us
    unnamed x18, local copies, waits for them, and re-layouts  2.6 us
    pallas_call x1, Pallas kernels, stokes(): pl.pallas_call(functools.partial(stokes_kernel, cells_y), out_shape=(jax....  1.8 us
    pallas_call x1, Pallas kernels, gather(): pl.pallas_call(functools.partial(gather_kernel, marks), out_shape=jax.Sha...  1.18 us
  transfers between devices with their start and end apart: 9, of which 4 were waited for; matrix products, arithmetic and copies ran while one was open for 2% of the time, Pallas kernels for 2%

profile of v1, /device:TPU:0, one launch (start us, length us, event | category | flops | bytes accessed | tf_op | source)
XLA Modules:
  0.0 54.7 jit_solution(5403674154649180118)
XLA Ops:
  1.3 0.0 copy-start.4
  1.3 0.7 %copy-done.4 = s32[256]{0:T(256)S(1)} copy-done((s32[256]{0:T(256)S(1)}, s32[256]{0:T(256)}, u32[]{:S(2)}) %copy-start.4) | copy-done | bytes 1048
  2.0 0.0 copy-done.3
  2.0 0.9 %copy-done = f32[256,256]{1,0:T(8,128)S(1)} copy-done((f32[256,256]{1,0:T(8,128)S(1)}, f32[256,256]{1,0:T(8,128)}, u32[]{:S(2)}) %copy-start) | copy-done | bytes 262168
  2.9 0.9 %copy-done.1 = f32[256,256]{1,0:T(8,128)S(1)} copy-done((f32[256,256]{1,0:T(8,128)S(1)}, f32[256,256]{1,0:T(8,128)}, u32[]{:S(2)}) %copy-start.1) | copy-done | bytes 262168
  3.9 9.8 %deposit.1 = f32[512,256]{1,0:T(8,128)} custom-call(s32[1]{0:T(128)S(6)} %copy.12.count_ref, s32[1,256]{1,0:T(1,128)S(1)} %bitcast.20, s32[1,256]{1,0:T(1,128)S(1)} %bitcast.21, f32[256,256]{1,0:T(8,128)S(1)} %copy-done, f32[256,256]{1,0:T(8,128)S(1)} %copy-done.1), custom_call_target="tpu_custom_call" | custom-call | tf_op jit(solution)/shard_map/deposit/pallas_call | solution.py:106
  13.7 7.3 %all-to-all-start = ((f32[32,16,256]{2,1,0:T(8,128)}), f32[32,16,256]{2,1,0:T(8,128)S(1)}, u32[]{:S(2)}, u32[]{:S(2)}) async-start(f32[32,16,256]{2,1,0:T(8,128)} %bitcast.8), calls=%async_computation | async-start | bytes 1048576 | tf_op jit(solution)/shard_map/all_to_all | solution.py:340
  21.0 2.2 %collective-permute-start = (f32[5,2,8,128]{3,2,1,0:T(8,128)S(1)}, f32[5,2,8,128]{3,2,1,0:T(8,128)S(1)}, u32[]{:S(2)}, u32[]{:S(2)}) collective-permute-start(f32[5,2,8,128]{3,2,1,0:T(8,128)S(1)} %get-tuple-element.11), channel_id=1, source_target_pairs={{0,8},{8,16},{16,24},{1,9},{9,17},{17,25},{2,10},{10,18},{18,26},{... | collective-permute-start | bytes 122888 | tf_op jit(solution)/shard_map/ppermute | solution.py:301
  23.2 1.3 %collective-permute-start.1 = (f32[5,2,8,128]{3,2,1,0:T(8,128)S(1)}, f32[5,2,8,128]{3,2,1,0:T(8,128)S(1)}, u32[]{:S(2)}, u32[]{:S(2)}) collective-permute-start(f32[5,2,8,128]{3,2,1,0:T(8,128)S(1)} %get-tuple-element.12), channel_id=1, source_target_pairs={{8,0},{16,8},{24,16},{9,1},{17,9},{25,17},{10,2},{18,10},{26,18},{... | collective-permute-start | bytes 122888 | tf_op jit(solution)/shard_map/ppermute | solution.py:301
  24.5 0.1 pad_add_fusion.limits_ref
  24.6 0.1 pad.16.clone
  24.7 0.0 collective-permute-done
  24.7 2.8 %collective-permute-done.1 = f32[5,2,8,128]{3,2,1,0:T(8,128)S(1)} collective-permute-done((f32[5,2,8,128]{3,2,1,0:T(8,128)S(1)}, f32[5,2,8,128]{3,2,1,0:T(8,128)S(1)}, u32[]{:S(2)}, u32[]{:S(2)}) %collective-permute-start.1) | collective-permute-done | bytes 40992 | tf_op jit(solution)/shard_map/ppermute | solution.py:301
  27.5 3.4 %collective-permute-start.2 = (f32[5,12,2,128]{3,2,1,0:T(2,128)S(1)}, f32[5,12,2,128]{3,2,1,0:T(2,128)S(1)}, u32[]{:S(2)}, u32[]{:S(2)}) collective-permute-start(f32[5,12,2,128]{3,2,1,0:T(2,128)S(1)} %get-tuple-element.9), channel_id=1, source_target_pairs={{0,1},{1,2},{2,3},{3,4},{4,5},{5,6},{6,7},{8,9},{9,10},{10,11},{11... | collective-permute-start | bytes 184328 | tf_op jit(solution)/shard_map/ppermute | solution.py:301
  30.9 1.3 %collective-permute-start.3 = (f32[5,12,2,128]{3,2,1,0:T(2,128)S(1)}, f32[5,12,2,128]{3,2,1,0:T(2,128)S(1)}, u32[]{:S(2)}, u32[]{:S(2)}) collective-permute-start(f32[5,12,2,128]{3,2,1,0:T(2,128)S(1)} %get-tuple-element.10), channel_id=1, source_target_pairs={{1,0},{2,1},{3,2},{4,3},{5,4},{6,5},{7,6},{9,8},{10,9},{11,10},{12... | collective-permute-start | bytes 184328 | tf_op jit(solution)/shard_map/ppermute | solution.py:301
  32.2 5.2 %all-to-all-done = f32[32,16,256]{2,1,0:T(8,128)S(1)} async-done(((f32[32,16,256]{2,1,0:T(8,128)}), f32[32,16,256]{2,1,0:T(8,128)S(1)}, u32[]{:S(2)}, u32[]{:S(2)}) %all-to-all-start) | async-done | bytes 524320 | tf_op jit(solution)/shard_map/all_to_all | solution.py:340
  37.4 1.2 %gather.1 = f32[64,128]{1,0:T(8,128)} custom-call(f32[512,256]{1,0:T(8,128)S(1)} %bitcast.18, f32[64,128]{1,0:T(8,128)S(1)} %bitcast.19), custom_call_target="tpu_custom_call" | custom-call | tf_op jit(solution)/shard_map/gather/pallas_call | solution.py:140
  38.5 0.7 %slice_bitcast_fusion.3 = (f32[2,8,128]{2,1,0:T(8,128)S(1)}, f32[2,8,128]{2,1,0:T(8,128)S(1)}) fusion(f32[64,128]{1,0:T(8,128)} %gather.1), kind=kLoop, calls=%fused_computation.16 | loop fusion | bytes 32768 | tf_op jit(solution)/shard_map/slice | solution.py:299
  39.3 1.4 %collective-permute-start.4 = (f32[2,8,128]{2,1,0:T(8,128)S(1)}, f32[2,8,128]{2,1,0:T(8,128)S(1)}, u32[]{:S(2)}, u32[]{:S(2)}) collective-permute-start(f32[2,8,128]{2,1,0:T(8,128)S(1)} %get-tuple-element.15), channel_id=1, source_target_pairs={{0,8},{8,16},{16,24},{1,9},{9,17},{17,25},{2,10},{10,18},{18,26},{... | collective-permute-start | bytes 24584 | tf_op jit(solution)/shard_map/ppermute | solution.py:301
  40.6 0.0 copy-start.6
  40.6 1.3 %collective-permute-start.5 = (f32[2,8,128]{2,1,0:T(8,128)S(1)}, f32[2,8,128]{2,1,0:T(8,128)S(1)}, u32[]{:S(2)}, u32[]{:S(2)}) collective-permute-start(f32[2,8,128]{2,1,0:T(8,128)S(1)} %get-tuple-element.16), channel_id=1, source_target_pairs={{8,0},{16,8},{24,16},{9,1},{17,9},{25,17},{10,2},{18,10},{26,18},{... | collective-permute-start | bytes 24584 | tf_op jit(solution)/shard_map/ppermute | solution.py:301
  41.9 0.0 collective-permute-done.2
  42.0 0.0 collective-permute-done.3
  42.0 0.1 maximum_maximum_fusion
  42.1 0.0 collective-permute-done.4
  42.1 2.3 %collective-permute-done.5 = f32[2,8,128]{2,1,0:T(8,128)S(1)} collective-permute-done((f32[2,8,128]{2,1,0:T(8,128)S(1)}, f32[2,8,128]{2,1,0:T(8,128)S(1)}, u32[]{:S(2)}, u32[]{:S(2)}) %collective-permute-start.5) | collective-permute-done | bytes 8224 | tf_op jit(solution)/shard_map/ppermute | solution.py:301
  44.4 2.8 %collective-permute-start.6 = (f32[12,2,128]{2,1,0:T(2,128)S(1)}, f32[12,2,128]{2,1,0:T(2,128)S(1)}, u32[]{:S(2)}, u32[]{:S(2)}) collective-permute-start(f32[12,2,128]{2,1,0:T(2,128)S(1)} %get-tuple-element.13), channel_id=1, source_target_pairs={{0,1},{1,2},{2,3},{3,4},{4,5},{5,6},{6,7},{8,9},{9,10},{10,11},{11... | collective-permute-start | bytes 36872 | tf_op jit(solution)/shard_map/ppermute | solution.py:301
  47.2 1.3 %collective-permute-start.7 = (f32[12,2,128]{2,1,0:T(2,128)S(1)}, f32[12,2,128]{2,1,0:T(2,128)S(1)}, u32[]{:S(2)}, u32[]{:S(2)}) collective-permute-start(f32[12,2,128]{2,1,0:T(2,128)S(1)} %get-tuple-element.14), channel_id=1, source_target_pairs={{1,0},{2,1},{3,2},{4,3},{5,4},{6,5},{7,6},{9,8},{10,9},{11,10},{12... | collective-permute-start | bytes 36872 | tf_op jit(solution)/shard_map/ppermute | solution.py:301
  48.6 0.0 collective-permute-done.6
  48.6 4.2 %collective-permute-done.7 = f32[12,2,128]{2,1,0:T(2,128)S(1)} collective-permute-done((f32[12,2,128]{2,1,0:T(2,128)S(1)}, f32[12,2,128]{2,1,0:T(2,128)S(1)}, u32[]{:S(2)}, u32[]{:S(2)}) %collective-permute-start.7) | collective-permute-done | bytes 12320 | tf_op jit(solution)/shard_map/ppermute | solution.py:301
  52.8 0.1 maximum_maximum_fusion.1.visc_ref
  52.9 1.8 %stokes.1 = (f32[3,8,8,128]{3,2,1,0:T(8,128)}, f32[8,8,128]{2,1,0:T(8,128)}) custom-call(s32[4]{0:T(128)S(1)} %pad_add_fusion.limits_ref, f32[3,12,16,128]{3,2,1,0:T(8,128)S(1)} %slice.52.vel_ref, f32[12,16,128]{2,1,0:T(8,128)S(1)} %get-tuple-element.8.press_ref, f32[12,16,128]{2,1,0:T(8,128)S(1)} %get-tuple-element.7.buoy_ref, ...), custom_call_target="tpu_custom_call" | custom-call | tf_op jit(solution)/shard_map/stokes/pallas_call | solution.py:282
  (18 shorter events, 0.1 us)
Async XLA Ops:
  1.3 0.7 %copy-start.4 = (s32[256]{0:T(256)S(1)}, s32[256]{0:T(256)}, u32[]{:S(2)}) copy-start(s32[256]{0:T(256)} %param.16) | copy-start | bytes 3076
  1.3 0.7 %copy-start.3 = (s32[256,1]{0,1:T(1,128)S(1)}, s32[256,1]{0,1:T(1,128)}, u32[]{:S(2)}) copy-start(s32[256,1]{0,1:T(1,128)} %param.15) | copy-start | bytes 3076
  2.0 0.9 %copy-start = (f32[256,256]{1,0:T(8,128)S(1)}, f32[256,256]{1,0:T(8,128)}, u32[]{:S(2)}) copy-start(f32[256,256]{1,0:T(8,128)} %value_ref.1) | copy-start | bytes 786436
  2.9 0.9 %copy-start.1 = (f32[256,256]{1,0:T(8,128)S(1)}, f32[256,256]{1,0:T(8,128)}, u32[]{:S(2)}) copy-start(f32[256,256]{1,0:T(8,128)} %height_ref.1) | copy-start | bytes 786436
  13.7 7.3 %copy-start.5 = (f32[3,8,8,128]{3,2,1,0:T(8,128)S(1)}, f32[3,8,8,128]{3,2,1,0:T(8,128)}, u32[]{:S(2)}) copy-start(f32[3,8,8,128]{3,2,1,0:T(8,128)} %param.9) | copy-start | bytes 294916
  13.7 7.3 %copy-start.7 = (f32[8,8,128]{2,1,0:T(8,128)S(1)}, f32[8,8,128]{2,1,0:T(8,128)}, u32[]{:S(2)}) copy-start(f32[8,8,128]{2,1,0:T(8,128)} %param.11) | copy-start | bytes 98308
  13.7 7.3 %copy-start.8 = (f32[8,8,128]{2,1,0:T(8,128)S(1)}, f32[8,8,128]{2,1,0:T(8,128)}, u32[]{:S(2)}) copy-start(f32[8,8,128]{2,1,0:T(8,128)} %param.10) | copy-start | bytes 98308
  13.7 23.7 %all-to-all-start = ((f32[32,16,256]{2,1,0:T(8,128)}), f32[32,16,256]{2,1,0:T(8,128)S(1)}, u32[]{:S(2)}, u32[]{:S(2)}) async-start(f32[32,16,256]{2,1,0:T(8,128)} %bitcast.8), calls=%async_computation | async-start | bytes 1048576 | tf_op jit(solution)/shard_map/all_to_all | solution.py:340
  21.0 3.6 %collective-permute-start = (f32[5,2,8,128]{3,2,1,0:T(8,128)S(1)}, f32[5,2,8,128]{3,2,1,0:T(8,128)S(1)}, u32[]{:S(2)}, u32[]{:S(2)}) collective-permute-start(f32[5,2,8,128]{3,2,1,0:T(8,128)S(1)} %get-tuple-element.11), channel_id=1, source_target_pairs={{0,8},{8,16},{16,24},{1,9},{9,17},{17,25},{2,10},{10,18},{18,26},{... | collective-permute-start | bytes 122888 | tf_op jit(solution)/shard_map/ppermute | solution.py:301
  23.2 4.2 %collective-permute-start.1 = (f32[5,2,8,128]{3,2,1,0:T(8,128)S(1)}, f32[5,2,8,128]{3,2,1,0:T(8,128)S(1)}, u32[]{:S(2)}, u32[]{:S(2)}) collective-permute-start(f32[5,2,8,128]{3,2,1,0:T(8,128)S(1)} %get-tuple-element.12), channel_id=1, source_target_pairs={{8,0},{16,8},{24,16},{9,1},{17,9},{25,17},{10,2},{18,10},{26,18},{... | collective-permute-start | bytes 122888 | tf_op jit(solution)/shard_map/ppermute | solution.py:301
  24.7 12.7 %copy-start.2 = (f32[8,8,128]{2,1,0:T(8,128)S(1)}, f32[8,8,128]{2,1,0:T(8,128)}, u32[]{:S(2)}) copy-start(f32[8,8,128]{2,1,0:T(8,128)} %param.12) | copy-start | bytes 98308
  27.5 14.4 %collective-permute-start.2 = (f32[5,12,2,128]{3,2,1,0:T(2,128)S(1)}, f32[5,12,2,128]{3,2,1,0:T(2,128)S(1)}, u32[]{:S(2)}, u32[]{:S(2)}) collective-permute-start(f32[5,12,2,128]{3,2,1,0:T(2,128)S(1)} %get-tuple-element.9), channel_id=1, source_target_pairs={{0,1},{1,2},{2,3},{3,4},{4,5},{5,6},{6,7},{8,9},{9,10},{10,11},{11... | collective-permute-start | bytes 184328 | tf_op jit(solution)/shard_map/ppermute | solution.py:301
  30.9 11.1 %collective-permute-start.3 = (f32[5,12,2,128]{3,2,1,0:T(2,128)S(1)}, f32[5,12,2,128]{3,2,1,0:T(2,128)S(1)}, u32[]{:S(2)}, u32[]{:S(2)}) collective-permute-start(f32[5,12,2,128]{3,2,1,0:T(2,128)S(1)} %get-tuple-element.10), channel_id=1, source_target_pairs={{1,0},{2,1},{3,2},{4,3},{5,4},{6,5},{7,6},{9,8},{10,9},{11,10},{12... | collective-permute-start | bytes 184328 | tf_op jit(solution)/shard_map/ppermute | solution.py:301
  39.3 2.8 %collective-permute-start.4 = (f32[2,8,128]{2,1,0:T(8,128)S(1)}, f32[2,8,128]{2,1,0:T(8,128)S(1)}, u32[]{:S(2)}, u32[]{:S(2)}) collective-permute-start(f32[2,8,128]{2,1,0:T(8,128)S(1)} %get-tuple-element.15), channel_id=1, source_target_pairs={{0,8},{8,16},{16,24},{1,9},{9,17},{17,25},{2,10},{10,18},{18,26},{... | collective-permute-start | bytes 24584 | tf_op jit(solution)/shard_map/ppermute | solution.py:301
  40.6 3.8 %copy-start.6 = (f32[64,128]{1,0:T(8,128)S(1)}, f32[64,128]{1,0:T(8,128)}, u32[]{:S(2)}) copy-start(f32[64,128]{1,0:T(8,128)} %gather.1) | copy-start | bytes 98308
  40.6 3.7 %collective-permute-start.5 = (f32[2,8,128]{2,1,0:T(8,128)S(1)}, f32[2,8,128]{2,1,0:T(8,128)S(1)}, u32[]{:S(2)}, u32[]{:S(2)}) collective-permute-start(f32[2,8,128]{2,1,0:T(8,128)S(1)} %get-tuple-element.16), channel_id=1, source_target_pairs={{8,0},{16,8},{24,16},{9,1},{17,9},{25,17},{10,2},{18,10},{26,18},{... | collective-permute-start | bytes 24584 | tf_op jit(solution)/shard_map/ppermute | solution.py:301
  44.4 4.2 %collective-permute-start.6 = (f32[12,2,128]{2,1,0:T(2,128)S(1)}, f32[12,2,128]{2,1,0:T(2,128)S(1)}, u32[]{:S(2)}, u32[]{:S(2)}) collective-permute-start(f32[12,2,128]{2,1,0:T(2,128)S(1)} %get-tuple-element.13), channel_id=1, source_target_pairs={{0,1},{1,2},{2,3},{3,4},{4,5},{5,6},{6,7},{8,9},{9,10},{10,11},{11... | collective-permute-start | bytes 36872 | tf_op jit(solution)/shard_map/ppermute | solution.py:301
  47.2 5.6 %collective-permute-start.7 = (f32[12,2,128]{2,1,0:T(2,128)S(1)}, f32[12,2,128]{2,1,0:T(2,128)S(1)}, u32[]{:S(2)}, u32[]{:S(2)}) collective-permute-start(f32[12,2,128]{2,1,0:T(2,128)S(1)} %get-tuple-element.14), channel_id=1, source_target_pairs={{1,0},{2,1},{3,2},{4,3},{5,4},{6,5},{7,6},{9,8},{10,9},{11,10},{12... | collective-permute-start | bytes 36872 | tf_op jit(solution)/shard_map/ppermute | solution.py:301

commit v2 on v1

--- a/solution.py
+++ b/solution.py
@@ -9,6 +9,7 @@
 
 ITERS = 2
 HALO = 2
+CHUNKS = 8
 
 PRESS_STEP = 0.5
 VEL_STEP = 0.05
@@ -17,6 +18,7 @@
 F32 = jnp.float32
 BF16 = jnp.bfloat16
 VMEM = pl.BlockSpec(memory_space=pltpu.VMEM)
+HBM = pl.BlockSpec(memory_space=pltpu.HBM)
 SMEM = pl.BlockSpec(memory_space=pltpu.SMEM)
 NT = (((1,), (1,)), ((), ()))
 TN = (((0,), (0,)), ((), ()))
@@ -31,10 +33,69 @@
 
 
 def deposit_kernel(
-    num_owners, capacity, count_ref, owner_ref, column_ref, value_ref, height_ref, out_ref, part_ref
+    num_owners,
+    capacity,
+    count_ref,
+    owner_hbm,
+    column_hbm,
+    value_hbm,
+    height_hbm,
+    out_ref,
+    value_ref,
+    height_ref,
+    owner_ref,
+    column_ref,
+    place_ref,
+    code_ref,
+    part_ref,
+    index_sem,
+    block_sem,
 ):
     blocks, marks = value_ref.shape
     num_levels = out_ref.shape[1] // 2
+    slots = num_owners * capacity
+    chunk = blocks // CHUNKS
+
+    def chunk_copies(k):
+        rows = pl.ds(pl.multiple_of(k * chunk, chunk), chunk)
+        return (
+            pltpu.make_async_copy(height_hbm.at[rows], height_ref.at[rows], block_sem.at[0, k]),
+            pltpu.make_async_copy(value_hbm.at[rows], value_ref.at[rows], block_sem.at[1, k]),
+        )
+
+    index_copies = (
+        pltpu.make_async_copy(owner_hbm, owner_ref, index_sem.at[0]),
+        pltpu.make_async_copy(column_hbm, column_ref, index_sem.at[1]),
+    )
+    for copy in index_copies:
+        copy.start()
+    for k in range(CHUNKS):
+        for copy in chunk_copies(k):
+            copy.start()
+    for copy in index_copies:
+        copy.wait()
+
+    owner = owner_ref[...]
+    block_id = lax.broadcasted_iota(jnp.int32, (1, blocks), 1)
+    owner = jnp.where(block_id < count_ref[0], owner, num_owners)
+    owned = lax.broadcasted_iota(jnp.int32, (num_owners, blocks), 0) == owner
+    hits = jnp.where(owned, 1.0, 0.0)
+    earlier = jnp.where(
+        lax.broadcasted_iota(jnp.int32, (blocks, blocks), 0)
+        < lax.broadcasted_iota(jnp.int32, (blocks, blocks), 1),
+        1.0,
+        0.0,
+    ).astype(BF16)
+    before = jnp.dot(hits.astype(BF16), earlier, preferred_element_type=F32)
+    rank = jnp.sum(hits * before, axis=0, keepdims=True)
+    slot = owner * capacity + rank.astype(jnp.int32)
+    place = jnp.where(
+        lax.broadcasted_iota(jnp.int32, (slots, blocks), 0) == slot, 1.0, 0.0
+    ).astype(BF16)
+    place_ref[...] = place
+    code = jnp.broadcast_to((column_ref[...] + 1).astype(F32), (num_levels, blocks)).astype(BF16)
+    code_ref[...] = lax.dot_general(place, code, NT, preferred_element_type=F32)
+
     row8 = lax.broadcasted_iota(jnp.int32, (8, marks), 0)
     upper_part = (row8 & 1) == 1
     with_value = (row8 & 2) == 0
@@ -57,12 +118,14 @@
         sums = lax.dot_general(pieces, hot, NT, preferred_element_type=F32)
         part_ref[pl.ds(pl.multiple_of(b * 8, 8), 8), :] = sums[:8]
 
-    def some_blocks(step, carry):
-        for k in range(8):
-            one_block(step * 8 + k)
+    def one_chunk(k, carry):
+        for copy in chunk_copies(k):
+            copy.wait()
+        for i in range(chunk):
+            one_block(k * chunk + i)
         return carry
 
-    lax.fori_loop(0, blocks // 8, some_blocks, 0)
+    lax.fori_loop(0, CHUNKS, one_chunk, 0)
 
     def part(kind):
         high = part_ref[pl.ds(kind, blocks, stride=8), :]
@@ -70,27 +133,7 @@
 
     value_sum = part(0) + pltpu.roll(part(1), 1, 1)
     weight_sum = part(2) + pltpu.roll(part(3), 1, 1)
-
-    owner = owner_ref[...]
-    block_id = lax.broadcasted_iota(jnp.int32, (1, blocks), 1)
-    owner = jnp.where(block_id < count_ref[0], owner, num_owners)
-    owned = lax.broadcasted_iota(jnp.int32, (num_owners, blocks), 0) == owner
-    hits = jnp.where(owned, 1.0, 0.0)
-    earlier = jnp.where(
-        lax.broadcasted_iota(jnp.int32, (blocks, blocks), 0)
-        < lax.broadcasted_iota(jnp.int32, (blocks, blocks), 1),
-        1.0,
-        0.0,
-    ).astype(BF16)
-    before = jnp.dot(hits.astype(BF16), earlier, preferred_element_type=F32)
-    rank = jnp.sum(hits * before, axis=0, keepdims=True)
-    slot = owner * capacity + rank.astype(jnp.int32)
-    slots = num_owners * capacity
-    place = jnp.where(
-        lax.broadcasted_iota(jnp.int32, (slots, blocks), 0) == slot, 1.0, 0.0
-    ).astype(BF16)
-    code = jnp.broadcast_to((column_ref[...] + 1).astype(F32), (num_levels, blocks)).astype(BF16)
-    codes = lax.dot_general(place, code, NT, preferred_element_type=F32)
+    place = place_ref[...]
 
     def placed(x):
         high, mid, low = (jnp.dot(place, y, preferred_element_type=F32) for y in split3(x))
@@ -98,25 +141,39 @@
 
     out_ref[:, :num_levels] = placed(value_sum)
     lane = lax.broadcasted_iota(jnp.int32, (slots, num_levels), 1)
-    out_ref[:, num_levels:] = jnp.where(lane == num_levels - 1, codes, placed(weight_sum))
+    out_ref[:, num_levels:] = jnp.where(
+        lane == num_levels - 1, code_ref[...], placed(weight_sum)
+    )
 
 
 def deposit(count, owner, column, value, height, num_owners, capacity, num_levels):
     blocks, marks = value.shape
+    slots = num_owners * capacity
     return pl.pallas_call(
         functools.partial(deposit_kernel, num_owners, capacity),
-        out_shape=jax.ShapeDtypeStruct((num_owners * capacity, 2 * num_levels), F32),
-        in_specs=[SMEM, VMEM, VMEM, VMEM, VMEM],
+        out_shape=jax.ShapeDtypeStruct((slots, 2 * num_levels), F32),
+        in_specs=[SMEM, HBM, HBM, HBM, HBM],
         out_specs=VMEM,
-        scratch_shapes=[pltpu.VMEM((blocks * 8, num_levels), F32)],
+        scratch_shapes=[
+            pltpu.VMEM((blocks, marks), F32),
+            pltpu.VMEM((blocks, marks), F32),
+            pltpu.VMEM((1, blocks), jnp.int32),
+            pltpu.VMEM((1, blocks), jnp.int32),
+            pltpu.VMEM((slots, blocks), BF16),
+            pltpu.VMEM((slots, num_levels), F32),
+            pltpu.VMEM((blocks * 8, num_levels), F32),
+            pltpu.SemaphoreType.DMA((2,)),
+            pltpu.SemaphoreType.DMA((2, CHUNKS)),
+        ],
         compiler_params=pltpu.CompilerParams(vmem_limit_bytes=48 << 20),
         name="deposit",
     )(count, owner.reshape(1, blocks), column.reshape(1, blocks), value, height)
 
 
-def gather_kernel(marks, arrived_ref, background_ref, out_ref):
+def gather_kernel(marks, odd_ref, arrived_ref, background_ref, out_ref, near_ref, far_ref):
     slots = arrived_ref.shape[0]
-    columns, num_levels = out_ref.shape
+    cells_x, cells_y, num_levels = out_ref.shape
+    columns = cells_x * cells_y
     values = arrived_ref[:, :num_levels]
     weights = arrived_ref[:, num_levels:]
     lane = lax.broadcasted_iota(jnp.int32, (slots, num_levels), 1)
@@ -132,20 +189,30 @@
         )
         return high + (mid + low)
 
-    out_ref[...] = jnp.exp((placed(values) + background_ref[...]) / (placed(weights) + 1.0))
-
-
-def gather(arrived, background, marks):
-    cells_x, cells_y, num_levels = background.shape
-    out = pl.pallas_call(
+    background = background_ref[...].reshape(columns, num_levels)
+    visc = jnp.exp((placed(values) + background) / (placed(weights) + 1.0))
+    visc = visc.reshape(cells_x, cells_y, num_levels)
+    out_ref[...] = visc
+    odd = odd_ref[0] == 1
+    first, final = visc[:HALO], visc[cells_x - HALO :]
+    near_ref[...] = jnp.where(odd, first, final)
+    far_ref[...] = jnp.where(odd, final, first)
+
+
+def gather(odd, arrived, background, marks):
+    strip = (HALO,) + background.shape[1:]
+    return pl.pallas_call(
         functools.partial(gather_kernel, marks),
-        out_shape=jax.ShapeDtypeStruct((cells_x * cells_y, num_levels), F32),
-        in_specs=[VMEM, VMEM],
-        out_specs=VMEM,
+        out_shape=(
+            jax.ShapeDtypeStruct(background.shape, F32),
+            jax.ShapeDtypeStruct(strip, F32),
+            jax.ShapeDtypeStruct(strip, F32),
+        ),
+        in_specs=[SMEM, VMEM, VMEM],
+        out_specs=(VMEM, VMEM, VMEM),
         compiler_params=pltpu.CompilerParams(vmem_limit_bytes=48 << 20),
         name="gather",
-    )(arrived, background.reshape(cells_x * cells_y, num_levels))
-    return out.reshape(cells_x, cells_y, num_levels)
+    )(odd, arrived, background)
 
 
 def stokes_kernel(
@@ -189,9 +256,14 @@
         at_x = first_x - HALO + x
         return (at_x >= 0) & (at_x < size_x - 1)
 
-    visc = [visc_ref[x] for x in range(wide_x)]
-    vel = [[vel_ref[c, x] for x in range(wide_x)] for c in range(3)]
-    press = [press_ref[x] for x in range(wide_x)]
+    inside = [in_y & in_x(x) for x in range(wide_x)]
+
+    def known(ref, x, *lead):
+        return jnp.where(inside[x], ref[(*lead, x)], 0.0)
+
+    visc = [known(visc_ref, x) for x in range(wide_x)]
+    vel = [[known(vel_ref, x, c) for x in range(wide_x)] for c in range(3)]
+    press = [known(press_ref, x) for x in range(wide_x)]
     side_x = [visc[x] + visc[x + 1] for x in range(wide_x - 1)]
     side_y = [visc[x] + north(visc[x]) for x in range(wide_x)]
     side_z = [visc[x] + upper(visc[x]) for x in range(wide_x)]
@@ -223,9 +295,8 @@
                     in_y, corner_yz[x] * (upper(v) - v + north(w) - w), 0.0
                 )
             if x < end - 1:
-                inside = in_y & in_x(x)
                 tau_xy[x] = jnp.where(
-                    inside, corner_xy[x] * (north(u) - u + vel[1][x + 1] - v), 0.0
+                    inside[x], corner_xy[x] * (north(u) - u + vel[1][x + 1] - v), 0.0
                 )
                 tau_xz[x] = jnp.where(
                     in_x(x), corner_xz[x] * (upper(u) - u + vel[2][x + 1] - w), 0.0
@@ -292,22 +363,41 @@
     )(limits, vel, press, buoy, visc)
 
 
-def shifted(x, axis, dim, width):
-    devices, length = lax.axis_size(axis), x.shape[dim]
-    up = [(i, i + 1) for i in range(devices - 1)]
-    down = [(j, i) for i, j in up]
-    last = lax.slice_in_dim(x, length - width, length, axis=dim)
-    first = lax.slice_in_dim(x, 0, width, axis=dim)
-    return lax.ppermute(last, axis, up), lax.ppermute(first, axis, down)
-
-
-def widened(x):
-    before, after = shifted(x, "gx", x.ndim - 3, HALO)
-    x = jnp.concatenate([before, x, after], axis=x.ndim - 3)
-    before, after = shifted(x, "gy", x.ndim - 2, HALO)
-    rows = x.shape[-2] + 2 * HALO
-    pad = jnp.zeros(x.shape[:-2] + (-rows % 8, x.shape[-1]), x.dtype)
-    return jnp.concatenate([before, x, after, pad], axis=x.ndim - 2)
+def partners(size_x, size_y):
+    def flat(x, y):
+        return (x % size_x) * size_y + y
+
+    cells = [(x, y) for x in range(size_x) for y in range(size_y)]
+    x_near = [(flat(x, y), flat(x ^ 1, y)) for x, y in cells]
+    x_far = [(flat(x, y), flat(x + 1 if x % 2 else x - 1, y)) for x, y in cells]
+    y_near = [(flat(x, y), flat(x, y ^ 1)) for x, y in cells]
+    y_far = [
+        (flat(x, y), flat(x ^ 1, y) if y in (0, size_y - 1) else flat(x, y + 1 if y % 2 else y - 1))
+        for x, y in cells
+    ]
+    return x_near, x_far, y_near, y_far
+
+
+def swapped(near, far, near_pairs, far_pairs, odd, dim, x):
+    near = lax.ppermute(near, ("gx", "gy"), near_pairs)
+    far = lax.ppermute(far, ("gx", "gy"), far_pairs)
+    before, after = jnp.where(odd, near, far), jnp.where(odd, far, near)
+    return jnp.concatenate([before, x, after], axis=dim)
+
+
+def strips(x, odd, dim):
+    length = x.shape[dim]
+    first = lax.slice_in_dim(x, 0, HALO, axis=dim)
+    final = lax.slice_in_dim(x, length - HALO, length, axis=dim)
+    return jnp.where(odd, first, final), jnp.where(odd, final, first)
+
+
+def widened(x, near, far, pairs, odd_x, odd_y):
+    dim = x.ndim - 3
+    x = swapped(near, far, pairs[0], pairs[1], odd_x, dim, x)
+    x = swapped(*strips(x, odd_y, dim + 1), pairs[2], pairs[3], odd_y, dim + 1, x)
+    pad = jnp.zeros(x.shape[:-2] + (-x.shape[-2] % 8, x.shape[-1]), x.dtype)
+    return jnp.concatenate([x, pad], axis=dim + 1)
 
 
 def shards(
@@ -344,9 +434,13 @@
         concat_axis=0,
         tiled=True,
     ).reshape(devices * capacity, 2 * num_levels)
-    fields = widened(jnp.concatenate([velocity, pressure[None], buoyancy[None]], axis=0))
-    viscosity = gather(arrived, background, marks)
-    visc = widened(viscosity)
+    pairs = partners(size_x, size_y)
+    odd_x = lax.axis_index("gx") % 2
+    odd_y = lax.axis_index("gy") % 2
+    fields = jnp.concatenate([velocity, pressure[None], buoyancy[None]], axis=0)
+    fields = widened(fields, *strips(fields, odd_x == 1, 1), pairs, odd_x == 1, odd_y == 1)
+    viscosity, near, far = gather(odd_x.astype(jnp.int32)[None], arrived, background, marks)
+    visc = widened(viscosity, near, far, pairs, odd_x == 1, odd_y == 1)
     limits = jnp.stack(
         [
             lax.axis_index("gx") * cells_x,

time: 55.7 us -> 46.5 us (0.83); the launches traced: 54.7 us -> 46.1 us
  starting transfers between devices: 22.1 us -> 14.5 us
  Pallas kernels: 12.8 us -> 11.1 us
  waiting for transfers between devices: 14.5 us -> 15.2 us
    ppermute x8, starting transfers between devices: 14.8 us -> 7.22 us  [the longest x4 4.18 us: swapped(): near = lax.ppermute(near, ('gx', 'gy'), near_pairs)]
    pallas_call x1, Pallas kernels: 9.82 us -> 8.07 us  [deposit(): pl.pallas_call(functools.partial(deposit_kernel, num_owners, capacity), o...]
    ppermute x8, waiting for transfers between devices: 9.31 us -> 10.4 us  [the longest x4 5.46 us: swapped(): far = lax.ppermute(far, ('gx', 'gy'), far_pairs)]
    unnamed x18, local copies, waits for them, and re-layouts: 2.6 us -> 3.32 us
    slice x1 -> x0, local copies, waits for them, and re-layouts: 0.72 us -> none  [shifted(): last = lax.slice_in_dim(x, length - width, length, axis=dim)]
  transfers between devices with their start and end apart: 9 -> 9, of which waited for: 4 -> 6; matrix products, arithmetic and copies ran while one was open for 2% -> 1% of each run, Pallas kernels for 2% -> 0%
where the time goes in v2:
time: 46.5 us; the launch traced here: 46.1 us
  waiting for transfers between devices  15.2 us (33%)
  starting transfers between devices  14.5 us (31%)
  Pallas kernels  11.1 us (24%)
  local copies, waits for them, and re-layouts  3.43 us (7%)
  between operations  1.46 us (3%)
    pallas_call x1, Pallas kernels, deposit(): pl.pallas_call(functools.partial(deposit_kernel, num_owners, capacity), o...  8.07 us
    all_to_all x1, starting transfers between devices, shards(): lax.all_to_all(send.reshape(devices, capacity, 2 * num_levels), ('gx', 'g...  7.3 us
    ppermute x4, waiting for transfers between devices, swapped(): far = lax.ppermute(far, ('gx', 'gy'), far_pairs)  5.46 us
    ppermute x4, waiting for transfers between devices, swapped(): near = lax.ppermute(near, ('gx', 'gy'), near_pairs)  4.91 us
    all_to_all x1, waiting for transfers between devices, shards(): lax.all_to_all(send.reshape(devices, capacity, 2 * num_levels), ('gx', 'g...  4.85 us
    ppermute x4, starting transfers between devices, swapped(): near = lax.ppermute(near, ('gx', 'gy'), near_pairs)  4.18 us
    unnamed x18, local copies, waits for them, and re-layouts  3.32 us
    ppermute x4, starting transfers between devices, swapped(): far = lax.ppermute(far, ('gx', 'gy'), far_pairs)  3.04 us
  transfers between devices with their start and end apart: 9, of which 6 were waited for; matrix products, arithmetic and copies ran while one was open for 1% of the time, Pallas kernels for 0%

profile of v2, /device:TPU:0, one launch (start us, length us, event | category | flops | bytes accessed | tf_op | source)
XLA Modules:
  0.0 46.1 jit_solution(8074028705160498241)
XLA Ops:
  1.3 0.7 %copy-done.4 = s32[256]{0:T(256)S(1)} copy-done((s32[256]{0:T(256)S(1)}, s32[256]{0:T(256)}, u32[]{:S(2)}) %copy-start.4) | copy-done | bytes 1048
  2.0 0.0 copy-done.3
  2.0 0.9 %copy-done = f32[256,256]{1,0:T(8,128)S(1)} copy-done((f32[256,256]{1,0:T(8,128)S(1)}, f32[256,256]{1,0:T(8,128)}, u32[]{:S(2)}) %copy-start) | copy-done | bytes 262168
  2.9 0.9 %copy-done.1 = f32[256,256]{1,0:T(8,128)S(1)} copy-done((f32[256,256]{1,0:T(8,128)S(1)}, f32[256,256]{1,0:T(8,128)}, u32[]{:S(2)}) %copy-start.1) | copy-done | bytes 262168
  3.9 8.1 %deposit.1 = f32[512,256]{1,0:T(8,128)} custom-call(s32[1]{0:T(128)S(6)} %copy.12.count_ref, s32[1,256]{1,0:T(1,128)S(1)} %bitcast.28, s32[1,256]{1,0:T(1,128)S(1)} %bitcast.29, f32[256,256]{1,0:T(8,128)S(1)} %copy-done, f32[256,256]{1,0:T(8,128)S(1)} %copy-done.1), custom_call_target="tpu_custom_call" | custom-call | tf_op jit(solution)/shard_map/deposit/pallas_call | solution.py:152
  12.0 0.0 copy-start.5
  12.0 0.0 copy-start.7
  12.0 7.3 %all-to-all-start = ((f32[32,16,256]{2,1,0:T(8,128)}), f32[32,16,256]{2,1,0:T(8,128)S(1)}, u32[]{:S(2)}, u32[]{:S(2)}) async-start(f32[32,16,256]{2,1,0:T(8,128)} %bitcast.9), calls=%async_computation | async-start | bytes 1048576 | tf_op jit(solution)/shard_map/all_to_all | solution.py:430
  19.3 0.0 copy-start.6
  19.3 0.7 %copy-done.6 = f32[8,8,128]{2,1,0:T(8,128)S(1)} copy-done((f32[8,8,128]{2,1,0:T(8,128)S(1)}, f32[8,8,128]{2,1,0:T(8,128)}, u32[]{:S(2)}) %copy-start.6) | copy-done | bytes 32792
  20.1 1.6 %collective-permute-start.1 = (f32[5,2,8,128]{3,2,1,0:T(8,128)S(1)}, f32[5,2,8,128]{3,2,1,0:T(8,128)S(1)}, u32[]{:S(2)}, u32[]{:S(2)}) collective-permute-start(f32[5,2,8,128]{3,2,1,0:T(8,128)S(1)} %broadcast_select_fusion.6), channel_id=1, source_target_pairs={{0,24},{1,25},{2,26},{3,27},{4,28},{5,29},{6,30},{7,31},{8,16},{9,... | collective-permute-start | bytes 122888 | tf_op jit(solution)/shard_map/ppermute | solution.py:383
  21.7 0.4 collective-permute-start
  22.0 0.1 pad.16.clone
  22.1 3.6 %collective-permute-done.1 = f32[5,2,8,128]{3,2,1,0:T(8,128)S(1)} collective-permute-done((f32[5,2,8,128]{3,2,1,0:T(8,128)S(1)}, f32[5,2,8,128]{3,2,1,0:T(8,128)S(1)}, u32[]{:S(2)}, u32[]{:S(2)}) %collective-permute-start.1) | collective-permute-done | bytes 40992 | tf_op jit(solution)/shard_map/ppermute | solution.py:383
  25.7 0.1 broadcast_select_fusion.3
  25.8 0.2 collective-permute-start.3
  26.0 2.1 %collective-permute-start.2 = (f32[5,12,2,128]{3,2,1,0:T(2,128)S(1)}, f32[5,12,2,128]{3,2,1,0:T(2,128)S(1)}, u32[]{:S(2)}, u32[]{:S(2)}) collective-permute-start(f32[5,12,2,128]{3,2,1,0:T(2,128)S(1)} %get-tuple-element.16), channel_id=1, source_target_pairs={{0,1},{1,0},{2,3},{3,2},{4,5},{5,4},{6,7},{7,6},{8,9},{9,8},{10,11... | collective-permute-start | bytes 184328 | tf_op jit(solution)/shard_map/ppermute | solution.py:382
  28.1 0.1 pad_add_fusion.limits_ref
  28.1 0.0 collective-permute-done.3
  28.1 2.6 %collective-permute-done.2 = f32[5,12,2,128]{3,2,1,0:T(2,128)S(1)} collective-permute-done((f32[5,12,2,128]{3,2,1,0:T(2,128)S(1)}, f32[5,12,2,128]{3,2,1,0:T(2,128)S(1)}, u32[]{:S(2)}, u32[]{:S(2)}) %collective-permute-start.2) | collective-permute-done | bytes 61472 | tf_op jit(solution)/shard_map/ppermute | solution.py:382
  30.8 4.8 %all-to-all-done = f32[32,16,256]{2,1,0:T(8,128)S(1)} async-done(((f32[32,16,256]{2,1,0:T(8,128)}), f32[32,16,256]{2,1,0:T(8,128)S(1)}, u32[]{:S(2)}, u32[]{:S(2)}) %all-to-all-start) | async-done | bytes 524320 | tf_op jit(solution)/shard_map/all_to_all | solution.py:430
  35.6 1.2 %gather.1 = (f32[8,8,128]{2,1,0:T(8,128)}, f32[2,8,128]{2,1,0:T(8,128)S(1)}, f32[2,8,128]{2,1,0:T(8,128)S(1)}) custom-call(s32[1]{0:T(128)} %bitcast.6.odd_ref, f32[512,256]{1,0:T(8,128)S(1)} %bitcast.27, f32[8,8,128]{2,1,0:T(8,128)S(1)} %copy-done.2), custom_call_target="tpu_custom_call" | custom-call | tf_op jit(solution)/shard_map/gather/pallas_call | solution.py:204
  36.8 0.7 %collective-permute-start.5 = (f32[2,8,128]{2,1,0:T(8,128)S(1)}, f32[2,8,128]{2,1,0:T(8,128)S(1)}, u32[]{:S(2)}, u32[]{:S(2)}) collective-permute-start(f32[2,8,128]{2,1,0:T(8,128)S(1)} %get-tuple-element.9), channel_id=1, source_target_pairs={{0,24},{1,25},{2,26},{3,27},{4,28},{5,29},{6,30},{7,31},{8,16},{9,... | collective-permute-start | bytes 24584 | tf_op jit(solution)/shard_map/ppermute | solution.py:383
  37.5 0.1 maximum_maximum_fusion
  37.6 0.0 copy-start.8
  37.6 0.4 collective-permute-done.4
  38.0 1.9 %collective-permute-done.5 = f32[2,8,128]{2,1,0:T(8,128)S(1)} collective-permute-done((f32[2,8,128]{2,1,0:T(8,128)S(1)}, f32[2,8,128]{2,1,0:T(8,128)S(1)}, u32[]{:S(2)}, u32[]{:S(2)}) %collective-permute-start.5) | collective-permute-done | bytes 8224 | tf_op jit(solution)/shard_map/ppermute | solution.py:383
  39.9 0.6 %collective-permute-start.7 = (f32[12,2,128]{2,1,0:T(2,128)S(1)}, f32[12,2,128]{2,1,0:T(2,128)S(1)}, u32[]{:S(2)}, u32[]{:S(2)}) collective-permute-start(f32[12,2,128]{2,1,0:T(2,128)S(1)} %bitcast.49), channel_id=1, source_target_pairs={{0,8},{1,2},{2,1},{3,4},{4,3},{5,6},{6,5},{7,15},{8,0},{9,10},{10,... | collective-permute-start | bytes 36872 | tf_op jit(solution)/shard_map/ppermute | solution.py:383
  40.5 1.7 %collective-permute-start.6 = (f32[12,2,128]{2,1,0:T(2,128)S(1)}, f32[12,2,128]{2,1,0:T(2,128)S(1)}, u32[]{:S(2)}, u32[]{:S(2)}) collective-permute-start(f32[12,2,128]{2,1,0:T(2,128)S(1)} %get-tuple-element.13), channel_id=1, source_target_pairs={{0,1},{1,0},{2,3},{3,2},{4,5},{5,4},{6,7},{7,6},{8,9},{9,8},{10,11... | collective-permute-start | bytes 36872 | tf_op jit(solution)/shard_map/ppermute | solution.py:382
  42.3 1.9 %collective-permute-done.6 = f32[12,2,128]{2,1,0:T(2,128)S(1)} collective-permute-done((f32[12,2,128]{2,1,0:T(2,128)S(1)}, f32[12,2,128]{2,1,0:T(2,128)S(1)}, u32[]{:S(2)}, u32[]{:S(2)}) %collective-permute-start.6) | collective-permute-done | bytes 12320 | tf_op jit(solution)/shard_map/ppermute | solution.py:382
  44.2 0.1 maximum_maximum_fusion.1.visc_ref
  44.3 1.8 %stokes.1 = (f32[3,8,8,128]{3,2,1,0:T(8,128)}, f32[8,8,128]{2,1,0:T(8,128)}) custom-call(s32[4]{0:T(128)S(1)} %pad_add_fusion.limits_ref, f32[3,12,16,128]{3,2,1,0:T(8,128)S(1)} %slice.36.vel_ref, f32[12,16,128]{2,1,0:T(8,128)S(1)} %get-tuple-element.23.press_ref, f32[12,16,128]{2,1,0:T(8,128)S(1)} %get-tuple-element.22.buoy_ref, ...), custom_call_target="tpu_custom_call" | custom-call | tf_op jit(solution)/shard_map/stokes/pallas_call | solution.py:353
  (24 shorter events, 0.1 us)
Async XLA Ops:
  1.3 0.7 %copy-start.4 = (s32[256]{0:T(256)S(1)}, s32[256]{0:T(256)}, u32[]{:S(2)}) copy-start(s32[256]{0:T(256)} %param.16) | copy-start | bytes 3076
  1.3 0.7 %copy-start.3 = (s32[256,1]{0,1:T(1,128)S(1)}, s32[256,1]{0,1:T(1,128)}, u32[]{:S(2)}) copy-start(s32[256,1]{0,1:T(1,128)} %param.15) | copy-start | bytes 3076
  2.0 0.9 %copy-start = (f32[256,256]{1,0:T(8,128)S(1)}, f32[256,256]{1,0:T(8,128)}, u32[]{:S(2)}) copy-start(f32[256,256]{1,0:T(8,128)} %value_hbm.1) | copy-start | bytes 786436
  2.9 0.9 %copy-start.1 = (f32[256,256]{1,0:T(8,128)S(1)}, f32[256,256]{1,0:T(8,128)}, u32[]{:S(2)}) copy-start(f32[256,256]{1,0:T(8,128)} %height_hbm.1) | copy-start | bytes 786436
  12.0 7.4 %copy-start.5 = (f32[3,8,8,128]{3,2,1,0:T(8,128)S(1)}, f32[3,8,8,128]{3,2,1,0:T(8,128)}, u32[]{:S(2)}) copy-start(f32[3,8,8,128]{3,2,1,0:T(8,128)} %param.9) | copy-start | bytes 294916
  12.0 7.4 %copy-start.7 = (f32[8,8,128]{2,1,0:T(8,128)S(1)}, f32[8,8,128]{2,1,0:T(8,128)}, u32[]{:S(2)}) copy-start(f32[8,8,128]{2,1,0:T(8,128)} %param.10) | copy-start | bytes 98308
  12.0 23.7 %all-to-all-start = ((f32[32,16,256]{2,1,0:T(8,128)}), f32[32,16,256]{2,1,0:T(8,128)S(1)}, u32[]{:S(2)}, u32[]{:S(2)}) async-start(f32[32,16,256]{2,1,0:T(8,128)} %bitcast.9), calls=%async_computation | async-start | bytes 1048576 | tf_op jit(solution)/shard_map/all_to_all | solution.py:430
  19.3 0.8 %copy-start.6 = (f32[8,8,128]{2,1,0:T(8,128)S(1)}, f32[8,8,128]{2,1,0:T(8,128)}, u32[]{:S(2)}) copy-start(f32[8,8,128]{2,1,0:T(8,128)} %param.11) | copy-start | bytes 98308
  20.1 5.6 %collective-permute-start.1 = (f32[5,2,8,128]{3,2,1,0:T(8,128)S(1)}, f32[5,2,8,128]{3,2,1,0:T(8,128)S(1)}, u32[]{:S(2)}, u32[]{:S(2)}) collective-permute-start(f32[5,2,8,128]{3,2,1,0:T(8,128)S(1)} %broadcast_select_fusion.6), channel_id=1, source_target_pairs={{0,24},{1,25},{2,26},{3,27},{4,28},{5,29},{6,30},{7,31},{8,16},{9,... | collective-permute-start | bytes 122888 | tf_op jit(solution)/shard_map/ppermute | solution.py:383
  21.7 4.0 %collective-permute-start = (f32[5,2,8,128]{3,2,1,0:T(8,128)S(1)}, f32[5,2,8,128]{3,2,1,0:T(8,128)S(1)}, u32[]{:S(2)}, u32[]{:S(2)}) collective-permute-start(f32[5,2,8,128]{3,2,1,0:T(8,128)S(1)} %get-tuple-element.19), channel_id=1, source_target_pairs={{0,8},{1,9},{2,10},{3,11},{4,12},{5,13},{6,14},{7,15},{8,0},{9,1},... | collective-permute-start | bytes 122888 | tf_op jit(solution)/shard_map/ppermute | solution.py:382
  25.8 2.4 %collective-permute-start.3 = (f32[5,12,2,128]{3,2,1,0:T(2,128)S(1)}, f32[5,12,2,128]{3,2,1,0:T(2,128)S(1)}, u32[]{:S(2)}, u32[]{:S(2)}) collective-permute-start(f32[5,12,2,128]{3,2,1,0:T(2,128)S(1)} %bitcast.40), channel_id=1, source_target_pairs={{0,8},{1,2},{2,1},{3,4},{4,3},{5,6},{6,5},{7,15},{8,0},{9,10},{10,... | collective-permute-start | bytes 184328 | tf_op jit(solution)/shard_map/ppermute | solution.py:383
  26.0 4.8 %collective-permute-start.2 = (f32[5,12,2,128]{3,2,1,0:T(2,128)S(1)}, f32[5,12,2,128]{3,2,1,0:T(2,128)S(1)}, u32[]{:S(2)}, u32[]{:S(2)}) collective-permute-start(f32[5,12,2,128]{3,2,1,0:T(2,128)S(1)} %get-tuple-element.16), channel_id=1, source_target_pairs={{0,1},{1,0},{2,3},{3,2},{4,5},{5,4},{6,7},{7,6},{8,9},{9,8},{10,11... | collective-permute-start | bytes 184328 | tf_op jit(solution)/shard_map/ppermute | solution.py:382
  30.8 4.9 %copy-start.2 = (f32[8,8,128]{2,1,0:T(8,128)S(1)}, f32[8,8,128]{2,1,0:T(8,128)}, u32[]{:S(2)}) copy-start(f32[8,8,128]{2,1,0:T(8,128)} %background_ref.1) | copy-start | bytes 98308
  36.8 1.2 %collective-permute-start.4 = (f32[2,8,128]{2,1,0:T(8,128)S(1)}, f32[2,8,128]{2,1,0:T(8,128)S(1)}, u32[]{:S(2)}, u32[]{:S(2)}) collective-permute-start(f32[2,8,128]{2,1,0:T(8,128)S(1)} %get-tuple-element.8), channel_id=1, source_target_pairs={{0,8},{1,9},{2,10},{3,11},{4,12},{5,13},{6,14},{7,15},{8,0},{9,1},... | collective-permute-start | bytes 24584 | tf_op jit(solution)/shard_map/ppermute | solution.py:382
  36.8 3.1 %collective-permute-start.5 = (f32[2,8,128]{2,1,0:T(8,128)S(1)}, f32[2,8,128]{2,1,0:T(8,128)S(1)}, u32[]{:S(2)}, u32[]{:S(2)}) collective-permute-start(f32[2,8,128]{2,1,0:T(8,128)S(1)} %get-tuple-element.9), channel_id=1, source_target_pairs={{0,24},{1,25},{2,26},{3,27},{4,28},{5,29},{6,30},{7,31},{8,16},{9,... | collective-permute-start | bytes 24584 | tf_op jit(solution)/shard_map/ppermute | solution.py:383
  37.6 2.3 %copy-start.8 = (f32[8,8,128]{2,1,0:T(8,128)S(1)}, f32[8,8,128]{2,1,0:T(8,128)}, u32[]{:S(2)}) copy-start(f32[8,8,128]{2,1,0:T(8,128)} %get-tuple-element.7) | copy-start | bytes 98308
  39.9 2.4 %collective-permute-start.7 = (f32[12,2,128]{2,1,0:T(2,128)S(1)}, f32[12,2,128]{2,1,0:T(2,128)S(1)}, u32[]{:S(2)}, u32[]{:S(2)}) collective-permute-start(f32[12,2,128]{2,1,0:T(2,128)S(1)} %bitcast.49), channel_id=1, source_target_pairs={{0,8},{1,2},{2,1},{3,4},{4,3},{5,6},{6,5},{7,15},{8,0},{9,10},{10,... | collective-permute-start | bytes 36872 | tf_op jit(solution)/shard_map/ppermute | solution.py:383
  40.5 3.7 %collective-permute-start.6 = (f32[12,2,128]{2,1,0:T(2,128)S(1)}, f32[12,2,128]{2,1,0:T(2,128)S(1)}, u32[]{:S(2)}, u32[]{:S(2)}) collective-permute-start(f32[12,2,128]{2,1,0:T(2,128)S(1)} %get-tuple-element.13), channel_id=1, source_target_pairs={{0,1},{1,0},{2,3},{3,2},{4,5},{5,4},{6,7},{7,6},{8,9},{9,8},{10,11... | collective-permute-start | bytes 36872 | tf_op jit(solution)/shard_map/ppermute | solution.py:382

commit v3 on v2

--- a/solution.py
+++ b/solution.py
@@ -9,7 +9,9 @@
 
 ITERS = 2
 HALO = 2
-CHUNKS = 8
+CHUNKS = 4
+WAYS = 4
+OUT_PARTS = 2
 
 PRESS_STEP = 0.5
 VEL_STEP = 0.05
@@ -21,7 +23,6 @@
 HBM = pl.BlockSpec(memory_space=pltpu.HBM)
 SMEM = pl.BlockSpec(memory_space=pltpu.SMEM)
 NT = (((1,), (1,)), ((), ()))
-TN = (((0,), (0,)), ((), ()))
 
 
 def split3(x):
@@ -40,16 +41,20 @@
     column_hbm,
     value_hbm,
     height_hbm,
-    out_ref,
+    out_hbm,
     value_ref,
     height_ref,
     owner_ref,
     column_ref,
     place_ref,
     code_ref,
+    lower_ref,
+    fraction_ref,
     part_ref,
+    out_ref,
     index_sem,
     block_sem,
+    out_sem,
 ):
     blocks, marks = value_ref.shape
     num_levels = out_ref.shape[1] // 2
@@ -96,33 +101,54 @@
     code = jnp.broadcast_to((column_ref[...] + 1).astype(F32), (num_levels, blocks)).astype(BF16)
     code_ref[...] = lax.dot_general(place, code, NT, preferred_element_type=F32)
 
+    span = num_levels // WAYS
     row8 = lax.broadcasted_iota(jnp.int32, (8, marks), 0)
     upper_part = (row8 & 1) == 1
     with_value = (row8 & 2) == 0
     leading = row8 < 4
-    level = lax.broadcasted_iota(jnp.int32, (num_levels, marks), 0).astype(F32).astype(BF16)
-
-    def one_block(b):
-        height = jnp.broadcast_to(height_ref[pl.ds(b, 1), :], (8, marks))
+    offset_id = lax.broadcasted_iota(jnp.int32, (span, marks), 0).astype(F32).astype(BF16)
+    lane_window = lax.broadcasted_iota(jnp.int32, (8, num_levels), 1) // span
+
+    def operands(b):
+        lower = jnp.broadcast_to(lower_ref[pl.ds(b, 1), :], (8, marks))
+        fraction = jnp.broadcast_to(fraction_ref[pl.ds(b, 1), :], (8, marks))
         value = jnp.broadcast_to(value_ref[pl.ds(b, 1), :], (8, marks))
-        lower = jnp.minimum(jnp.floor(height), num_levels - 2.0)
-        fraction = height - lower
         share = jnp.where(upper_part, fraction, 1.0 - fraction)
         share = share * jnp.where(with_value, value, 1.0)
         high = share.astype(BF16).astype(F32)
         pieces = jnp.where(leading, high, share - high)
-        pieces = jnp.concatenate([pieces, pieces], axis=0).astype(BF16)
-        lower16 = jnp.concatenate([lower, lower], axis=0).astype(BF16)
-        lower_all = jnp.concatenate([lower16] * (num_levels // 16), axis=0)
-        hot = jnp.where(lower_all == level, jnp.ones((), BF16), jnp.zeros((), BF16))
-        sums = lax.dot_general(pieces, hot, NT, preferred_element_type=F32)
-        part_ref[pl.ds(pl.multiple_of(b * 8, 8), 8), :] = sums[:8]
+        window = jnp.floor(lower * (1.0 / span))
+        offset = lower - window * span
+        offset = jnp.concatenate([offset, offset], axis=0).astype(BF16)
+        offset = jnp.concatenate([offset] * (span // 16), axis=0)
+        hot = jnp.where(offset == offset_id, jnp.ones((), BF16), jnp.zeros((), BF16))
+        return [jnp.where(window == a, pieces, 0.0) for a in range(WAYS)], hot
 
     def one_chunk(k, carry):
         for copy in chunk_copies(k):
             copy.wait()
-        for i in range(chunk):
-            one_block(k * chunk + i)
+        rows = pl.ds(pl.multiple_of(k * chunk, chunk), chunk)
+        height = height_ref[rows, :]
+        lower = jnp.minimum(jnp.floor(height), num_levels - 2.0)
+        lower_ref[rows, :] = lower
+        fraction_ref[rows, :] = height - lower
+        for first in range(0, chunk, WAYS):
+            b = k * chunk + first
+            pieces, hots = zip(*(operands(b + i) for i in range(WAYS)))
+            sums = lax.dot_general(
+                jnp.concatenate(sum(pieces, []), axis=0).astype(BF16),
+                jnp.concatenate(hots, axis=0),
+                NT,
+                preferred_element_type=F32,
+            )
+            for i in range(WAYS):
+                total = jnp.zeros((8, num_levels), F32)
+                for a in range(WAYS):
+                    found = sums[(i * WAYS + a) * 8 : (i * WAYS + a + 1) * 8]
+                    turn = ((a - i) * span) % num_levels
+                    found = pltpu.roll(found, turn, 1) if turn else found
+                    total = jnp.where(lane_window == a, found, total)
+                part_ref[pl.ds(pl.multiple_of((b + i) * 8, 8), 8), :] = total
         return carry
 
     lax.fori_loop(0, CHUNKS, one_chunk, 0)
@@ -133,17 +159,25 @@
 
     value_sum = part(0) + pltpu.roll(part(1), 1, 1)
     weight_sum = part(2) + pltpu.roll(part(3), 1, 1)
-    place = place_ref[...]
-
-    def placed(x):
-        high, mid, low = (jnp.dot(place, y, preferred_element_type=F32) for y in split3(x))
-        return high + (mid + low)
-
-    out_ref[:, :num_levels] = placed(value_sum)
-    lane = lax.broadcasted_iota(jnp.int32, (slots, num_levels), 1)
-    out_ref[:, num_levels:] = jnp.where(
-        lane == num_levels - 1, code_ref[...], placed(weight_sum)
-    )
+    pieces = split3(jnp.concatenate([value_sum, weight_sum], axis=1))
+    size = slots // OUT_PARTS
+    copies = []
+    for p in range(OUT_PARTS):
+        rows = slice(p * size, (p + 1) * size)
+        high, mid, low = (
+            jnp.dot(place_ref[rows], y, preferred_element_type=F32) for y in pieces
+        )
+        sums = high + (mid + low)
+        lane = lax.broadcasted_iota(jnp.int32, (size, num_levels), 1)
+        out_ref[rows, :num_levels] = sums[:, :num_levels]
+        out_ref[rows, num_levels:] = jnp.where(
+            lane == num_levels - 1, code_ref[rows], sums[:, num_levels:]
+        )
+        copy = pltpu.make_async_copy(out_ref.at[rows], out_hbm.at[rows], out_sem.at[p])
+        copy.start()
+        copies.append(copy)
+    for copy in copies:
+        copy.wait()
 
 
 def deposit(count, owner, column, value, height, num_owners, capacity, num_levels):
@@ -153,7 +187,7 @@
         functools.partial(deposit_kernel, num_owners, capacity),
         out_shape=jax.ShapeDtypeStruct((slots, 2 * num_levels), F32),
         in_specs=[SMEM, HBM, HBM, HBM, HBM],
-        out_specs=VMEM,
+        out_specs=HBM,
         scratch_shapes=[
             pltpu.VMEM((blocks, marks), F32),
             pltpu.VMEM((blocks, marks), F32),
@@ -161,11 +195,15 @@
             pltpu.VMEM((1, blocks), jnp.int32),
             pltpu.VMEM((slots, blocks), BF16),
             pltpu.VMEM((slots, num_levels), F32),
+            pltpu.VMEM((blocks, marks), F32),
+            pltpu.VMEM((blocks, marks), F32),
             pltpu.VMEM((blocks * 8, num_levels), F32),
+            pltpu.VMEM((slots, 2 * num_levels), F32),
             pltpu.SemaphoreType.DMA((2,)),
             pltpu.SemaphoreType.DMA((2, CHUNKS)),
+            pltpu.SemaphoreType.DMA((OUT_PARTS,)),
         ],
-        compiler_params=pltpu.CompilerParams(vmem_limit_bytes=48 << 20),
+        compiler_params=pltpu.CompilerParams(vmem_limit_bytes=60 << 20),
         name="deposit",
     )(count, owner.reshape(1, blocks), column.reshape(1, blocks), value, height)
 
@@ -176,21 +214,22 @@
     columns = cells_x * cells_y
     values = arrived_ref[:, :num_levels]
     weights = arrived_ref[:, num_levels:]
-    lane = lax.broadcasted_iota(jnp.int32, (slots, num_levels), 1)
-    last = lane == num_levels - 1
-    code = weights[:, num_levels - 1 :]
+    last = lax.broadcasted_iota(jnp.int32, (slots, num_levels), 1) == num_levels - 1
+    pick = jnp.where(
+        lax.broadcasted_iota(jnp.int32, (8, num_levels), 1) == num_levels - 1, 1.0, 0.0
+    ).astype(BF16)
+    column_id = (lax.broadcasted_iota(jnp.int32, (columns, slots), 0) + 1).astype(F32)
+    codes = lax.dot_general(pick, weights.astype(BF16), NT, preferred_element_type=F32)
+    place = jnp.where(codes[:1] == column_id, 1.0, 0.0).astype(BF16)
     others = jnp.sum(jnp.where(last, 0.0, weights), axis=1, keepdims=True)
     weights = jnp.where(last, float(marks) - others, weights)
-    place = jnp.where(code == (lane + 1).astype(F32), 1.0, 0.0).astype(BF16)
-
-    def placed(x):
-        high, mid, low = (
-            lax.dot_general(place, y, TN, preferred_element_type=F32)[:columns] for y in split3(x)
-        )
-        return high + (mid + low)
-
+    high, mid, low = (
+        jnp.dot(place, y, preferred_element_type=F32)
+        for y in split3(jnp.concatenate([values, weights], axis=1))
+    )
+    sums = high + (mid + low)
     background = background_ref[...].reshape(columns, num_levels)
-    visc = jnp.exp((placed(values) + background) / (placed(weights) + 1.0))
+    visc = jnp.exp((sums[:, :num_levels] + background) / (sums[:, num_levels:] + 1.0))
     visc = visc.reshape(cells_x, cells_y, num_levels)
     out_ref[...] = visc
     odd = odd_ref[0] == 1

time: 46.5 us -> 40.9 us (0.88)
  Pallas kernels: 11.1 us -> 8.14 us
  local copies, waits for them, and re-layouts: 3.43 us -> 0.85 us
    pallas_call x1, Pallas kernels: 8.07 us -> 5.28 us  [deposit(): pl.pallas_call(functools.partial(deposit_kernel, num_owners, capacity), o...]
    unnamed x18 -> x10, local copies, waits for them, and re-layouts: 3.32 us -> 0.74 us
where the time goes in v3:
time: 40.9 us; the launch traced here: 40.6 us
  waiting for transfers between devices  15.2 us (37%)
  starting transfers between devices  14.5 us (35%)
  Pallas kernels  8.14 us (20%)
  between operations  1.44 us (4%)
  local copies, waits for them, and re-layouts  0.85 us (2%)
    all_to_all x1, starting transfers between devices, shards(): lax.all_to_all(send.reshape(devices, capacity, 2 * num_levels), ('gx', 'g...  7.3 us
    ppermute x4, waiting for transfers between devices, swapped(): far = lax.ppermute(far, ('gx', 'gy'), far_pairs)  5.46 us
    pallas_call x1, Pallas kernels, deposit(): pl.pallas_call(functools.partial(deposit_kernel, num_owners, capacity), o...  5.28 us
    ppermute x4, waiting for transfers between devices, swapped(): near = lax.ppermute(near, ('gx', 'gy'), near_pairs)  4.91 us
    all_to_all x1, waiting for transfers between devices, shards(): lax.all_to_all(send.reshape(devices, capacity, 2 * num_levels), ('gx', 'g...  4.85 us
    ppermute x4, starting transfers between devices, swapped(): near = lax.ppermute(near, ('gx', 'gy'), near_pairs)  4.19 us
    ppermute x4, starting transfers between devices, swapped(): far = lax.ppermute(far, ('gx', 'gy'), far_pairs)  3.04 us
    pallas_call x1, Pallas kernels, stokes(): pl.pallas_call(functools.partial(stokes_kernel, cells_y), out_shape=(jax....  1.83 us
  transfers between devices with their start and end apart: 9, of which 6 were waited for; matrix products, arithmetic and copies ran while one was open for 1% of the time, Pallas kernels for 0%

profile of v3, /device:TPU:0, one launch (start us, length us, event | category | flops | bytes accessed | tf_op | source)
XLA Modules:
  0.0 40.6 jit_solution(671335036417126116)
XLA Ops:
  1.3 5.3 %deposit.1 = f32[512,256]{1,0:T(8,128)} custom-call(s32[1]{0:T(128)S(6)} %copy.12.count_ref, s32[1,256]{1,0:T(1,128)} %bitcast.49, s32[1,256]{1,0:T(1,128)} %bitcast.50, f32[256,256]{1,0:T(8,128)} %value_hbm.1, f32[256,256]{1,0:T(8,128)} %height_hbm.1), custom_call_target="tpu_custom_call" | custom-call | tf_op jit(solution)/shard_map/deposit/pallas_call | solution.py:186
  6.6 0.0 copy-start.1
  6.6 0.0 copy-start.3
  6.6 7.3 %all-to-all-start = ((f32[32,16,256]{2,1,0:T(8,128)}), f32[32,16,256]{2,1,0:T(8,128)S(1)}, u32[]{:S(2)}, u32[]{:S(2)}) async-start(f32[32,16,256]{2,1,0:T(8,128)} %bitcast.28), calls=%async_computation | async-start | bytes 1048576 | tf_op jit(solution)/shard_map/all_to_all | solution.py:469
  13.9 0.0 copy-start.2
  13.9 0.0 copy-done.1
  13.9 0.7 %copy-done.2 = f32[8,8,128]{2,1,0:T(8,128)S(1)} copy-done((f32[8,8,128]{2,1,0:T(8,128)S(1)}, f32[8,8,128]{2,1,0:T(8,128)}, u32[]{:S(2)}) %copy-start.2) | copy-done | bytes 32792
  14.7 1.6 %collective-permute-start.1 = (f32[5,2,8,128]{3,2,1,0:T(8,128)S(1)}, f32[5,2,8,128]{3,2,1,0:T(8,128)S(1)}, u32[]{:S(2)}, u32[]{:S(2)}) collective-permute-start(f32[5,2,8,128]{3,2,1,0:T(8,128)S(1)} %broadcast_select_fusion.6), channel_id=1, source_target_pairs={{0,24},{1,25},{2,26},{3,27},{4,28},{5,29},{6,30},{7,31},{8,16},{9,... | collective-permute-start | bytes 122888 | tf_op jit(solution)/shard_map/ppermute | solution.py:422
  16.3 0.4 collective-permute-start
  16.6 0.1 pad.16.clone
  16.7 3.6 %collective-permute-done.1 = f32[5,2,8,128]{3,2,1,0:T(8,128)S(1)} collective-permute-done((f32[5,2,8,128]{3,2,1,0:T(8,128)S(1)}, f32[5,2,8,128]{3,2,1,0:T(8,128)S(1)}, u32[]{:S(2)}, u32[]{:S(2)}) %collective-permute-start.1) | collective-permute-done | bytes 40992 | tf_op jit(solution)/shard_map/ppermute | solution.py:422
  20.3 0.0 collective-permute-done
  20.3 0.1 broadcast_select_fusion.3
  20.4 0.2 collective-permute-start.3
  20.6 2.1 %collective-permute-start.2 = (f32[5,12,2,128]{3,2,1,0:T(2,128)S(1)}, f32[5,12,2,128]{3,2,1,0:T(2,128)S(1)}, u32[]{:S(2)}, u32[]{:S(2)}) collective-permute-start(f32[5,12,2,128]{3,2,1,0:T(2,128)S(1)} %get-tuple-element.16), channel_id=1, source_target_pairs={{0,1},{1,0},{2,3},{3,2},{4,5},{5,4},{6,7},{7,6},{8,9},{9,8},{10,11... | collective-permute-start | bytes 184328 | tf_op jit(solution)/shard_map/ppermute | solution.py:421
  22.7 0.1 pad_add_fusion.limits_ref
  22.7 0.0 collective-permute-done.3
  22.7 2.6 %collective-permute-done.2 = f32[5,12,2,128]{3,2,1,0:T(2,128)S(1)} collective-permute-done((f32[5,12,2,128]{3,2,1,0:T(2,128)S(1)}, f32[5,12,2,128]{3,2,1,0:T(2,128)S(1)}, u32[]{:S(2)}, u32[]{:S(2)}) %collective-permute-start.2) | collective-permute-done | bytes 61472 | tf_op jit(solution)/shard_map/ppermute | solution.py:421
  25.4 4.8 %all-to-all-done = f32[32,16,256]{2,1,0:T(8,128)S(1)} async-done(((f32[32,16,256]{2,1,0:T(8,128)}), f32[32,16,256]{2,1,0:T(8,128)S(1)}, u32[]{:S(2)}, u32[]{:S(2)}) %all-to-all-start) | async-done | bytes 524320 | tf_op jit(solution)/shard_map/all_to_all | solution.py:469
  30.2 1.0 %gather.1 = (f32[8,8,128]{2,1,0:T(8,128)}, f32[2,8,128]{2,1,0:T(8,128)S(1)}, f32[2,8,128]{2,1,0:T(8,128)S(1)}) custom-call(s32[1]{0:T(128)} %bitcast.6.odd_ref, f32[512,256]{1,0:T(8,128)S(1)} %bitcast.27, f32[8,8,128]{2,1,0:T(8,128)S(1)} %copy-done), custom_call_target="tpu_custom_call" | custom-call | tf_op jit(solution)/shard_map/gather/pallas_call | solution.py:243
  31.3 0.0 collective-permute-start.4
  31.3 0.6 %collective-permute-start.5 = (f32[2,8,128]{2,1,0:T(8,128)S(1)}, f32[2,8,128]{2,1,0:T(8,128)S(1)}, u32[]{:S(2)}, u32[]{:S(2)}) collective-permute-start(f32[2,8,128]{2,1,0:T(8,128)S(1)} %get-tuple-element.9), channel_id=1, source_target_pairs={{0,24},{1,25},{2,26},{3,27},{4,28},{5,29},{6,30},{7,31},{8,16},{9,... | collective-permute-start | bytes 24584 | tf_op jit(solution)/shard_map/ppermute | solution.py:422
  31.9 0.1 maximum_maximum_fusion
  32.1 0.0 copy-start.4
  32.1 0.4 collective-permute-done.4
  32.5 1.9 %collective-permute-done.5 = f32[2,8,128]{2,1,0:T(8,128)S(1)} collective-permute-done((f32[2,8,128]{2,1,0:T(8,128)S(1)}, f32[2,8,128]{2,1,0:T(8,128)S(1)}, u32[]{:S(2)}, u32[]{:S(2)}) %collective-permute-start.5) | collective-permute-done | bytes 8224 | tf_op jit(solution)/shard_map/ppermute | solution.py:422
  34.4 0.6 %collective-permute-start.7 = (f32[12,2,128]{2,1,0:T(2,128)S(1)}, f32[12,2,128]{2,1,0:T(2,128)S(1)}, u32[]{:S(2)}, u32[]{:S(2)}) collective-permute-start(f32[12,2,128]{2,1,0:T(2,128)S(1)} %bitcast.48), channel_id=1, source_target_pairs={{0,8},{1,2},{2,1},{3,4},{4,3},{5,6},{6,5},{7,15},{8,0},{9,10},{10,... | collective-permute-start | bytes 36872 | tf_op jit(solution)/shard_map/ppermute | solution.py:422
  35.0 1.8 %collective-permute-start.6 = (f32[12,2,128]{2,1,0:T(2,128)S(1)}, f32[12,2,128]{2,1,0:T(2,128)S(1)}, u32[]{:S(2)}, u32[]{:S(2)}) collective-permute-start(f32[12,2,128]{2,1,0:T(2,128)S(1)} %get-tuple-element.13), channel_id=1, source_target_pairs={{0,1},{1,0},{2,3},{3,2},{4,5},{5,4},{6,7},{7,6},{8,9},{9,8},{10,11... | collective-permute-start | bytes 36872 | tf_op jit(solution)/shard_map/ppermute | solution.py:421
  36.8 0.0 collective-permute-done.7
  36.8 1.9 %collective-permute-done.6 = f32[12,2,128]{2,1,0:T(2,128)S(1)} collective-permute-done((f32[12,2,128]{2,1,0:T(2,128)S(1)}, f32[12,2,128]{2,1,0:T(2,128)S(1)}, u32[]{:S(2)}, u32[]{:S(2)}) %collective-permute-start.6) | collective-permute-done | bytes 12320 | tf_op jit(solution)/shard_map/ppermute | solution.py:421
  38.7 0.1 maximum_maximum_fusion.1.visc_ref
  38.8 1.8 %stokes.1 = (f32[3,8,8,128]{3,2,1,0:T(8,128)}, f32[8,8,128]{2,1,0:T(8,128)}) custom-call(s32[4]{0:T(128)S(1)} %pad_add_fusion.limits_ref, f32[3,12,16,128]{3,2,1,0:T(8,128)S(1)} %slice.36.vel_ref, f32[12,16,128]{2,1,0:T(8,128)S(1)} %get-tuple-element.23.press_ref, f32[12,16,128]{2,1,0:T(8,128)S(1)} %get-tuple-element.22.buoy_ref, ...), custom_call_target="tpu_custom_call" | custom-call | tf_op jit(solution)/shard_map/stokes/pallas_call | solution.py:392
  (16 shorter events, 0.1 us)
Async XLA Ops:
  6.6 7.4 %copy-start.1 = (f32[3,8,8,128]{3,2,1,0:T(8,128)S(1)}, f32[3,8,8,128]{3,2,1,0:T(8,128)}, u32[]{:S(2)}) copy-start(f32[3,8,8,128]{3,2,1,0:T(8,128)} %param.9) | copy-start | bytes 294916
  6.6 7.4 %copy-start.3 = (f32[8,8,128]{2,1,0:T(8,128)S(1)}, f32[8,8,128]{2,1,0:T(8,128)}, u32[]{:S(2)}) copy-start(f32[8,8,128]{2,1,0:T(8,128)} %param.10) | copy-start | bytes 98308
  6.6 23.7 %all-to-all-start = ((f32[32,16,256]{2,1,0:T(8,128)}), f32[32,16,256]{2,1,0:T(8,128)S(1)}, u32[]{:S(2)}, u32[]{:S(2)}) async-start(f32[32,16,256]{2,1,0:T(8,128)} %bitcast.28), calls=%async_computation | async-start | bytes 1048576 | tf_op jit(solution)/shard_map/all_to_all | solution.py:469
  13.9 0.8 %copy-start.2 = (f32[8,8,128]{2,1,0:T(8,128)S(1)}, f32[8,8,128]{2,1,0:T(8,128)}, u32[]{:S(2)}) copy-start(f32[8,8,128]{2,1,0:T(8,128)} %param.11) | copy-start | bytes 98308
  14.7 5.6 %collective-permute-start.1 = (f32[5,2,8,128]{3,2,1,0:T(8,128)S(1)}, f32[5,2,8,128]{3,2,1,0:T(8,128)S(1)}, u32[]{:S(2)}, u32[]{:S(2)}) collective-permute-start(f32[5,2,8,128]{3,2,1,0:T(8,128)S(1)} %broadcast_select_fusion.6), channel_id=1, source_target_pairs={{0,24},{1,25},{2,26},{3,27},{4,28},{5,29},{6,30},{7,31},{8,16},{9,... | collective-permute-start | bytes 122888 | tf_op jit(solution)/shard_map/ppermute | solution.py:422
  16.3 4.0 %collective-permute-start = (f32[5,2,8,128]{3,2,1,0:T(8,128)S(1)}, f32[5,2,8,128]{3,2,1,0:T(8,128)S(1)}, u32[]{:S(2)}, u32[]{:S(2)}) collective-permute-start(f32[5,2,8,128]{3,2,1,0:T(8,128)S(1)} %get-tuple-element.19), channel_id=1, source_target_pairs={{0,8},{1,9},{2,10},{3,11},{4,12},{5,13},{6,14},{7,15},{8,0},{9,1},... | collective-permute-start | bytes 122888 | tf_op jit(solution)/shard_map/ppermute | solution.py:421
  20.4 2.4 %collective-permute-start.3 = (f32[5,12,2,128]{3,2,1,0:T(2,128)S(1)}, f32[5,12,2,128]{3,2,1,0:T(2,128)S(1)}, u32[]{:S(2)}, u32[]{:S(2)}) collective-permute-start(f32[5,12,2,128]{3,2,1,0:T(2,128)S(1)} %bitcast.39), channel_id=1, source_target_pairs={{0,8},{1,2},{2,1},{3,4},{4,3},{5,6},{6,5},{7,15},{8,0},{9,10},{10,... | collective-permute-start | bytes 184328 | tf_op jit(solution)/shard_map/ppermute | solution.py:422
  20.6 4.8 %collective-permute-start.2 = (f32[5,12,2,128]{3,2,1,0:T(2,128)S(1)}, f32[5,12,2,128]{3,2,1,0:T(2,128)S(1)}, u32[]{:S(2)}, u32[]{:S(2)}) collective-permute-start(f32[5,12,2,128]{3,2,1,0:T(2,128)S(1)} %get-tuple-element.16), channel_id=1, source_target_pairs={{0,1},{1,0},{2,3},{3,2},{4,5},{5,4},{6,7},{7,6},{8,9},{9,8},{10,11... | collective-permute-start | bytes 184328 | tf_op jit(solution)/shard_map/ppermute | solution.py:421
  25.4 4.9 %copy-start = (f32[8,8,128]{2,1,0:T(8,128)S(1)}, f32[8,8,128]{2,1,0:T(8,128)}, u32[]{:S(2)}) copy-start(f32[8,8,128]{2,1,0:T(8,128)} %background_ref.1) | copy-start | bytes 98308
  31.3 1.2 %collective-permute-start.4 = (f32[2,8,128]{2,1,0:T(8,128)S(1)}, f32[2,8,128]{2,1,0:T(8,128)S(1)}, u32[]{:S(2)}, u32[]{:S(2)}) collective-permute-start(f32[2,8,128]{2,1,0:T(8,128)S(1)} %get-tuple-element.8), channel_id=1, source_target_pairs={{0,8},{1,9},{2,10},{3,11},{4,12},{5,13},{6,14},{7,15},{8,0},{9,1},... | collective-permute-start | bytes 24584 | tf_op jit(solution)/shard_map/ppermute | solution.py:421
  31.3 3.1 %collective-permute-start.5 = (f32[2,8,128]{2,1,0:T(8,128)S(1)}, f32[2,8,128]{2,1,0:T(8,128)S(1)}, u32[]{:S(2)}, u32[]{:S(2)}) collective-permute-start(f32[2,8,128]{2,1,0:T(8,128)S(1)} %get-tuple-element.9), channel_id=1, source_target_pairs={{0,24},{1,25},{2,26},{3,27},{4,28},{5,29},{6,30},{7,31},{8,16},{9,... | collective-permute-start | bytes 24584 | tf_op jit(solution)/shard_map/ppermute | solution.py:422
  32.1 2.3 %copy-start.4 = (f32[8,8,128]{2,1,0:T(8,128)S(1)}, f32[8,8,128]{2,1,0:T(8,128)}, u32[]{:S(2)}) copy-start(f32[8,8,128]{2,1,0:T(8,128)} %get-tuple-element.7) | copy-start | bytes 98308
  34.4 2.4 %collective-permute-start.7 = (f32[12,2,128]{2,1,0:T(2,128)S(1)}, f32[12,2,128]{2,1,0:T(2,128)S(1)}, u32[]{:S(2)}, u32[]{:S(2)}) collective-permute-start(f32[12,2,128]{2,1,0:T(2,128)S(1)} %bitcast.48), channel_id=1, source_target_pairs={{0,8},{1,2},{2,1},{3,4},{4,3},{5,6},{6,5},{7,15},{8,0},{9,10},{10,... | collective-permute-start | bytes 36872 | tf_op jit(solution)/shard_map/ppermute | solution.py:422
  35.0 3.7 %collective-permute-start.6 = (f32[12,2,128]{2,1,0:T(2,128)S(1)}, f32[12,2,128]{2,1,0:T(2,128)S(1)}, u32[]{:S(2)}, u32[]{:S(2)}) collective-permute-start(f32[12,2,128]{2,1,0:T(2,128)S(1)} %get-tuple-element.13), channel_id=1, source_target_pairs={{0,1},{1,0},{2,3},{3,2},{4,5},{5,4},{6,7},{7,6},{8,9},{9,8},{10,11... | collective-permute-start | bytes 36872 | tf_op jit(solution)/shard_map/ppermute | solution.py:421

commit v4 on v3

--- a/solution.py
+++ b/solution.py
@@ -9,7 +9,7 @@
 
 ITERS = 2
 HALO = 2
-CHUNKS = 4
+CHUNKS = 1
 WAYS = 4
 OUT_PARTS = 2
 
@@ -208,7 +208,7 @@
     )(count, owner.reshape(1, blocks), column.reshape(1, blocks), value, height)
 
 
-def gather_kernel(marks, odd_ref, arrived_ref, background_ref, out_ref, near_ref, far_ref):
+def gather_kernel(marks, here_ref, arrived_ref, background_ref, out_ref, near_ref, far_ref):
     slots = arrived_ref.shape[0]
     cells_x, cells_y, num_levels = out_ref.shape
     columns = cells_x * cells_y
@@ -232,13 +232,13 @@
     visc = jnp.exp((sums[:, :num_levels] + background) / (sums[:, num_levels:] + 1.0))
     visc = visc.reshape(cells_x, cells_y, num_levels)
     out_ref[...] = visc
-    odd = odd_ref[0] == 1
+    odd = here_ref[:1, :] % 2 == 1
     first, final = visc[:HALO], visc[cells_x - HALO :]
     near_ref[...] = jnp.where(odd, first, final)
     far_ref[...] = jnp.where(odd, final, first)
 
 
-def gather(odd, arrived, background, marks):
+def gather(here, arrived, background, marks):
     strip = (HALO,) + background.shape[1:]
     return pl.pallas_call(
         functools.partial(gather_kernel, marks),
@@ -247,29 +247,32 @@
             jax.ShapeDtypeStruct(strip, F32),
             jax.ShapeDtypeStruct(strip, F32),
         ),
-        in_specs=[SMEM, VMEM, VMEM],
+        in_specs=[VMEM, VMEM, VMEM],
         out_specs=(VMEM, VMEM, VMEM),
         compiler_params=pltpu.CompilerParams(vmem_limit_bytes=48 << 20),
         name="gather",
-    )(odd, arrived, background)
+    )(here, arrived, background)
 
 
 def stokes_kernel(
     cells_y,
-    limits_ref,
+    sizes,
+    here_ref,
     vel_ref,
     press_ref,
     buoy_ref,
     visc_ref,
     new_vel_ref,
     new_press_ref,
+    visc_out_ref,
 ):
     wide_x, rows, num_levels = visc_ref.shape
     cells_x = wide_x - 2 * HALO
     row = lax.broadcasted_iota(jnp.int32, (rows, num_levels), 0)
     lane = lax.broadcasted_iota(jnp.int32, (rows, num_levels), 1)
-    first_x, size_x, first_y, size_y = (limits_ref[k] for k in range(4))
-    at_y = row + (first_y - HALO)
+    size_x, size_y = sizes[0] * cells_x, sizes[1] * cells_y
+    first_x = jnp.broadcast_to(here_ref[:1, :], row.shape) * cells_x
+    at_y = row + (here_ref[1:2, :] * cells_y - HALO)
     in_y = (at_y >= 0) & (at_y < size_y)
     in_y_face = (at_y >= 0) & (at_y < size_y - 1)
     low_lane = lane == 0
@@ -384,22 +387,24 @@
         for c in range(3):
             new_vel_ref[c, x] = vel[c][x + HALO][HALO : HALO + cells_y]
         new_press_ref[x] = press[x + HALO][HALO : HALO + cells_y]
-
-
-def stokes(limits, vel, press, buoy, visc, cells_y):
+        visc_out_ref[x] = visc[x + HALO][HALO : HALO + cells_y]
+
+
+def stokes(here, vel, press, buoy, visc, cells_y, sizes):
     wide_x, _, num_levels = visc.shape
     cells_x = wide_x - 2 * HALO
     return pl.pallas_call(
-        functools.partial(stokes_kernel, cells_y),
+        functools.partial(stokes_kernel, cells_y, sizes),
         out_shape=(
             jax.ShapeDtypeStruct((3, cells_x, cells_y, num_levels), F32),
             jax.ShapeDtypeStruct((cells_x, cells_y, num_levels), F32),
+            jax.ShapeDtypeStruct((cells_x, cells_y, num_levels), F32),
         ),
-        in_specs=[SMEM] + [VMEM] * 4,
-        out_specs=(VMEM, VMEM),
+        in_specs=[VMEM] * 5,
+        out_specs=(VMEM, VMEM, VMEM),
         compiler_params=pltpu.CompilerParams(vmem_limit_bytes=48 << 20),
         name="stokes",
-    )(limits, vel, press, buoy, visc)
+    )(here, vel, press, buoy, visc)
 
 
 def partners(size_x, size_y):
@@ -474,22 +479,16 @@
         tiled=True,
     ).reshape(devices * capacity, 2 * num_levels)
     pairs = partners(size_x, size_y)
-    odd_x = lax.axis_index("gx") % 2
-    odd_y = lax.axis_index("gy") % 2
+    place_x, place_y = lax.axis_index("gx"), lax.axis_index("gy")
+    odd_x, odd_y = place_x % 2, place_y % 2
+    here = jnp.where(lax.broadcasted_iota(jnp.int32, (8, num_levels), 0) == 0, place_x, place_y)
     fields = jnp.concatenate([velocity, pressure[None], buoyancy[None]], axis=0)
     fields = widened(fields, *strips(fields, odd_x == 1, 1), pairs, odd_x == 1, odd_y == 1)
-    viscosity, near, far = gather(odd_x.astype(jnp.int32)[None], arrived, background, marks)
-    visc = widened(viscosity, near, far, pairs, odd_x == 1, odd_y == 1)
-    limits = jnp.stack(
-        [
-            lax.axis_index("gx") * cells_x,
-            jnp.int32(size_x * cells_x),
-            lax.axis_index("gy") * cells_y,
-            jnp.int32(size_y * cells_y),
-        ]
-    ).astype(jnp.int32)
-    new_vel, new_press = stokes(limits, fields[:3], fields[3], fields[4], visc, cells_y)
-    return (new_vel, new_press, viscosity)
+    visc, near, far = gather(here, arrived, background, marks)
+    visc = widened(visc, near, far, pairs, odd_x == 1, odd_y == 1)
+    return stokes(
+        here, fields[:3], fields[3], fields[4], visc, cells_y, (size_x, size_y)
+    )
 
 
 def solution(mesh):

time: 40.9 us -> 39.1 us (0.956)
  Pallas kernels: 8.14 us -> 6.23 us
    pallas_call x1, Pallas kernels: 5.28 us -> 4.52 us  [deposit(): pl.pallas_call(functools.partial(deposit_kernel, num_owners, capacity), o...]
    pallas_call x1, Pallas kernels: 1.04 us -> 0.42 us  [gather(): pl.pallas_call(functools.partial(gather_kernel, marks), out_shape=(jax.Sh...]
    pallas_call x1, Pallas kernels: 1.83 us -> 1.29 us  [stokes(): pl.pallas_call(functools.partial(stokes_kernel, cells_y, sizes), out_shap...]
where the time goes in v4:
time: 39.1 us; the launch traced here: 38.8 us
  waiting for transfers between devices  15.4 us (39%)
  starting transfers between devices  14.5 us (37%)
  Pallas kernels  6.23 us (16%)
  between operations  1.44 us (4%)
  local copies, waits for them, and re-layouts  0.92 us (2%)
    all_to_all x1, starting transfers between devices, shards(): lax.all_to_all(send.reshape(devices, capacity, 2 * num_levels), ('gx', 'g...  7.31 us
    ppermute x4, waiting for transfers between devices, swapped(): far = lax.ppermute(far, ('gx', 'gy'), far_pairs)  5.54 us
    ppermute x4, waiting for transfers between devices, swapped(): near = lax.ppermute(near, ('gx', 'gy'), near_pairs)  5.01 us
    all_to_all x1, waiting for transfers between devices, shards(): lax.all_to_all(send.reshape(devices, capacity, 2 * num_levels), ('gx', 'g...  4.85 us
    pallas_call x1, Pallas kernels, deposit(): pl.pallas_call(functools.partial(deposit_kernel, num_owners, capacity), o...  4.52 us
    ppermute x4, starting transfers between devices, swapped(): near = lax.ppermute(near, ('gx', 'gy'), near_pairs)  4.24 us
    ppermute x4, starting transfers between devices, swapped(): far = lax.ppermute(far, ('gx', 'gy'), far_pairs)  2.96 us
    pallas_call x1, Pallas kernels, stokes(): pl.pallas_call(functools.partial(stokes_kernel, cells_y, sizes), out_shap...  1.29 us
  transfers between devices with their start and end apart: 9, of which 6 were waited for; matrix products, arithmetic and copies ran while one was open for 1% of the time, Pallas kernels for 0%

profile of v4, /device:TPU:0, one launch (start us, length us, event | category | flops | bytes accessed | tf_op | source)
XLA Modules:
  0.0 38.8 jit_solution(8708252605789262154)
XLA Ops:
  1.3 4.5 %deposit.1 = f32[512,256]{1,0:T(8,128)} custom-call(s32[1]{0:T(128)S(6)} %copy.12.count_ref, s32[1,256]{1,0:T(1,128)} %bitcast.46, s32[1,256]{1,0:T(1,128)} %bitcast.47, f32[256,256]{1,0:T(8,128)} %value_hbm.1, f32[256,256]{1,0:T(8,128)} %height_hbm.1), custom_call_target="tpu_custom_call" | custom-call | tf_op jit(solution)/shard_map/deposit/pallas_call | solution.py:186
  5.8 0.0 copy-start.1
  5.8 0.0 copy-start.3
  5.8 7.3 %all-to-all-start = ((f32[32,16,256]{2,1,0:T(8,128)}), f32[32,16,256]{2,1,0:T(8,128)S(1)}, u32[]{:S(2)}, u32[]{:S(2)}) async-start(f32[32,16,256]{2,1,0:T(8,128)} %bitcast.25), calls=%async_computation | async-start | bytes 1048576 | tf_op jit(solution)/shard_map/all_to_all | solution.py:474
  13.1 0.0 copy-start.2
  13.2 0.0 copy-done.1
  13.2 0.0 copy-done.3
  13.2 0.7 %copy-done.2 = f32[8,8,128]{2,1,0:T(8,128)S(1)} copy-done((f32[8,8,128]{2,1,0:T(8,128)S(1)}, f32[8,8,128]{2,1,0:T(8,128)}, u32[]{:S(2)}) %copy-start.2) | copy-done | bytes 32792
  13.9 1.6 %collective-permute-start.1 = (f32[5,2,8,128]{3,2,1,0:T(8,128)S(1)}, f32[5,2,8,128]{3,2,1,0:T(8,128)S(1)}, u32[]{:S(2)}, u32[]{:S(2)}) collective-permute-start(f32[5,2,8,128]{3,2,1,0:T(8,128)S(1)} %broadcast_select_fusion.6), channel_id=1, source_target_pairs={{0,24},{1,25},{2,26},{3,27},{4,28},{5,29},{6,30},{7,31},{8,16},{9,... | collective-permute-start | bytes 122888 | tf_op jit(solution)/shard_map/ppermute | solution.py:427
  15.5 0.4 collective-permute-start
  15.9 0.1 pad.16.clone
  16.0 3.6 %collective-permute-done.1 = f32[5,2,8,128]{3,2,1,0:T(8,128)S(1)} collective-permute-done((f32[5,2,8,128]{3,2,1,0:T(8,128)S(1)}, f32[5,2,8,128]{3,2,1,0:T(8,128)S(1)}, u32[]{:S(2)}, u32[]{:S(2)}) %collective-permute-start.1) | collective-permute-done | bytes 40992 | tf_op jit(solution)/shard_map/ppermute | solution.py:427
  19.5 0.0 collective-permute-done
  19.5 0.1 broadcast_select_fusion.3
  19.6 0.2 collective-permute-start.3
  19.8 2.1 %collective-permute-start.2 = (f32[5,12,2,128]{3,2,1,0:T(2,128)S(1)}, f32[5,12,2,128]{3,2,1,0:T(2,128)S(1)}, u32[]{:S(2)}, u32[]{:S(2)}) collective-permute-start(f32[5,12,2,128]{3,2,1,0:T(2,128)S(1)} %get-tuple-element.12), channel_id=1, source_target_pairs={{0,1},{1,0},{2,3},{3,2},{4,5},{5,4},{6,7},{7,6},{8,9},{9,8},{10,11... | collective-permute-start | bytes 184328 | tf_op jit(solution)/shard_map/ppermute | solution.py:426
  21.9 0.0 collective-permute-done.3
  21.9 2.7 %collective-permute-done.2 = f32[5,12,2,128]{3,2,1,0:T(2,128)S(1)} collective-permute-done((f32[5,12,2,128]{3,2,1,0:T(2,128)S(1)}, f32[5,12,2,128]{3,2,1,0:T(2,128)S(1)}, u32[]{:S(2)}, u32[]{:S(2)}) %collective-permute-start.2) | collective-permute-done | bytes 61472 | tf_op jit(solution)/shard_map/ppermute | solution.py:426
  24.7 4.8 %all-to-all-done = f32[32,16,256]{2,1,0:T(8,128)S(1)} async-done(((f32[32,16,256]{2,1,0:T(8,128)}), f32[32,16,256]{2,1,0:T(8,128)S(1)}, u32[]{:S(2)}, u32[]{:S(2)}) %all-to-all-start) | async-done | bytes 524320 | tf_op jit(solution)/shard_map/all_to_all | solution.py:474
  29.5 0.1 iota.7.here_ref
  29.6 0.4 %gather.1 = (f32[8,8,128]{2,1,0:T(8,128)S(1)}, f32[2,8,128]{2,1,0:T(8,128)S(1)}, f32[2,8,128]{2,1,0:T(8,128)S(1)}) custom-call(s32[8,128]{1,0:T(8,128)S(1)} %iota.7.here_ref, f32[512,256]{1,0:T(8,128)S(1)} %bitcast.24, f32[8,8,128]{2,1,0:T(8,128)S(1)} %copy-done), custom_call_target="tpu_custom_call" | custom-call | tf_op jit(solution)/shard_map/gather/pallas_call | solution.py:243
  30.0 0.1 collective-permute-start.4
  30.1 0.6 %collective-permute-start.5 = (f32[2,8,128]{2,1,0:T(8,128)S(1)}, f32[2,8,128]{2,1,0:T(8,128)S(1)}, u32[]{:S(2)}, u32[]{:S(2)}) collective-permute-start(f32[2,8,128]{2,1,0:T(8,128)S(1)} %get-tuple-element.7), channel_id=1, source_target_pairs={{0,24},{1,25},{2,26},{3,27},{4,28},{5,29},{6,30},{7,31},{8,16},{9,... | collective-permute-start | bytes 24584 | tf_op jit(solution)/shard_map/ppermute | solution.py:427
  30.7 0.1 maximum_maximum_fusion
  30.8 0.4 %collective-permute-done.4 = f32[2,8,128]{2,1,0:T(8,128)S(1)} collective-permute-done((f32[2,8,128]{2,1,0:T(8,128)S(1)}, f32[2,8,128]{2,1,0:T(8,128)S(1)}, u32[]{:S(2)}, u32[]{:S(2)}) %collective-permute-start.4) | collective-permute-done | bytes 8224 | tf_op jit(solution)/shard_map/ppermute | solution.py:426
  31.2 2.0 %collective-permute-done.5 = f32[2,8,128]{2,1,0:T(8,128)S(1)} collective-permute-done((f32[2,8,128]{2,1,0:T(8,128)S(1)}, f32[2,8,128]{2,1,0:T(8,128)S(1)}, u32[]{:S(2)}, u32[]{:S(2)}) %collective-permute-start.5) | collective-permute-done | bytes 8224 | tf_op jit(solution)/shard_map/ppermute | solution.py:427
  33.3 0.5 %collective-permute-start.7 = (f32[12,2,128]{2,1,0:T(2,128)S(1)}, f32[12,2,128]{2,1,0:T(2,128)S(1)}, u32[]{:S(2)}, u32[]{:S(2)}) collective-permute-start(f32[12,2,128]{2,1,0:T(2,128)S(1)} %bitcast.45), channel_id=1, source_target_pairs={{0,8},{1,2},{2,1},{3,4},{4,3},{5,6},{6,5},{7,15},{8,0},{9,10},{10,... | collective-permute-start | bytes 36872 | tf_op jit(solution)/shard_map/ppermute | solution.py:427
  33.8 1.7 %collective-permute-start.6 = (f32[12,2,128]{2,1,0:T(2,128)S(1)}, f32[12,2,128]{2,1,0:T(2,128)S(1)}, u32[]{:S(2)}, u32[]{:S(2)}) collective-permute-start(f32[12,2,128]{2,1,0:T(2,128)S(1)} %get-tuple-element.9), channel_id=1, source_target_pairs={{0,1},{1,0},{2,3},{3,2},{4,5},{5,4},{6,7},{7,6},{8,9},{9,8},{10,11... | collective-permute-start | bytes 36872 | tf_op jit(solution)/shard_map/ppermute | solution.py:426
  35.6 0.0 collective-permute-done.7
  35.6 1.9 %collective-permute-done.6 = f32[12,2,128]{2,1,0:T(2,128)S(1)} collective-permute-done((f32[12,2,128]{2,1,0:T(2,128)S(1)}, f32[12,2,128]{2,1,0:T(2,128)S(1)}, u32[]{:S(2)}, u32[]{:S(2)}) %collective-permute-start.6) | collective-permute-done | bytes 12320 | tf_op jit(solution)/shard_map/ppermute | solution.py:426
  37.5 0.1 maximum_maximum_fusion.1.visc_ref
  37.5 1.3 %stokes.1 = (f32[3,8,8,128]{3,2,1,0:T(8,128)}, f32[8,8,128]{2,1,0:T(8,128)}, f32[8,8,128]{2,1,0:T(8,128)}) custom-call(s32[8,128]{1,0:T(8,128)S(1)} %iota.7.here_ref, f32[3,12,16,128]{3,2,1,0:T(8,128)S(1)} %slice.36.vel_ref, f32[12,16,128]{2,1,0:T(8,128)S(1)} %get-tuple-element.19.press_ref, f32[12,16,128]{2,1,0:T(8,128)S(1)} %get-tuple-element.18.buoy_ref, ...), custom_call_target="tpu_custom_call" | custom-call | tf_op jit(solution)/shard_map/stokes/pallas_call | solution.py:396
  (15 shorter events, 0.1 us)
Async XLA Ops:
  5.8 7.4 %copy-start.1 = (f32[3,8,8,128]{3,2,1,0:T(8,128)S(1)}, f32[3,8,8,128]{3,2,1,0:T(8,128)}, u32[]{:S(2)}) copy-start(f32[3,8,8,128]{3,2,1,0:T(8,128)} %param.9) | copy-start | bytes 294916
  5.8 7.4 %copy-start.3 = (f32[8,8,128]{2,1,0:T(8,128)S(1)}, f32[8,8,128]{2,1,0:T(8,128)}, u32[]{:S(2)}) copy-start(f32[8,8,128]{2,1,0:T(8,128)} %param.10) | copy-start | bytes 98308
  5.8 23.7 %all-to-all-start = ((f32[32,16,256]{2,1,0:T(8,128)}), f32[32,16,256]{2,1,0:T(8,128)S(1)}, u32[]{:S(2)}, u32[]{:S(2)}) async-start(f32[32,16,256]{2,1,0:T(8,128)} %bitcast.25), calls=%async_computation | async-start | bytes 1048576 | tf_op jit(solution)/shard_map/all_to_all | solution.py:474
  13.1 0.8 %copy-start.2 = (f32[8,8,128]{2,1,0:T(8,128)S(1)}, f32[8,8,128]{2,1,0:T(8,128)}, u32[]{:S(2)}) copy-start(f32[8,8,128]{2,1,0:T(8,128)} %param.11) | copy-start | bytes 98308
  13.9 5.6 %collective-permute-start.1 = (f32[5,2,8,128]{3,2,1,0:T(8,128)S(1)}, f32[5,2,8,128]{3,2,1,0:T(8,128)S(1)}, u32[]{:S(2)}, u32[]{:S(2)}) collective-permute-start(f32[5,2,8,128]{3,2,1,0:T(8,128)S(1)} %broadcast_select_fusion.6), channel_id=1, source_target_pairs={{0,24},{1,25},{2,26},{3,27},{4,28},{5,29},{6,30},{7,31},{8,16},{9,... | collective-permute-start | bytes 122888 | tf_op jit(solution)/shard_map/ppermute | solution.py:427
  15.5 4.0 %collective-permute-start = (f32[5,2,8,128]{3,2,1,0:T(8,128)S(1)}, f32[5,2,8,128]{3,2,1,0:T(8,128)S(1)}, u32[]{:S(2)}, u32[]{:S(2)}) collective-permute-start(f32[5,2,8,128]{3,2,1,0:T(8,128)S(1)} %get-tuple-element.15), channel_id=1, source_target_pairs={{0,8},{1,9},{2,10},{3,11},{4,12},{5,13},{6,14},{7,15},{8,0},{9,1},... | collective-permute-start | bytes 122888 | tf_op jit(solution)/shard_map/ppermute | solution.py:426
  19.6 2.3 %collective-permute-start.3 = (f32[5,12,2,128]{3,2,1,0:T(2,128)S(1)}, f32[5,12,2,128]{3,2,1,0:T(2,128)S(1)}, u32[]{:S(2)}, u32[]{:S(2)}) collective-permute-start(f32[5,12,2,128]{3,2,1,0:T(2,128)S(1)} %bitcast.36), channel_id=1, source_target_pairs={{0,8},{1,2},{2,1},{3,4},{4,3},{5,6},{6,5},{7,15},{8,0},{9,10},{10,... | collective-permute-start | bytes 184328 | tf_op jit(solution)/shard_map/ppermute | solution.py:427
  19.8 4.8 %collective-permute-start.2 = (f32[5,12,2,128]{3,2,1,0:T(2,128)S(1)}, f32[5,12,2,128]{3,2,1,0:T(2,128)S(1)}, u32[]{:S(2)}, u32[]{:S(2)}) collective-permute-start(f32[5,12,2,128]{3,2,1,0:T(2,128)S(1)} %get-tuple-element.12), channel_id=1, source_target_pairs={{0,1},{1,0},{2,3},{3,2},{4,5},{5,4},{6,7},{7,6},{8,9},{9,8},{10,11... | collective-permute-start | bytes 184328 | tf_op jit(solution)/shard_map/ppermute | solution.py:426
  24.6 4.9 %copy-start = (f32[8,8,128]{2,1,0:T(8,128)S(1)}, f32[8,8,128]{2,1,0:T(8,128)}, u32[]{:S(2)}) copy-start(f32[8,8,128]{2,1,0:T(8,128)} %background_ref.1) | copy-start | bytes 98308
  30.0 1.2 %collective-permute-start.4 = (f32[2,8,128]{2,1,0:T(8,128)S(1)}, f32[2,8,128]{2,1,0:T(8,128)S(1)}, u32[]{:S(2)}, u32[]{:S(2)}) collective-permute-start(f32[2,8,128]{2,1,0:T(8,128)S(1)} %get-tuple-element.6), channel_id=1, source_target_pairs={{0,8},{1,9},{2,10},{3,11},{4,12},{5,13},{6,14},{7,15},{8,0},{9,1},... | collective-permute-start | bytes 24584 | tf_op jit(solution)/shard_map/ppermute | solution.py:426
  30.1 3.1 %collective-permute-start.5 = (f32[2,8,128]{2,1,0:T(8,128)S(1)}, f32[2,8,128]{2,1,0:T(8,128)S(1)}, u32[]{:S(2)}, u32[]{:S(2)}) collective-permute-start(f32[2,8,128]{2,1,0:T(8,128)S(1)} %get-tuple-element.7), channel_id=1, source_target_pairs={{0,24},{1,25},{2,26},{3,27},{4,28},{5,29},{6,30},{7,31},{8,16},{9,... | collective-permute-start | bytes 24584 | tf_op jit(solution)/shard_map/ppermute | solution.py:427
  33.3 2.3 %collective-permute-start.7 = (f32[12,2,128]{2,1,0:T(2,128)S(1)}, f32[12,2,128]{2,1,0:T(2,128)S(1)}, u32[]{:S(2)}, u32[]{:S(2)}) collective-permute-start(f32[12,2,128]{2,1,0:T(2,128)S(1)} %bitcast.45), channel_id=1, source_target_pairs={{0,8},{1,2},{2,1},{3,4},{4,3},{5,6},{6,5},{7,15},{8,0},{9,10},{10,... | collective-permute-start | bytes 36872 | tf_op jit(solution)/shard_map/ppermute | solution.py:427
  33.8 3.7 %collective-permute-start.6 = (f32[12,2,128]{2,1,0:T(2,128)S(1)}, f32[12,2,128]{2,1,0:T(2,128)S(1)}, u32[]{:S(2)}, u32[]{:S(2)}) collective-permute-start(f32[12,2,128]{2,1,0:T(2,128)S(1)} %get-tuple-element.9), channel_id=1, source_target_pairs={{0,1},{1,0},{2,3},{3,2},{4,5},{5,4},{6,7},{7,6},{8,9},{9,8},{10,11... | collective-permute-start | bytes 36872 | tf_op jit(solution)/shard_map/ppermute | solution.py:426

commit v5 on v4

--- a/solution.py
+++ b/solution.py
@@ -9,9 +9,8 @@
 
 ITERS = 2
 HALO = 2
-CHUNKS = 1
 WAYS = 4
-OUT_PARTS = 2
+OUT_PARTS = 4
 
 PRESS_STEP = 0.5
 VEL_STEP = 0.05
@@ -52,32 +51,22 @@
     fraction_ref,
     part_ref,
     out_ref,
-    index_sem,
-    block_sem,
+    sem,
     out_sem,
 ):
     blocks, marks = value_ref.shape
     num_levels = out_ref.shape[1] // 2
     slots = num_owners * capacity
-    chunk = blocks // CHUNKS
-
-    def chunk_copies(k):
-        rows = pl.ds(pl.multiple_of(k * chunk, chunk), chunk)
-        return (
-            pltpu.make_async_copy(height_hbm.at[rows], height_ref.at[rows], block_sem.at[0, k]),
-            pltpu.make_async_copy(value_hbm.at[rows], value_ref.at[rows], block_sem.at[1, k]),
-        )
-
-    index_copies = (
-        pltpu.make_async_copy(owner_hbm, owner_ref, index_sem.at[0]),
-        pltpu.make_async_copy(column_hbm, column_ref, index_sem.at[1]),
+
+    copies = (
+        pltpu.make_async_copy(owner_hbm, owner_ref, sem.at[0]),
+        pltpu.make_async_copy(column_hbm, column_ref, sem.at[1]),
+        pltpu.make_async_copy(height_hbm, height_ref, sem.at[2]),
+        pltpu.make_async_copy(value_hbm, value_ref, sem.at[3]),
     )
-    for copy in index_copies:
+    for copy in copies:
         copy.start()
-    for k in range(CHUNKS):
-        for copy in chunk_copies(k):
-            copy.start()
-    for copy in index_copies:
+    for copy in copies:
         copy.wait()
 
     owner = owner_ref[...]
@@ -124,34 +113,26 @@
         hot = jnp.where(offset == offset_id, jnp.ones((), BF16), jnp.zeros((), BF16))
         return [jnp.where(window == a, pieces, 0.0) for a in range(WAYS)], hot
 
-    def one_chunk(k, carry):
-        for copy in chunk_copies(k):
-            copy.wait()
-        rows = pl.ds(pl.multiple_of(k * chunk, chunk), chunk)
-        height = height_ref[rows, :]
-        lower = jnp.minimum(jnp.floor(height), num_levels - 2.0)
-        lower_ref[rows, :] = lower
-        fraction_ref[rows, :] = height - lower
-        for first in range(0, chunk, WAYS):
-            b = k * chunk + first
-            pieces, hots = zip(*(operands(b + i) for i in range(WAYS)))
-            sums = lax.dot_general(
-                jnp.concatenate(sum(pieces, []), axis=0).astype(BF16),
-                jnp.concatenate(hots, axis=0),
-                NT,
-                preferred_element_type=F32,
-            )
-            for i in range(WAYS):
-                total = jnp.zeros((8, num_levels), F32)
-                for a in range(WAYS):
-                    found = sums[(i * WAYS + a) * 8 : (i * WAYS + a + 1) * 8]
-                    turn = ((a - i) * span) % num_levels
-                    found = pltpu.roll(found, turn, 1) if turn else found
-                    total = jnp.where(lane_window == a, found, total)
-                part_ref[pl.ds(pl.multiple_of((b + i) * 8, 8), 8), :] = total
-        return carry
-
-    lax.fori_loop(0, CHUNKS, one_chunk, 0)
+    height = height_ref[...]
+    lower = jnp.minimum(jnp.floor(height), num_levels - 2.0)
+    lower_ref[...] = lower
+    fraction_ref[...] = height - lower
+    for b in range(0, blocks, WAYS):
+        pieces, hots = zip(*(operands(b + i) for i in range(WAYS)))
+        sums = lax.dot_general(
+            jnp.concatenate(sum(pieces, []), axis=0).astype(BF16),
+            jnp.concatenate(hots, axis=0),
+            NT,
+            preferred_element_type=F32,
+        )
+        for i in range(WAYS):
+            total = jnp.zeros((8, num_levels), F32)
+            for a in range(WAYS):
+                found = sums[(i * WAYS + a) * 8 : (i * WAYS + a + 1) * 8]
+                turn = ((a - i) * span) % num_levels
+                found = pltpu.roll(found, turn, 1) if turn else found
+                total = jnp.where(lane_window == a, found, total)
+            part_ref[(b + i) * 8 : (b + i + 1) * 8, :] = total
 
     def part(kind):
         high = part_ref[pl.ds(kind, blocks, stride=8), :]
@@ -199,8 +180,7 @@
             pltpu.VMEM((blocks, marks), F32),
             pltpu.VMEM((blocks * 8, num_levels), F32),
             pltpu.VMEM((slots, 2 * num_levels), F32),
-            pltpu.SemaphoreType.DMA((2,)),
-            pltpu.SemaphoreType.DMA((2, CHUNKS)),
+            pltpu.SemaphoreType.DMA((4,)),
             pltpu.SemaphoreType.DMA((OUT_PARTS,)),
         ],
         compiler_params=pltpu.CompilerParams(vmem_limit_bytes=60 << 20),
@@ -483,7 +463,9 @@
     odd_x, odd_y = place_x % 2, place_y % 2
     here = jnp.where(lax.broadcasted_iota(jnp.int32, (8, num_levels), 0) == 0, place_x, place_y)
     fields = jnp.concatenate([velocity, pressure[None], buoyancy[None]], axis=0)
-    fields = widened(fields, *strips(fields, odd_x == 1, 1), pairs, odd_x == 1, odd_y == 1)
+    near, far = strips(fields, odd_x == 1, 1)
+    near, here = lax.optimization_barrier((near, here))
+    fields = widened(fields, near, far, pairs, odd_x == 1, odd_y == 1)
     visc, near, far = gather(here, arrived, background, marks)
     visc = widened(visc, near, far, pairs, odd_x == 1, odd_y == 1)
     return stokes(

time: 39.1 us -> 39 us (level)
  no operation moved by 1% of the time
where the time goes in v5:
time: 39 us; the launch traced here: 38.7 us
  waiting for transfers between devices  15.1 us (39%)
  starting transfers between devices  14.7 us (38%)
  Pallas kernels  6.16 us (16%)
  between operations  1.45 us (4%)
  local copies, waits for them, and re-layouts  0.92 us (2%)
    all_to_all x1, starting transfers between devices, shards(): lax.all_to_all(send.reshape(devices, capacity, 2 * num_levels), ('gx', 'g...  7.3 us
    ppermute x4, waiting for transfers between devices, swapped(): far = lax.ppermute(far, ('gx', 'gy'), far_pairs)  5.51 us
    all_to_all x1, waiting for transfers between devices, shards(): lax.all_to_all(send.reshape(devices, capacity, 2 * num_levels), ('gx', 'g...  4.92 us
    ppermute x4, waiting for transfers between devices, swapped(): near = lax.ppermute(near, ('gx', 'gy'), near_pairs)  4.65 us
    pallas_call x1, Pallas kernels, deposit(): pl.pallas_call(functools.partial(deposit_kernel, num_owners, capacity), o...  4.44 us
    ppermute x4, starting transfers between devices, swapped(): near = lax.ppermute(near, ('gx', 'gy'), near_pairs)  4.36 us
    ppermute x4, starting transfers between devices, swapped(): far = lax.ppermute(far, ('gx', 'gy'), far_pairs)  3.09 us
    pallas_call x1, Pallas kernels, stokes(): pl.pallas_call(functools.partial(stokes_kernel, cells_y, sizes), out_shap...  1.29 us
  transfers between devices with their start and end apart: 9, of which 6 were waited for; matrix products, arithmetic and copies ran while one was open for 1% of the time, Pallas kernels for 0%

profile of v5, /device:TPU:0, one launch (start us, length us, event | category | flops | bytes accessed | tf_op | source)
XLA Modules:
  0.0 38.7 jit_solution(12405608736028644578)
XLA Ops:
  1.3 4.4 %deposit.1 = f32[512,256]{1,0:T(8,128)} custom-call(s32[1]{0:T(128)S(6)} %copy.12.count_ref, s32[1,256]{1,0:T(1,128)} %bitcast.46, s32[1,256]{1,0:T(1,128)} %bitcast.47, f32[256,256]{1,0:T(8,128)} %value_hbm.1, f32[256,256]{1,0:T(8,128)} %height_hbm.1), custom_call_target="tpu_custom_call" | custom-call | tf_op jit(solution)/shard_map/deposit/pallas_call | solution.py:167
  5.7 0.0 copy-start.1
  5.7 0.0 copy-start.3
  5.8 7.3 %all-to-all-start = ((f32[32,16,256]{2,1,0:T(8,128)}), f32[32,16,256]{2,1,0:T(8,128)S(1)}, u32[]{:S(2)}, u32[]{:S(2)}) async-start(f32[32,16,256]{2,1,0:T(8,128)} %bitcast.25), calls=%async_computation | async-start | bytes 1048576 | tf_op jit(solution)/shard_map/all_to_all | solution.py:454
  13.1 0.0 copy-start.2
  13.1 0.0 copy-done.1
  13.1 0.0 copy-done.3
  13.1 0.7 %copy-done.2 = f32[8,8,128]{2,1,0:T(8,128)S(1)} copy-done((f32[8,8,128]{2,1,0:T(8,128)S(1)}, f32[8,8,128]{2,1,0:T(8,128)}, u32[]{:S(2)}) %copy-start.2) | copy-done | bytes 32792
  13.9 0.1 iota.7.here_ref
  13.9 0.3 collective-permute-start
  14.2 1.6 %collective-permute-start.1 = (f32[5,2,8,128]{3,2,1,0:T(8,128)S(1)}, f32[5,2,8,128]{3,2,1,0:T(8,128)S(1)}, u32[]{:S(2)}, u32[]{:S(2)}) collective-permute-start(f32[5,2,8,128]{3,2,1,0:T(8,128)S(1)} %get-tuple-element.19), channel_id=1, source_target_pairs={{0,24},{1,25},{2,26},{3,27},{4,28},{5,29},{6,30},{7,31},{8,16},{9,... | collective-permute-start | bytes 122888 | tf_op jit(solution)/shard_map/ppermute | solution.py:407
  15.8 0.0 collective-permute-done
  15.8 3.5 %collective-permute-done.1 = f32[5,2,8,128]{3,2,1,0:T(8,128)S(1)} collective-permute-done((f32[5,2,8,128]{3,2,1,0:T(8,128)S(1)}, f32[5,2,8,128]{3,2,1,0:T(8,128)S(1)}, u32[]{:S(2)}, u32[]{:S(2)}) %collective-permute-start.1) | collective-permute-done | bytes 40992 | tf_op jit(solution)/shard_map/ppermute | solution.py:407
  19.4 0.1 broadcast_select_fusion.3
  19.5 0.3 collective-permute-start.3
  19.8 2.2 %collective-permute-start.2 = (f32[5,12,2,128]{3,2,1,0:T(2,128)S(1)}, f32[5,12,2,128]{3,2,1,0:T(2,128)S(1)}, u32[]{:S(2)}, u32[]{:S(2)}) collective-permute-start(f32[5,12,2,128]{3,2,1,0:T(2,128)S(1)} %get-tuple-element.16), channel_id=1, source_target_pairs={{0,1},{1,0},{2,3},{3,2},{4,5},{5,4},{6,7},{7,6},{8,9},{9,8},{10,11... | collective-permute-start | bytes 184328 | tf_op jit(solution)/shard_map/ppermute | solution.py:406
  22.0 0.1 pad.16.clone
  22.1 0.0 collective-permute-done.3
  22.1 2.4 %collective-permute-done.2 = f32[5,12,2,128]{3,2,1,0:T(2,128)S(1)} collective-permute-done((f32[5,12,2,128]{3,2,1,0:T(2,128)S(1)}, f32[5,12,2,128]{3,2,1,0:T(2,128)S(1)}, u32[]{:S(2)}, u32[]{:S(2)}) %collective-permute-start.2) | collective-permute-done | bytes 61472 | tf_op jit(solution)/shard_map/ppermute | solution.py:406
  24.5 4.9 %all-to-all-done = f32[32,16,256]{2,1,0:T(8,128)S(1)} async-done(((f32[32,16,256]{2,1,0:T(8,128)}), f32[32,16,256]{2,1,0:T(8,128)S(1)}, u32[]{:S(2)}, u32[]{:S(2)}) %all-to-all-start) | async-done | bytes 524320 | tf_op jit(solution)/shard_map/all_to_all | solution.py:454
  29.4 0.4 %gather.1 = (f32[8,8,128]{2,1,0:T(8,128)S(1)}, f32[2,8,128]{2,1,0:T(8,128)S(1)}, f32[2,8,128]{2,1,0:T(8,128)S(1)}) custom-call(s32[8,128]{1,0:T(8,128)S(1)} %iota.7.here_ref, f32[512,256]{1,0:T(8,128)S(1)} %bitcast.24, f32[8,8,128]{2,1,0:T(8,128)S(1)} %copy-done), custom_call_target="tpu_custom_call" | custom-call | tf_op jit(solution)/shard_map/gather/pallas_call | solution.py:223
  29.8 0.1 collective-permute-start.4
  29.9 0.6 %collective-permute-start.5 = (f32[2,8,128]{2,1,0:T(8,128)S(1)}, f32[2,8,128]{2,1,0:T(8,128)S(1)}, u32[]{:S(2)}, u32[]{:S(2)}) collective-permute-start(f32[2,8,128]{2,1,0:T(8,128)S(1)} %get-tuple-element.11), channel_id=1, source_target_pairs={{0,24},{1,25},{2,26},{3,27},{4,28},{5,29},{6,30},{7,31},{8,16},{9,... | collective-permute-start | bytes 24584 | tf_op jit(solution)/shard_map/ppermute | solution.py:407
  30.6 0.1 maximum_maximum_fusion
  30.7 0.4 %collective-permute-done.4 = f32[2,8,128]{2,1,0:T(8,128)S(1)} collective-permute-done((f32[2,8,128]{2,1,0:T(8,128)S(1)}, f32[2,8,128]{2,1,0:T(8,128)S(1)}, u32[]{:S(2)}, u32[]{:S(2)}) %collective-permute-start.4) | collective-permute-done | bytes 8224 | tf_op jit(solution)/shard_map/ppermute | solution.py:406
  31.1 2.0 %collective-permute-done.5 = f32[2,8,128]{2,1,0:T(8,128)S(1)} collective-permute-done((f32[2,8,128]{2,1,0:T(8,128)S(1)}, f32[2,8,128]{2,1,0:T(8,128)S(1)}, u32[]{:S(2)}, u32[]{:S(2)}) %collective-permute-start.5) | collective-permute-done | bytes 8224 | tf_op jit(solution)/shard_map/ppermute | solution.py:407
  33.1 0.5 %collective-permute-start.7 = (f32[12,2,128]{2,1,0:T(2,128)S(1)}, f32[12,2,128]{2,1,0:T(2,128)S(1)}, u32[]{:S(2)}, u32[]{:S(2)}) collective-permute-start(f32[12,2,128]{2,1,0:T(2,128)S(1)} %bitcast.45), channel_id=1, source_target_pairs={{0,8},{1,2},{2,1},{3,4},{4,3},{5,6},{6,5},{7,15},{8,0},{9,10},{10,... | collective-permute-start | bytes 36872 | tf_op jit(solution)/shard_map/ppermute | solution.py:407
  33.6 1.8 %collective-permute-start.6 = (f32[12,2,128]{2,1,0:T(2,128)S(1)}, f32[12,2,128]{2,1,0:T(2,128)S(1)}, u32[]{:S(2)}, u32[]{:S(2)}) collective-permute-start(f32[12,2,128]{2,1,0:T(2,128)S(1)} %get-tuple-element.13), channel_id=1, source_target_pairs={{0,1},{1,0},{2,3},{3,2},{4,5},{5,4},{6,7},{7,6},{8,9},{9,8},{10,11... | collective-permute-start | bytes 36872 | tf_op jit(solution)/shard_map/ppermute | solution.py:406
  35.4 0.0 collective-permute-done.7
  35.5 1.9 %collective-permute-done.6 = f32[12,2,128]{2,1,0:T(2,128)S(1)} collective-permute-done((f32[12,2,128]{2,1,0:T(2,128)S(1)}, f32[12,2,128]{2,1,0:T(2,128)S(1)}, u32[]{:S(2)}, u32[]{:S(2)}) %collective-permute-start.6) | collective-permute-done | bytes 12320 | tf_op jit(solution)/shard_map/ppermute | solution.py:406
  37.3 0.1 maximum_maximum_fusion.1.visc_ref
  37.4 1.3 %stokes.1 = (f32[3,8,8,128]{3,2,1,0:T(8,128)}, f32[8,8,128]{2,1,0:T(8,128)}, f32[8,8,128]{2,1,0:T(8,128)}) custom-call(s32[8,128]{1,0:T(8,128)S(1)} %iota.7.here_ref, f32[3,12,16,128]{3,2,1,0:T(8,128)S(1)} %slice.36.vel_ref, f32[12,16,128]{2,1,0:T(8,128)S(1)} %get-tuple-element.23.press_ref, f32[12,16,128]{2,1,0:T(8,128)S(1)} %get-tuple-element.22.buoy_ref, ...), custom_call_target="tpu_custom_call" | custom-call | tf_op jit(solution)/shard_map/stokes/pallas_call | solution.py:376
  (15 shorter events, 0.1 us)
Async XLA Ops:
  5.7 7.4 %copy-start.1 = (f32[3,8,8,128]{3,2,1,0:T(8,128)S(1)}, f32[3,8,8,128]{3,2,1,0:T(8,128)}, u32[]{:S(2)}) copy-start(f32[3,8,8,128]{3,2,1,0:T(8,128)} %param.9) | copy-start | bytes 294916
  5.7 7.4 %copy-start.3 = (f32[8,8,128]{2,1,0:T(8,128)S(1)}, f32[8,8,128]{2,1,0:T(8,128)}, u32[]{:S(2)}) copy-start(f32[8,8,128]{2,1,0:T(8,128)} %param.10) | copy-start | bytes 98308
  5.8 23.7 %all-to-all-start = ((f32[32,16,256]{2,1,0:T(8,128)}), f32[32,16,256]{2,1,0:T(8,128)S(1)}, u32[]{:S(2)}, u32[]{:S(2)}) async-start(f32[32,16,256]{2,1,0:T(8,128)} %bitcast.25), calls=%async_computation | async-start | bytes 1048576 | tf_op jit(solution)/shard_map/all_to_all | solution.py:454
  13.1 0.8 %copy-start.2 = (f32[8,8,128]{2,1,0:T(8,128)S(1)}, f32[8,8,128]{2,1,0:T(8,128)}, u32[]{:S(2)}) copy-start(f32[8,8,128]{2,1,0:T(8,128)} %param.11) | copy-start | bytes 98308
  13.9 1.9 %collective-permute-start = (f32[5,2,8,128]{3,2,1,0:T(8,128)S(1)}, f32[5,2,8,128]{3,2,1,0:T(8,128)S(1)}, u32[]{:S(2)}, u32[]{:S(2)}) collective-permute-start(f32[5,2,8,128]{3,2,1,0:T(8,128)S(1)} %broadcast_select_fusion.7), channel_id=1, source_target_pairs={{0,8},{1,9},{2,10},{3,11},{4,12},{5,13},{6,14},{7,15},{8,0},{9,1},... | collective-permute-start | bytes 122888 | tf_op jit(solution)/shard_map/ppermute | solution.py:406
  14.2 5.2 %collective-permute-start.1 = (f32[5,2,8,128]{3,2,1,0:T(8,128)S(1)}, f32[5,2,8,128]{3,2,1,0:T(8,128)S(1)}, u32[]{:S(2)}, u32[]{:S(2)}) collective-permute-start(f32[5,2,8,128]{3,2,1,0:T(8,128)S(1)} %get-tuple-element.19), channel_id=1, source_target_pairs={{0,24},{1,25},{2,26},{3,27},{4,28},{5,29},{6,30},{7,31},{8,16},{9,... | collective-permute-start | bytes 122888 | tf_op jit(solution)/shard_map/ppermute | solution.py:407
  19.5 2.6 %collective-permute-start.3 = (f32[5,12,2,128]{3,2,1,0:T(2,128)S(1)}, f32[5,12,2,128]{3,2,1,0:T(2,128)S(1)}, u32[]{:S(2)}, u32[]{:S(2)}) collective-permute-start(f32[5,12,2,128]{3,2,1,0:T(2,128)S(1)} %bitcast.36), channel_id=1, source_target_pairs={{0,8},{1,2},{2,1},{3,4},{4,3},{5,6},{6,5},{7,15},{8,0},{9,10},{10,... | collective-permute-start | bytes 184328 | tf_op jit(solution)/shard_map/ppermute | solution.py:407
  19.8 4.7 %collective-permute-start.2 = (f32[5,12,2,128]{3,2,1,0:T(2,128)S(1)}, f32[5,12,2,128]{3,2,1,0:T(2,128)S(1)}, u32[]{:S(2)}, u32[]{:S(2)}) collective-permute-start(f32[5,12,2,128]{3,2,1,0:T(2,128)S(1)} %get-tuple-element.16), channel_id=1, source_target_pairs={{0,1},{1,0},{2,3},{3,2},{4,5},{5,4},{6,7},{7,6},{8,9},{9,8},{10,11... | collective-permute-start | bytes 184328 | tf_op jit(solution)/shard_map/ppermute | solution.py:406
  24.5 4.9 %copy-start = (f32[8,8,128]{2,1,0:T(8,128)S(1)}, f32[8,8,128]{2,1,0:T(8,128)}, u32[]{:S(2)}) copy-start(f32[8,8,128]{2,1,0:T(8,128)} %background_ref.1) | copy-start | bytes 98308
  29.8 1.2 %collective-permute-start.4 = (f32[2,8,128]{2,1,0:T(8,128)S(1)}, f32[2,8,128]{2,1,0:T(8,128)S(1)}, u32[]{:S(2)}, u32[]{:S(2)}) collective-permute-start(f32[2,8,128]{2,1,0:T(8,128)S(1)} %get-tuple-element.10), channel_id=1, source_target_pairs={{0,8},{1,9},{2,10},{3,11},{4,12},{5,13},{6,14},{7,15},{8,0},{9,1},... | collective-permute-start | bytes 24584 | tf_op jit(solution)/shard_map/ppermute | solution.py:406
  29.9 3.1 %collective-permute-start.5 = (f32[2,8,128]{2,1,0:T(8,128)S(1)}, f32[2,8,128]{2,1,0:T(8,128)S(1)}, u32[]{:S(2)}, u32[]{:S(2)}) collective-permute-start(f32[2,8,128]{2,1,0:T(8,128)S(1)} %get-tuple-element.11), channel_id=1, source_target_pairs={{0,24},{1,25},{2,26},{3,27},{4,28},{5,29},{6,30},{7,31},{8,16},{9,... | collective-permute-start | bytes 24584 | tf_op jit(solution)/shard_map/ppermute | solution.py:407
  33.1 2.3 %collective-permute-start.7 = (f32[12,2,128]{2,1,0:T(2,128)S(1)}, f32[12,2,128]{2,1,0:T(2,128)S(1)}, u32[]{:S(2)}, u32[]{:S(2)}) collective-permute-start(f32[12,2,128]{2,1,0:T(2,128)S(1)} %bitcast.45), channel_id=1, source_target_pairs={{0,8},{1,2},{2,1},{3,4},{4,3},{5,6},{6,5},{7,15},{8,0},{9,10},{10,... | collective-permute-start | bytes 36872 | tf_op jit(solution)/shard_map/ppermute | solution.py:407
  33.6 3.7 %collective-permute-start.6 = (f32[12,2,128]{2,1,0:T(2,128)S(1)}, f32[12,2,128]{2,1,0:T(2,128)S(1)}, u32[]{:S(2)}, u32[]{:S(2)}) collective-permute-start(f32[12,2,128]{2,1,0:T(2,128)S(1)} %get-tuple-element.13), channel_id=1, source_target_pairs={{0,1},{1,0},{2,3},{3,2},{4,5},{5,4},{6,7},{7,6},{8,9},{9,8},{10,11... | collective-permute-start | bytes 36872 | tf_op jit(solution)/shard_map/ppermute | solution.py:406

commit v6 on v5

--- a/solution.py
+++ b/solution.py
@@ -178,7 +178,7 @@
             pltpu.VMEM((slots, num_levels), F32),
             pltpu.VMEM((blocks, marks), F32),
             pltpu.VMEM((blocks, marks), F32),
-            pltpu.VMEM((blocks * 8, num_levels), F32),
+            pltpu.VMEM((blocks * 8 + 8, num_levels), F32),
             pltpu.VMEM((slots, 2 * num_levels), F32),
             pltpu.SemaphoreType.DMA((4,)),
             pltpu.SemaphoreType.DMA((OUT_PARTS,)),

time: 39 us -> 39 us (level)
  no operation moved by 1% of the time
where the time goes in v6:
time: 39 us; the launch traced here: 38.7 us
  waiting for transfers between devices  15.1 us (39%)
  starting transfers between devices  14.7 us (38%)
  Pallas kernels  6.16 us (16%)
  between operations  1.45 us (4%)
  local copies, waits for them, and re-layouts  0.92 us (2%)
    all_to_all x1, starting transfers between devices, shards(): lax.all_to_all(send.reshape(devices, capacity, 2 * num_levels), ('gx', 'g...  7.3 us
    ppermute x4, waiting for transfers between devices, swapped(): far = lax.ppermute(far, ('gx', 'gy'), far_pairs)  5.51 us
    all_to_all x1, waiting for transfers between devices, shards(): lax.all_to_all(send.reshape(devices, capacity, 2 * num_levels), ('gx', 'g...  4.92 us
    ppermute x4, waiting for transfers between devices, swapped(): near = lax.ppermute(near, ('gx', 'gy'), near_pairs)  4.65 us
    pallas_call x1, Pallas kernels, deposit(): pl.pallas_call(functools.partial(deposit_kernel, num_owners, capacity), o...  4.44 us
    ppermute x4, starting transfers between devices, swapped(): near = lax.ppermute(near, ('gx', 'gy'), near_pairs)  4.36 us
    ppermute x4, starting transfers between devices, swapped(): far = lax.ppermute(far, ('gx', 'gy'), far_pairs)  3.09 us
    pallas_call x1, Pallas kernels, stokes(): pl.pallas_call(functools.partial(stokes_kernel, cells_y, sizes), out_shap...  1.29 us
  transfers between devices with their start and end apart: 9, of which 6 were waited for; matrix products, arithmetic and copies ran while one was open for 1% of the time, Pallas kernels for 0%

profile of v6, /device:TPU:0, one launch (start us, length us, event | category | flops | bytes accessed | tf_op | source)
XLA Modules:
  0.0 38.7 jit_solution(8593125050926346661)
XLA Ops:
  1.3 4.4 %deposit.1 = f32[512,256]{1,0:T(8,128)} custom-call(s32[1]{0:T(128)S(6)} %copy.12.count_ref, s32[1,256]{1,0:T(1,128)} %bitcast.46, s32[1,256]{1,0:T(1,128)} %bitcast.47, f32[256,256]{1,0:T(8,128)} %value_hbm.1, f32[256,256]{1,0:T(8,128)} %height_hbm.1), custom_call_target="tpu_custom_call" | custom-call | tf_op jit(solution)/shard_map/deposit/pallas_call | solution.py:167
  5.7 0.0 copy-start.1
  5.7 0.0 copy-start.3
  5.8 7.3 %all-to-all-start = ((f32[32,16,256]{2,1,0:T(8,128)}), f32[32,16,256]{2,1,0:T(8,128)S(1)}, u32[]{:S(2)}, u32[]{:S(2)}) async-start(f32[32,16,256]{2,1,0:T(8,128)} %bitcast.25), calls=%async_computation | async-start | bytes 1048576 | tf_op jit(solution)/shard_map/all_to_all | solution.py:454
  13.1 0.0 copy-start.2
  13.1 0.0 copy-done.1
  13.1 0.0 copy-done.3
  13.1 0.7 %copy-done.2 = f32[8,8,128]{2,1,0:T(8,128)S(1)} copy-done((f32[8,8,128]{2,1,0:T(8,128)S(1)}, f32[8,8,128]{2,1,0:T(8,128)}, u32[]{:S(2)}) %copy-start.2) | copy-done | bytes 32792
  13.9 0.1 iota.7.here_ref
  13.9 0.3 collective-permute-start
  14.2 1.6 %collective-permute-start.1 = (f32[5,2,8,128]{3,2,1,0:T(8,128)S(1)}, f32[5,2,8,128]{3,2,1,0:T(8,128)S(1)}, u32[]{:S(2)}, u32[]{:S(2)}) collective-permute-start(f32[5,2,8,128]{3,2,1,0:T(8,128)S(1)} %get-tuple-element.19), channel_id=1, source_target_pairs={{0,24},{1,25},{2,26},{3,27},{4,28},{5,29},{6,30},{7,31},{8,16},{9,... | collective-permute-start | bytes 122888 | tf_op jit(solution)/shard_map/ppermute | solution.py:407
  15.8 0.0 collective-permute-done
  15.8 3.5 %collective-permute-done.1 = f32[5,2,8,128]{3,2,1,0:T(8,128)S(1)} collective-permute-done((f32[5,2,8,128]{3,2,1,0:T(8,128)S(1)}, f32[5,2,8,128]{3,2,1,0:T(8,128)S(1)}, u32[]{:S(2)}, u32[]{:S(2)}) %collective-permute-start.1) | collective-permute-done | bytes 40992 | tf_op jit(solution)/shard_map/ppermute | solution.py:407
  19.4 0.1 broadcast_select_fusion.3
  19.5 0.3 collective-permute-start.3
  19.8 2.2 %collective-permute-start.2 = (f32[5,12,2,128]{3,2,1,0:T(2,128)S(1)}, f32[5,12,2,128]{3,2,1,0:T(2,128)S(1)}, u32[]{:S(2)}, u32[]{:S(2)}) collective-permute-start(f32[5,12,2,128]{3,2,1,0:T(2,128)S(1)} %get-tuple-element.16), channel_id=1, source_target_pairs={{0,1},{1,0},{2,3},{3,2},{4,5},{5,4},{6,7},{7,6},{8,9},{9,8},{10,11... | collective-permute-start | bytes 184328 | tf_op jit(solution)/shard_map/ppermute | solution.py:406
  22.0 0.1 pad.16.clone
  22.1 0.0 collective-permute-done.3
  22.1 2.4 %collective-permute-done.2 = f32[5,12,2,128]{3,2,1,0:T(2,128)S(1)} collective-permute-done((f32[5,12,2,128]{3,2,1,0:T(2,128)S(1)}, f32[5,12,2,128]{3,2,1,0:T(2,128)S(1)}, u32[]{:S(2)}, u32[]{:S(2)}) %collective-permute-start.2) | collective-permute-done | bytes 61472 | tf_op jit(solution)/shard_map/ppermute | solution.py:406
  24.5 4.9 %all-to-all-done = f32[32,16,256]{2,1,0:T(8,128)S(1)} async-done(((f32[32,16,256]{2,1,0:T(8,128)}), f32[32,16,256]{2,1,0:T(8,128)S(1)}, u32[]{:S(2)}, u32[]{:S(2)}) %all-to-all-start) | async-done | bytes 524320 | tf_op jit(solution)/shard_map/all_to_all | solution.py:454
  29.4 0.4 %gather.1 = (f32[8,8,128]{2,1,0:T(8,128)S(1)}, f32[2,8,128]{2,1,0:T(8,128)S(1)}, f32[2,8,128]{2,1,0:T(8,128)S(1)}) custom-call(s32[8,128]{1,0:T(8,128)S(1)} %iota.7.here_ref, f32[512,256]{1,0:T(8,128)S(1)} %bitcast.24, f32[8,8,128]{2,1,0:T(8,128)S(1)} %copy-done), custom_call_target="tpu_custom_call" | custom-call | tf_op jit(solution)/shard_map/gather/pallas_call | solution.py:223
  29.8 0.1 collective-permute-start.4
  29.9 0.6 %collective-permute-start.5 = (f32[2,8,128]{2,1,0:T(8,128)S(1)}, f32[2,8,128]{2,1,0:T(8,128)S(1)}, u32[]{:S(2)}, u32[]{:S(2)}) collective-permute-start(f32[2,8,128]{2,1,0:T(8,128)S(1)} %get-tuple-element.11), channel_id=1, source_target_pairs={{0,24},{1,25},{2,26},{3,27},{4,28},{5,29},{6,30},{7,31},{8,16},{9,... | collective-permute-start | bytes 24584 | tf_op jit(solution)/shard_map/ppermute | solution.py:407
  30.6 0.1 maximum_maximum_fusion
  30.7 0.4 %collective-permute-done.4 = f32[2,8,128]{2,1,0:T(8,128)S(1)} collective-permute-done((f32[2,8,128]{2,1,0:T(8,128)S(1)}, f32[2,8,128]{2,1,0:T(8,128)S(1)}, u32[]{:S(2)}, u32[]{:S(2)}) %collective-permute-start.4) | collective-permute-done | bytes 8224 | tf_op jit(solution)/shard_map/ppermute | solution.py:406
  31.1 2.0 %collective-permute-done.5 = f32[2,8,128]{2,1,0:T(8,128)S(1)} collective-permute-done((f32[2,8,128]{2,1,0:T(8,128)S(1)}, f32[2,8,128]{2,1,0:T(8,128)S(1)}, u32[]{:S(2)}, u32[]{:S(2)}) %collective-permute-start.5) | collective-permute-done | bytes 8224 | tf_op jit(solution)/shard_map/ppermute | solution.py:407
  33.1 0.5 %collective-permute-start.7 = (f32[12,2,128]{2,1,0:T(2,128)S(1)}, f32[12,2,128]{2,1,0:T(2,128)S(1)}, u32[]{:S(2)}, u32[]{:S(2)}) collective-permute-start(f32[12,2,128]{2,1,0:T(2,128)S(1)} %bitcast.45), channel_id=1, source_target_pairs={{0,8},{1,2},{2,1},{3,4},{4,3},{5,6},{6,5},{7,15},{8,0},{9,10},{10,... | collective-permute-start | bytes 36872 | tf_op jit(solution)/shard_map/ppermute | solution.py:407
  33.6 1.8 %collective-permute-start.6 = (f32[12,2,128]{2,1,0:T(2,128)S(1)}, f32[12,2,128]{2,1,0:T(2,128)S(1)}, u32[]{:S(2)}, u32[]{:S(2)}) collective-permute-start(f32[12,2,128]{2,1,0:T(2,128)S(1)} %get-tuple-element.13), channel_id=1, source_target_pairs={{0,1},{1,0},{2,3},{3,2},{4,5},{5,4},{6,7},{7,6},{8,9},{9,8},{10,11... | collective-permute-start | bytes 36872 | tf_op jit(solution)/shard_map/ppermute | solution.py:406
  35.4 0.0 collective-permute-done.7
  35.5 1.9 %collective-permute-done.6 = f32[12,2,128]{2,1,0:T(2,128)S(1)} collective-permute-done((f32[12,2,128]{2,1,0:T(2,128)S(1)}, f32[12,2,128]{2,1,0:T(2,128)S(1)}, u32[]{:S(2)}, u32[]{:S(2)}) %collective-permute-start.6) | collective-permute-done | bytes 12320 | tf_op jit(solution)/shard_map/ppermute | solution.py:406
  37.3 0.1 maximum_maximum_fusion.1.visc_ref
  37.4 1.3 %stokes.1 = (f32[3,8,8,128]{3,2,1,0:T(8,128)}, f32[8,8,128]{2,1,0:T(8,128)}, f32[8,8,128]{2,1,0:T(8,128)}) custom-call(s32[8,128]{1,0:T(8,128)S(1)} %iota.7.here_ref, f32[3,12,16,128]{3,2,1,0:T(8,128)S(1)} %slice.36.vel_ref, f32[12,16,128]{2,1,0:T(8,128)S(1)} %get-tuple-element.23.press_ref, f32[12,16,128]{2,1,0:T(8,128)S(1)} %get-tuple-element.22.buoy_ref, ...), custom_call_target="tpu_custom_call" | custom-call | tf_op jit(solution)/shard_map/stokes/pallas_call | solution.py:376
  (15 shorter events, 0.1 us)
Async XLA Ops:
  5.7 7.4 %copy-start.1 = (f32[3,8,8,128]{3,2,1,0:T(8,128)S(1)}, f32[3,8,8,128]{3,2,1,0:T(8,128)}, u32[]{:S(2)}) copy-start(f32[3,8,8,128]{3,2,1,0:T(8,128)} %param.9) | copy-start | bytes 294916
  5.7 7.4 %copy-start.3 = (f32[8,8,128]{2,1,0:T(8,128)S(1)}, f32[8,8,128]{2,1,0:T(8,128)}, u32[]{:S(2)}) copy-start(f32[8,8,128]{2,1,0:T(8,128)} %param.10) | copy-start | bytes 98308
  5.8 23.7 %all-to-all-start = ((f32[32,16,256]{2,1,0:T(8,128)}), f32[32,16,256]{2,1,0:T(8,128)S(1)}, u32[]{:S(2)}, u32[]{:S(2)}) async-start(f32[32,16,256]{2,1,0:T(8,128)} %bitcast.25), calls=%async_computation | async-start | bytes 1048576 | tf_op jit(solution)/shard_map/all_to_all | solution.py:454
  13.1 0.8 %copy-start.2 = (f32[8,8,128]{2,1,0:T(8,128)S(1)}, f32[8,8,128]{2,1,0:T(8,128)}, u32[]{:S(2)}) copy-start(f32[8,8,128]{2,1,0:T(8,128)} %param.11) | copy-start | bytes 98308
  13.9 1.9 %collective-permute-start = (f32[5,2,8,128]{3,2,1,0:T(8,128)S(1)}, f32[5,2,8,128]{3,2,1,0:T(8,128)S(1)}, u32[]{:S(2)}, u32[]{:S(2)}) collective-permute-start(f32[5,2,8,128]{3,2,1,0:T(8,128)S(1)} %broadcast_select_fusion.7), channel_id=1, source_target_pairs={{0,8},{1,9},{2,10},{3,11},{4,12},{5,13},{6,14},{7,15},{8,0},{9,1},... | collective-permute-start | bytes 122888 | tf_op jit(solution)/shard_map/ppermute | solution.py:406
  14.2 5.2 %collective-permute-start.1 = (f32[5,2,8,128]{3,2,1,0:T(8,128)S(1)}, f32[5,2,8,128]{3,2,1,0:T(8,128)S(1)}, u32[]{:S(2)}, u32[]{:S(2)}) collective-permute-start(f32[5,2,8,128]{3,2,1,0:T(8,128)S(1)} %get-tuple-element.19), channel_id=1, source_target_pairs={{0,24},{1,25},{2,26},{3,27},{4,28},{5,29},{6,30},{7,31},{8,16},{9,... | collective-permute-start | bytes 122888 | tf_op jit(solution)/shard_map/ppermute | solution.py:407
  19.5 2.6 %collective-permute-start.3 = (f32[5,12,2,128]{3,2,1,0:T(2,128)S(1)}, f32[5,12,2,128]{3,2,1,0:T(2,128)S(1)}, u32[]{:S(2)}, u32[]{:S(2)}) collective-permute-start(f32[5,12,2,128]{3,2,1,0:T(2,128)S(1)} %bitcast.36), channel_id=1, source_target_pairs={{0,8},{1,2},{2,1},{3,4},{4,3},{5,6},{6,5},{7,15},{8,0},{9,10},{10,... | collective-permute-start | bytes 184328 | tf_op jit(solution)/shard_map/ppermute | solution.py:407
  19.8 4.7 %collective-permute-start.2 = (f32[5,12,2,128]{3,2,1,0:T(2,128)S(1)}, f32[5,12,2,128]{3,2,1,0:T(2,128)S(1)}, u32[]{:S(2)}, u32[]{:S(2)}) collective-permute-start(f32[5,12,2,128]{3,2,1,0:T(2,128)S(1)} %get-tuple-element.16), channel_id=1, source_target_pairs={{0,1},{1,0},{2,3},{3,2},{4,5},{5,4},{6,7},{7,6},{8,9},{9,8},{10,11... | collective-permute-start | bytes 184328 | tf_op jit(solution)/shard_map/ppermute | solution.py:406
  24.5 4.9 %copy-start = (f32[8,8,128]{2,1,0:T(8,128)S(1)}, f32[8,8,128]{2,1,0:T(8,128)}, u32[]{:S(2)}) copy-start(f32[8,8,128]{2,1,0:T(8,128)} %background_ref.1) | copy-start | bytes 98308
  29.8 1.2 %collective-permute-start.4 = (f32[2,8,128]{2,1,0:T(8,128)S(1)}, f32[2,8,128]{2,1,0:T(8,128)S(1)}, u32[]{:S(2)}, u32[]{:S(2)}) collective-permute-start(f32[2,8,128]{2,1,0:T(8,128)S(1)} %get-tuple-element.10), channel_id=1, source_target_pairs={{0,8},{1,9},{2,10},{3,11},{4,12},{5,13},{6,14},{7,15},{8,0},{9,1},... | collective-permute-start | bytes 24584 | tf_op jit(solution)/shard_map/ppermute | solution.py:406
  29.9 3.1 %collective-permute-start.5 = (f32[2,8,128]{2,1,0:T(8,128)S(1)}, f32[2,8,128]{2,1,0:T(8,128)S(1)}, u32[]{:S(2)}, u32[]{:S(2)}) collective-permute-start(f32[2,8,128]{2,1,0:T(8,128)S(1)} %get-tuple-element.11), channel_id=1, source_target_pairs={{0,24},{1,25},{2,26},{3,27},{4,28},{5,29},{6,30},{7,31},{8,16},{9,... | collective-permute-start | bytes 24584 | tf_op jit(solution)/shard_map/ppermute | solution.py:407
  33.1 2.3 %collective-permute-start.7 = (f32[12,2,128]{2,1,0:T(2,128)S(1)}, f32[12,2,128]{2,1,0:T(2,128)S(1)}, u32[]{:S(2)}, u32[]{:S(2)}) collective-permute-start(f32[12,2,128]{2,1,0:T(2,128)S(1)} %bitcast.45), channel_id=1, source_target_pairs={{0,8},{1,2},{2,1},{3,4},{4,3},{5,6},{6,5},{7,15},{8,0},{9,10},{10,... | collective-permute-start | bytes 36872 | tf_op jit(solution)/shard_map/ppermute | solution.py:407
  33.6 3.7 %collective-permute-start.6 = (f32[12,2,128]{2,1,0:T(2,128)S(1)}, f32[12,2,128]{2,1,0:T(2,128)S(1)}, u32[]{:S(2)}, u32[]{:S(2)}) collective-permute-start(f32[12,2,128]{2,1,0:T(2,128)S(1)} %get-tuple-element.13), channel_id=1, source_target_pairs={{0,1},{1,0},{2,3},{3,2},{4,5},{5,4},{6,7},{7,6},{8,9},{9,8},{10,11... | collective-permute-start | bytes 36872 | tf_op jit(solution)/shard_map/ppermute | solution.py:406

commit v7 on v6

--- a/solution.py
+++ b/solution.py
@@ -241,13 +241,27 @@
     vel_ref,
     press_ref,
     buoy_ref,
-    visc_ref,
+    own_ref,
+    west_ref,
+    east_ref,
+    near_ref,
+    far_ref,
     new_vel_ref,
     new_press_ref,
     visc_out_ref,
+    visc_ref,
 ):
     wide_x, rows, num_levels = visc_ref.shape
     cells_x = wide_x - 2 * HALO
+    inner, end = slice(HALO, HALO + cells_y), HALO + cells_y
+    odd_y = here_ref[1:2, :] % 2 == 1
+    near, far = near_ref[...], far_ref[...]
+    visc_ref[:HALO, inner] = west_ref[...]
+    visc_ref[HALO : HALO + cells_x, inner] = own_ref[...]
+    visc_ref[HALO + cells_x :, inner] = east_ref[...]
+    visc_ref[:, :HALO] = jnp.where(odd_y, near, far)
+    visc_ref[:, end : end + HALO] = jnp.where(odd_y, far, near)
+    visc_ref[:, end + HALO :] = jnp.zeros((wide_x, rows - end - HALO, num_levels), F32)
     row = lax.broadcasted_iota(jnp.int32, (rows, num_levels), 0)
     lane = lax.broadcasted_iota(jnp.int32, (rows, num_levels), 1)
     size_x, size_y = sizes[0] * cells_x, sizes[1] * cells_y
@@ -371,7 +385,7 @@
 
 
 def stokes(here, vel, press, buoy, visc, cells_y, sizes):
-    wide_x, _, num_levels = visc.shape
+    wide_x, _, num_levels = press.shape
     cells_x = wide_x - 2 * HALO
     return pl.pallas_call(
         functools.partial(stokes_kernel, cells_y, sizes),
@@ -380,11 +394,12 @@
             jax.ShapeDtypeStruct((cells_x, cells_y, num_levels), F32),
             jax.ShapeDtypeStruct((cells_x, cells_y, num_levels), F32),
         ),
-        in_specs=[VMEM] * 5,
+        in_specs=[VMEM] * 9,
         out_specs=(VMEM, VMEM, VMEM),
+        scratch_shapes=[pltpu.VMEM(press.shape, F32)],
         compiler_params=pltpu.CompilerParams(vmem_limit_bytes=48 << 20),
         name="stokes",
-    )(here, vel, press, buoy, visc)
+    )(here, vel, press, buoy, *visc)
 
 
 def partners(size_x, size_y):
@@ -467,7 +482,11 @@
     near, here = lax.optimization_barrier((near, here))
     fields = widened(fields, near, far, pairs, odd_x == 1, odd_y == 1)
     visc, near, far = gather(here, arrived, background, marks)
-    visc = widened(visc, near, far, pairs, odd_x == 1, odd_y == 1)
+    wide = swapped(near, far, pairs[0], pairs[1], odd_x == 1, 0, visc)
+    near, far = strips(wide, odd_y == 1, 1)
+    near = lax.ppermute(near, ("gx", "gy"), pairs[2])
+    far = lax.ppermute(far, ("gx", "gy"), pairs[3])
+    visc = (visc, wide[:HALO], wide[HALO + cells_x :], near, far)
     return stokes(
         here, fields[:3], fields[3], fields[4], visc, cells_y, (size_x, size_y)
     )

time: 39 us -> 39.1 us (level)
  the two profiles are of different devices: /device:TPU:0 before, /device:TPU:8 now
where the time goes in v7:
time: 39.1 us; the launch traced here: 38.8 us
  starting transfers between devices  15.2 us (39%)
  waiting for transfers between devices  14.7 us (38%)
  Pallas kernels  6.18 us (16%)
  between operations  1.43 us (4%)
  local copies, waits for them, and re-layouts  0.99 us (3%)
    ppermute x3, waiting for transfers between devices, swapped(): far = lax.ppermute(far, ('gx', 'gy'), far_pairs)  7.74 us
    all_to_all x1, starting transfers between devices, shards(): lax.all_to_all(send.reshape(devices, capacity, 2 * num_levels), ('gx', 'g...  6.05 us
    pallas_call x1, Pallas kernels, deposit(): pl.pallas_call(functools.partial(deposit_kernel, num_owners, capacity), o...  4.44 us
    ppermute x3, starting transfers between devices, swapped(): far = lax.ppermute(far, ('gx', 'gy'), far_pairs)  4 us
    ppermute x1, waiting for transfers between devices, shards(): far = lax.ppermute(far, ('gx', 'gy'), pairs[3])  2.89 us
    ppermute x3, waiting for transfers between devices, swapped(): near = lax.ppermute(near, ('gx', 'gy'), near_pairs)  2.5 us
    ppermute x3, starting transfers between devices, swapped(): near = lax.ppermute(near, ('gx', 'gy'), near_pairs)  2.39 us
    ppermute x1, starting transfers between devices, shards(): near = lax.ppermute(near, ('gx', 'gy'), pairs[2])  2.06 us
  transfers between devices with their start and end apart: 9, of which 8 were waited for; matrix products, arithmetic and copies ran while one was open for 1% of the time, Pallas kernels for 0%

profile of v7, /device:TPU:8, one launch (start us, length us, event | category | flops | bytes accessed | tf_op | source)
XLA Modules:
  0.0 38.8 jit_solution(2409626292247618208)
XLA Ops:
  1.3 4.4 %deposit.1 = f32[512,256]{1,0:T(8,128)} custom-call(s32[1]{0:T(128)S(6)} %copy.12.count_ref, s32[1,256]{1,0:T(1,128)} %bitcast.38, s32[1,256]{1,0:T(1,128)} %bitcast.39, f32[256,256]{1,0:T(8,128)} %value_hbm.1, f32[256,256]{1,0:T(8,128)} %height_hbm.1), custom_call_target="tpu_custom_call" | custom-call | tf_op jit(solution)/shard_map/deposit/pallas_call | solution.py:167
  5.7 0.0 copy-start.1
  5.7 0.0 copy-start.3
  5.8 6.0 %all-to-all-start = ((f32[32,16,256]{2,1,0:T(8,128)}), f32[32,16,256]{2,1,0:T(8,128)S(1)}, u32[]{:S(2)}, u32[]{:S(2)}) async-start(f32[32,16,256]{2,1,0:T(8,128)} %bitcast.21), calls=%async_computation | async-start | bytes 1048576 | tf_op jit(solution)/shard_map/all_to_all | solution.py:469
  11.8 0.0 copy-start.2
  11.8 0.0 copy-done.1
  11.8 0.0 copy-done.3
  11.9 0.7 %copy-done.2 = f32[8,8,128]{2,1,0:T(8,128)S(1)} copy-done((f32[8,8,128]{2,1,0:T(8,128)S(1)}, f32[8,8,128]{2,1,0:T(8,128)}, u32[]{:S(2)}) %copy-start.2) | copy-done | bytes 32792
  12.6 0.1 iota.7.here_ref
  12.7 0.2 collective-permute-start
  12.8 1.4 %collective-permute-start.1 = (f32[5,2,8,128]{3,2,1,0:T(8,128)S(1)}, f32[5,2,8,128]{3,2,1,0:T(8,128)S(1)}, u32[]{:S(2)}, u32[]{:S(2)}) collective-permute-start(f32[5,2,8,128]{3,2,1,0:T(8,128)S(1)} %get-tuple-element.19), channel_id=1, source_target_pairs={{0,24},{1,25},{2,26},{3,27},{4,28},{5,29},{6,30},{7,31},{8,16},{9,... | collective-permute-start | bytes 122888 | tf_op jit(solution)/shard_map/ppermute | solution.py:422
  14.3 0.0 collective-permute-done
  14.3 3.1 %collective-permute-done.1 = f32[5,2,8,128]{3,2,1,0:T(8,128)S(1)} collective-permute-done((f32[5,2,8,128]{3,2,1,0:T(8,128)S(1)}, f32[5,2,8,128]{3,2,1,0:T(8,128)S(1)}, u32[]{:S(2)}, u32[]{:S(2)}) %collective-permute-start.1) | collective-permute-done | bytes 40992 | tf_op jit(solution)/shard_map/ppermute | solution.py:422
  17.4 0.1 broadcast_select_fusion.3
  17.5 2.0 %collective-permute-start.3 = (f32[5,12,2,128]{3,2,1,0:T(2,128)S(1)}, f32[5,12,2,128]{3,2,1,0:T(2,128)S(1)}, u32[]{:S(2)}, u32[]{:S(2)}) collective-permute-start(f32[5,12,2,128]{3,2,1,0:T(2,128)S(1)} %bitcast.32), channel_id=1, source_target_pairs={{0,8},{1,2},{2,1},{3,4},{4,3},{5,6},{6,5},{7,15},{8,0},{9,10},{10,... | collective-permute-start | bytes 184328 | tf_op jit(solution)/shard_map/ppermute | solution.py:422
  19.5 2.1 %collective-permute-start.2 = (f32[5,12,2,128]{3,2,1,0:T(2,128)S(1)}, f32[5,12,2,128]{3,2,1,0:T(2,128)S(1)}, u32[]{:S(2)}, u32[]{:S(2)}) collective-permute-start(f32[5,12,2,128]{3,2,1,0:T(2,128)S(1)} %get-tuple-element.16), channel_id=1, source_target_pairs={{0,1},{1,0},{2,3},{3,2},{4,5},{5,4},{6,7},{7,6},{8,9},{9,8},{10,11... | collective-permute-start | bytes 184328 | tf_op jit(solution)/shard_map/ppermute | solution.py:421
  21.6 0.1 pad.10.clone
  21.7 2.7 %collective-permute-done.3 = f32[5,12,2,128]{3,2,1,0:T(2,128)S(1)} collective-permute-done((f32[5,12,2,128]{3,2,1,0:T(2,128)S(1)}, f32[5,12,2,128]{3,2,1,0:T(2,128)S(1)}, u32[]{:S(2)}, u32[]{:S(2)}) %collective-permute-start.3) | collective-permute-done | bytes 61472 | tf_op jit(solution)/shard_map/ppermute | solution.py:422
  24.3 2.1 %collective-permute-done.2 = f32[5,12,2,128]{3,2,1,0:T(2,128)S(1)} collective-permute-done((f32[5,12,2,128]{3,2,1,0:T(2,128)S(1)}, f32[5,12,2,128]{3,2,1,0:T(2,128)S(1)}, u32[]{:S(2)}, u32[]{:S(2)}) %collective-permute-start.2) | collective-permute-done | bytes 61472 | tf_op jit(solution)/shard_map/ppermute | solution.py:421
  26.4 0.7 %all-to-all-done = f32[32,16,256]{2,1,0:T(8,128)S(1)} async-done(((f32[32,16,256]{2,1,0:T(8,128)}), f32[32,16,256]{2,1,0:T(8,128)S(1)}, u32[]{:S(2)}, u32[]{:S(2)}) %all-to-all-start) | async-done | bytes 524320 | tf_op jit(solution)/shard_map/all_to_all | solution.py:469
  27.1 0.1 copy-done
  27.2 0.4 %gather.1 = (f32[8,8,128]{2,1,0:T(8,128)S(1)}, f32[2,8,128]{2,1,0:T(8,128)S(1)}, f32[2,8,128]{2,1,0:T(8,128)S(1)}) custom-call(s32[8,128]{1,0:T(8,128)S(1)} %iota.7.here_ref, f32[512,256]{1,0:T(8,128)S(1)} %bitcast.20, f32[8,8,128]{2,1,0:T(8,128)S(1)} %copy-done), custom_call_target="tpu_custom_call" | custom-call | tf_op jit(solution)/shard_map/gather/pallas_call | solution.py:223
  27.6 0.1 collective-permute-start.4
  27.7 0.6 %collective-permute-start.5 = (f32[2,8,128]{2,1,0:T(8,128)S(1)}, f32[2,8,128]{2,1,0:T(8,128)S(1)}, u32[]{:S(2)}, u32[]{:S(2)}) collective-permute-start(f32[2,8,128]{2,1,0:T(8,128)S(1)} %get-tuple-element.12), channel_id=1, source_target_pairs={{0,24},{1,25},{2,26},{3,27},{4,28},{5,29},{6,30},{7,31},{8,16},{9,... | collective-permute-start | bytes 24584 | tf_op jit(solution)/shard_map/ppermute | solution.py:422
  28.3 0.1 maximum_maximum_fusion
  28.4 0.4 %collective-permute-done.4 = f32[2,8,128]{2,1,0:T(8,128)S(1)} collective-permute-done((f32[2,8,128]{2,1,0:T(8,128)S(1)}, f32[2,8,128]{2,1,0:T(8,128)S(1)}, u32[]{:S(2)}, u32[]{:S(2)}) %collective-permute-start.4) | collective-permute-done | bytes 8224 | tf_op jit(solution)/shard_map/ppermute | solution.py:421
  28.8 2.0 %collective-permute-done.5 = f32[2,8,128]{2,1,0:T(8,128)S(1)} collective-permute-done((f32[2,8,128]{2,1,0:T(8,128)S(1)}, f32[2,8,128]{2,1,0:T(8,128)S(1)}, u32[]{:S(2)}, u32[]{:S(2)}) %collective-permute-start.5) | collective-permute-done | bytes 8224 | tf_op jit(solution)/shard_map/ppermute | solution.py:422
  30.8 2.1 %collective-permute-start.6 = (f32[12,2,128]{2,1,0:T(2,128)S(1)}, f32[12,2,128]{2,1,0:T(2,128)S(1)}, u32[]{:S(2)}, u32[]{:S(2)}) collective-permute-start(f32[12,2,128]{2,1,0:T(2,128)S(1)} %bitcast.37), channel_id=1, source_target_pairs={{0,1},{1,0},{2,3},{3,2},{4,5},{5,4},{6,7},{7,6},{8,9},{9,8},{10,11... | collective-permute-start | bytes 36872 | tf_op jit(solution)/shard_map/ppermute | solution.py:487
  32.9 0.7 %collective-permute-start.7 = (f32[12,2,128]{2,1,0:T(2,128)S(1)}, f32[12,2,128]{2,1,0:T(2,128)S(1)}, u32[]{:S(2)}, u32[]{:S(2)}) collective-permute-start(f32[12,2,128]{2,1,0:T(2,128)S(1)} %get-tuple-element.13), channel_id=1, source_target_pairs={{0,8},{1,2},{2,1},{3,4},{4,3},{5,6},{6,5},{7,15},{8,0},{9,10},{10,... | collective-permute-start | bytes 36872 | tf_op jit(solution)/shard_map/ppermute | solution.py:488
  33.7 0.9 %collective-permute-done.6.near_ref = f32[12,2,128]{2,1,0:T(2,128)S(1)} collective-permute-done((f32[12,2,128]{2,1,0:T(2,128)S(1)}, f32[12,2,128]{2,1,0:T(2,128)S(1)}, u32[]{:S(2)}, u32[]{:S(2)}) %collective-permute-start.6) | collective-permute-done | bytes 12320 | tf_op jit(solution)/shard_map/ppermute | solution.py:487
  34.6 2.9 %collective-permute-done.7.far_ref = f32[12,2,128]{2,1,0:T(2,128)S(1)} collective-permute-done((f32[12,2,128]{2,1,0:T(2,128)S(1)}, f32[12,2,128]{2,1,0:T(2,128)S(1)}, u32[]{:S(2)}, u32[]{:S(2)}) %collective-permute-start.7) | collective-permute-done | bytes 12320 | tf_op jit(solution)/shard_map/ppermute | solution.py:488
  37.5 1.3 %stokes.1 = (f32[3,8,8,128]{3,2,1,0:T(8,128)}, f32[8,8,128]{2,1,0:T(8,128)}, f32[8,8,128]{2,1,0:T(8,128)}) custom-call(s32[8,128]{1,0:T(8,128)S(1)} %iota.7.here_ref, f32[3,12,16,128]{3,2,1,0:T(8,128)S(1)} %slice.36.vel_ref, f32[12,16,128]{2,1,0:T(8,128)S(1)} %get-tuple-element.23.press_ref, f32[12,16,128]{2,1,0:T(8,128)S(1)} %get-tuple-element.22.buoy_ref, ...), custom_call_target="tpu_custom_call" | custom-call | tf_op jit(solution)/shard_map/stokes/pallas_call | solution.py:390
  (13 shorter events, 0.1 us)
Async XLA Ops:
  5.7 6.1 %copy-start.1 = (f32[3,8,8,128]{3,2,1,0:T(8,128)S(1)}, f32[3,8,8,128]{3,2,1,0:T(8,128)}, u32[]{:S(2)}) copy-start(f32[3,8,8,128]{3,2,1,0:T(8,128)} %param.9) | copy-start | bytes 294916
  5.7 6.1 %copy-start.3 = (f32[8,8,128]{2,1,0:T(8,128)S(1)}, f32[8,8,128]{2,1,0:T(8,128)}, u32[]{:S(2)}) copy-start(f32[8,8,128]{2,1,0:T(8,128)} %param.10) | copy-start | bytes 98308
  5.8 21.3 %all-to-all-start = ((f32[32,16,256]{2,1,0:T(8,128)}), f32[32,16,256]{2,1,0:T(8,128)S(1)}, u32[]{:S(2)}, u32[]{:S(2)}) async-start(f32[32,16,256]{2,1,0:T(8,128)} %bitcast.21), calls=%async_computation | async-start | bytes 1048576 | tf_op jit(solution)/shard_map/all_to_all | solution.py:469
  11.8 0.8 %copy-start.2 = (f32[8,8,128]{2,1,0:T(8,128)S(1)}, f32[8,8,128]{2,1,0:T(8,128)}, u32[]{:S(2)}) copy-start(f32[8,8,128]{2,1,0:T(8,128)} %param.11) | copy-start | bytes 98308
  12.7 1.6 %collective-permute-start = (f32[5,2,8,128]{3,2,1,0:T(8,128)S(1)}, f32[5,2,8,128]{3,2,1,0:T(8,128)S(1)}, u32[]{:S(2)}, u32[]{:S(2)}) collective-permute-start(f32[5,2,8,128]{3,2,1,0:T(8,128)S(1)} %broadcast_select_fusion.7), channel_id=1, source_target_pairs={{0,8},{1,9},{2,10},{3,11},{4,12},{5,13},{6,14},{7,15},{8,0},{9,1},... | collective-permute-start | bytes 122888 | tf_op jit(solution)/shard_map/ppermute | solution.py:421
  12.8 4.5 %collective-permute-start.1 = (f32[5,2,8,128]{3,2,1,0:T(8,128)S(1)}, f32[5,2,8,128]{3,2,1,0:T(8,128)S(1)}, u32[]{:S(2)}, u32[]{:S(2)}) collective-permute-start(f32[5,2,8,128]{3,2,1,0:T(8,128)S(1)} %get-tuple-element.19), channel_id=1, source_target_pairs={{0,24},{1,25},{2,26},{3,27},{4,28},{5,29},{6,30},{7,31},{8,16},{9,... | collective-permute-start | bytes 122888 | tf_op jit(solution)/shard_map/ppermute | solution.py:422
  17.5 6.9 %collective-permute-start.3 = (f32[5,12,2,128]{3,2,1,0:T(2,128)S(1)}, f32[5,12,2,128]{3,2,1,0:T(2,128)S(1)}, u32[]{:S(2)}, u32[]{:S(2)}) collective-permute-start(f32[5,12,2,128]{3,2,1,0:T(2,128)S(1)} %bitcast.32), channel_id=1, source_target_pairs={{0,8},{1,2},{2,1},{3,4},{4,3},{5,6},{6,5},{7,15},{8,0},{9,10},{10,... | collective-permute-start | bytes 184328 | tf_op jit(solution)/shard_map/ppermute | solution.py:422
  19.5 6.9 %collective-permute-start.2 = (f32[5,12,2,128]{3,2,1,0:T(2,128)S(1)}, f32[5,12,2,128]{3,2,1,0:T(2,128)S(1)}, u32[]{:S(2)}, u32[]{:S(2)}) collective-permute-start(f32[5,12,2,128]{3,2,1,0:T(2,128)S(1)} %get-tuple-element.16), channel_id=1, source_target_pairs={{0,1},{1,0},{2,3},{3,2},{4,5},{5,4},{6,7},{7,6},{8,9},{9,8},{10,11... | collective-permute-start | bytes 184328 | tf_op jit(solution)/shard_map/ppermute | solution.py:421
  26.4 0.8 %copy-start = (f32[8,8,128]{2,1,0:T(8,128)S(1)}, f32[8,8,128]{2,1,0:T(8,128)}, u32[]{:S(2)}) copy-start(f32[8,8,128]{2,1,0:T(8,128)} %background_ref.1) | copy-start | bytes 98308
  27.6 1.2 %collective-permute-start.4 = (f32[2,8,128]{2,1,0:T(8,128)S(1)}, f32[2,8,128]{2,1,0:T(8,128)S(1)}, u32[]{:S(2)}, u32[]{:S(2)}) collective-permute-start(f32[2,8,128]{2,1,0:T(8,128)S(1)} %get-tuple-element.11), channel_id=1, source_target_pairs={{0,8},{1,9},{2,10},{3,11},{4,12},{5,13},{6,14},{7,15},{8,0},{9,1},... | collective-permute-start | bytes 24584 | tf_op jit(solution)/shard_map/ppermute | solution.py:421
  27.7 3.1 %collective-permute-start.5 = (f32[2,8,128]{2,1,0:T(8,128)S(1)}, f32[2,8,128]{2,1,0:T(8,128)S(1)}, u32[]{:S(2)}, u32[]{:S(2)}) collective-permute-start(f32[2,8,128]{2,1,0:T(8,128)S(1)} %get-tuple-element.12), channel_id=1, source_target_pairs={{0,24},{1,25},{2,26},{3,27},{4,28},{5,29},{6,30},{7,31},{8,16},{9,... | collective-permute-start | bytes 24584 | tf_op jit(solution)/shard_map/ppermute | solution.py:422
  30.8 3.8 %collective-permute-start.6 = (f32[12,2,128]{2,1,0:T(2,128)S(1)}, f32[12,2,128]{2,1,0:T(2,128)S(1)}, u32[]{:S(2)}, u32[]{:S(2)}) collective-permute-start(f32[12,2,128]{2,1,0:T(2,128)S(1)} %bitcast.37), channel_id=1, source_target_pairs={{0,1},{1,0},{2,3},{3,2},{4,5},{5,4},{6,7},{7,6},{8,9},{9,8},{10,11... | collective-permute-start | bytes 36872 | tf_op jit(solution)/shard_map/ppermute | solution.py:487
  32.9 4.6 %collective-permute-start.7 = (f32[12,2,128]{2,1,0:T(2,128)S(1)}, f32[12,2,128]{2,1,0:T(2,128)S(1)}, u32[]{:S(2)}, u32[]{:S(2)}) collective-permute-start(f32[12,2,128]{2,1,0:T(2,128)S(1)} %get-tuple-element.13), channel_id=1, source_target_pairs={{0,8},{1,2},{2,1},{3,4},{4,3},{5,6},{6,5},{7,15},{8,0},{9,10},{10,... | collective-permute-start | bytes 36872 | tf_op jit(solution)/shard_map/ppermute | solution.py:488
